TPU v7x, 32 devices: a whole 2x2x4 slice. The times are simulated.
32 devices in a mesh: gz: 2 (over core), row: 4 (over y, x), col: 4 (over z).
Axes of the slice: x: 2, y: 2, z: 4, core: 2. Of those that a mesh axis runs over, the one named last changes fastest.
Arguments:
- l_panel: float32 [2, 8, 4, 8, 128, 256], P('gz', None, 'row', 'col'), may hold values from -6 to 6
- l_rows: int32 [2, 8, 4, 8], P('gz', None, 'row'), may hold values from -1 to 7, as said below
- u_panel: float32 [2, 8, 4, 16, 256, 128], P('gz', None, 'col', 'row'), may hold values from -0.125 to 0.125
- u_cols: int32 [2, 8, 4, 16], P('gz', None, 'col'), may hold values from -1 to 15, as said below
- u11_inv: float32 [2, 8, 256, 256], P('gz'), as said below
- ancestor: float32 [4, 1024, 8192], P('row', 'gz', 'col'), may hold values from -6 to 6
Outputs:
- schur: float32 [4, 1024, 8192], P('row', 'gz', 'col')
Inputs may be any that keep to these rules, and one draw needn't show every extreme that they name: `l_rows`: within one layer, supernode and process row the live entries are distinct; at most 8 are live, and in every layer and process row some supernode has all 8 live. `u_cols`: within one layer, supernode and process column the live entries are distinct; at most 16 are live, and in every layer and process column some supernode has all 16 live. `u11_inv`: upper triangular, with diagonal entries between 0.5 and 1.5.
All inputs are finite; a program needn't handle non-finite values.
Results may differ from a plain program's by a relative error of at most 0.000058.
Values sent between devices are 32-bit elements; how exact they have to be, the bound alone decides.
No kernel may reach another device: no remote copies, remote signals or barrier semaphores. Data moves between devices by JAX's collectives and lax.ppermute only.
A program may use at most 128 MiB of HBM per device.

v0:
```python
import jax
import jax.numpy as jnp
from jax import lax
from jax.sharding import PartitionSpec as P

W = 256
B = 128
AR = 8
AC = 16


highest = lax.Precision.HIGHEST


def place_rows(targets, blocks):
    onehot = (targets[:, None, :] == jnp.arange(AR, dtype=jnp.int32)[None, :, None]).astype(
        jnp.float32
    )
    return jnp.einsum("sak,skbw->absw", onehot, blocks, precision=highest)


def place_columns(targets, blocks):
    onehot = (targets[:, None, :] == jnp.arange(AC, dtype=jnp.int32)[None, :, None]).astype(
        jnp.float32
    )
    return jnp.einsum("sak,skwb->swab", onehot, blocks, precision=highest)


def body(l_panel, l_rows, u_panel, u_cols, u11_inv, ancestor):
    l_blocks = l_panel[0, :, 0]
    scaled = jnp.einsum("skbw,swv->skbv", l_blocks, u11_inv[0], precision=highest)
    row_targets = l_rows[0, :, 0]
    col_targets = u_cols[0, :, 0]
    u_blocks = u_panel[0, :, 0]
    supernodes = scaled.shape[0]
    targets = row_targets
    l_placed = place_rows(targets, lax.all_gather(scaled, "col", axis=1, tiled=True))
    targets = col_targets
    u_placed = place_columns(targets, lax.all_gather(u_blocks, "row", axis=1, tiled=True))
    l_matrix = l_placed.reshape(AR * B, supernodes * W)
    u_matrix = u_placed.reshape(supernodes * W, AC * B)
    half_rows = ancestor.shape[1]
    summed = lax.psum(jnp.dot(l_matrix, u_matrix, precision=highest), "gz")
    own_share = lax.dynamic_slice_in_dim(summed, lax.axis_index("gz") * half_rows, half_rows, 0)
    return ancestor - own_share[None]


def solution(mesh):
    in_specs = (
        P("gz", None, "row", "col", None, None),
        P("gz", None, "row", None),
        P("gz", None, "col", "row", None, None),
        P("gz", None, "col", None),
        P("gz", None, None, None),
        P("row", "gz", "col"),
    )
    out_specs = P("row", "gz", "col")
    return jax.shard_map(body, mesh=mesh, in_specs=in_specs, out_specs=out_specs, check_vma=False)
```

profile of v0, /device:TPU:17, one launch (start us, length us, event | category | flops | bytes accessed | tf_op | source)
XLA Modules:
  0.0 465.8 jit_solution(12975585213557576710)
XLA Ops:
  6.5 0.0 copy-start
  6.5 0.0 all-gather.4.cloned.1.call-start
  6.5 1.6 copy-done
  8.1 5.1 %fusion.11 = f32[8,2,128,256]{3,2,0,1:T(8,128)} fusion(f32[1,8,256,256]{3,2,1,0:T(8,128)S(1)} %copy-done, f32[1,8,1,2,128,256]{5,4,3,2,1,0:T(8,128)} %param.6), kind=kOutput, calls=%fused_computation.10 | convolution fusion | flops 1610612736 | bytes 6291456 | tf_op jit(solution)/shard_map/skbw,swv->skbv/dot_general | solution.py:31
  13.2 0.0 copy-start.4
  13.2 0.0 all-gather.4.cloned.1.call-update
  13.2 0.0 all-gather.6.cloned.1.call-start
  13.3 4.7 copy.13
  17.9 0.0 all-gather.6.cloned.1.call-update
  17.9 0.0 all-reduce.2.cloned.1.call-start
  18.0 144.3 %all-gather.4.cloned.1.call-done = f32[8,8,128,256]{3,2,0,1:T(8,128)} async-done(((f32[8,2,128,256]{3,2,0,1:T(8,128)}), f32[8,8,128,256]{3,2,0,1:T(8,128)}) %all-gather.4.cloned.1.call-update) | async-done | bytes 8388624 | tf_op jit(solution)/shard_map/all_gather | solution.py:37
  162.3 0.0 copy-done.4
  162.3 12.2 %fusion.8 = f32[8,128,8,256]{3,0,1,2:T(8,128)S(1)} fusion(f32[8,8,128,256]{3,2,0,1:T(8,128)} %all-gather.4.cloned.1.call-done, s32[8,8]{1,0:T(8,128)S(1)} %bitcast.41), kind=kOutput, calls=%fused_computation.9 | convolution fusion | flops 201327104 | bytes 16777472 | tf_op jit(solution)/shard_map/sak,skbw->absw/dot_general | solution.py:19
  174.4 4.9 %copy.12 = f32[8,128,8,256]{3,2,1,0:T(8,128)S(1)} copy(f32[8,128,8,256]{3,0,1,2:T(8,128)S(1)} %fusion.8) | data formatting | bytes 16777216 | tf_op jit(solution)/shard_map/sak,skbw->absw/transpose | solution.py:19
  179.3 0.0 copy-start.3
  179.3 7.3 %copy.19 = f32[128,8,8,256]{3,1,2,0:T(8,128)} copy(f32[128,8,8,256]{3,2,1,0:T(8,128)S(1)} %bitcast.38) | data formatting | bytes 16777216
  186.6 135.0 %all-gather.6.cloned.1.call-done = f32[1,8,1,16,256,128]{5,4,2,1,0,3:T(8,128)} async-done(((f32[1,8,1,4,256,128]{5,4,2,1,0,3:T(8,128)}), f32[1,8,1,16,256,128]{5,4,2,1,0,3:T(8,128)}) %all-gather.6.cloned.1.call-update) | async-done | bytes 16777232 | tf_op jit(solution)/shard_map/all_gather | solution.py:39
  321.6 0.0 copy-done.3
  321.6 0.0 copy-start.2
  321.6 26.0 %fusion.3 = f32[8,16,256,128]{3,1,2,0:T(8,128)} fusion(f32[1,8,1,16,256,128]{5,4,2,1,0,3:T(8,128)} %all-gather.6.cloned.1.call-done, s32[8,16]{1,0:T(8,128)S(1)} %bitcast.40), kind=kOutput, calls=%fused_computation.3 | convolution fusion | flops 805308416 | bytes 33554944 | tf_op jit(solution)/shard_map/sak,skwb->swab/dot_general | solution.py:26
  347.6 0.0 copy-done.2
  347.6 64.9 %fusion = f32[1024,2048]{1,0:T(8,128)} fusion(f32[1024,2048]{1,0:T(8,128)S(1)} %bitcast.39, f32[256,8,16,128]{3,2,1,0:T(8,128)} %bitcast.37), kind=kOutput, calls=%fused_computation | convolution fusion | flops 51539607552 | bytes 33554432 | tf_op jit(solution)/shard_map/dot_general | solution.py:43
  412.5 0.0 all-reduce.2.cloned.1.call-update
  412.5 0.0 copy-start.1
  412.5 39.8 %all-reduce.2.cloned.1.call-done = f32[1024,2048]{1,0:T(8,128)} async-done(((f32[1024,2048]{1,0:T(8,128)}), f32[1024,2048]{1,0:T(8,128)}) %all-reduce.2.cloned.1.call-update) | async-done | bytes 8388624 | tf_op jit(solution)/shard_map/psum | solution.py:43
  452.3 6.6 %bitcast_subtract_fusion = f32[1,512,2048]{2,1,0:T(8,128)} fusion(f32[1,512,2048]{2,1,0:T(8,128)} %param.11, f32[1024,2048]{1,0:T(8,128)} %all-reduce.2.cloned.1.call-done, s32[]{:T(128)S(6)} %select_n.3), kind=kLoop, calls=%fused_computation.8 | loop fusion | flops 1048576 | bytes 12582916 | tf_op jit(solution)/shard_map/sub | solution.py:45
  458.8 0.0 copy-done.1
Async XLA Ops:
  6.5 1.6 copy-start
  6.5 155.7 %all-gather.4.cloned.1.call-start = ((), (), s32[]{:S(2)}) async-start(), calls=%async_computation | async-start | bytes 10485760 | tf_op jit(solution)/shard_map/all_gather | solution.py:37
  13.2 149.1 %copy-start.4 = (s32[1,8,1,8]{3,2,1,0:T(1,128)S(1)}, s32[1,8,1,8]{3,2,1,0:T(1,128)}, u32[]{:S(2)}) copy-start(s32[1,8,1,8]{3,2,1,0:T(1,128)} %param.7) | copy-start | bytes 772
  13.2 308.4 %all-gather.6.cloned.1.call-start = ((), (), s32[]{:S(2)}) async-start(), calls=%async_computation.2 | async-start | bytes 20971520 | tf_op jit(solution)/shard_map/all_gather | solution.py:39
  17.9 434.3 %all-reduce.2.cloned.1.call-start = ((), (), s32[]{:S(2)}) async-start(), calls=%async_computation.1 | async-start | bytes 16777216 | tf_op jit(solution)/shard_map/psum | solution.py:43
  179.3 142.3 %copy-start.3 = (s32[1,8,1,16]{3,2,1,0:T(1,128)S(1)}, s32[1,8,1,16]{3,2,1,0:T(1,128)}, u32[]{:S(2)}) copy-start(s32[1,8,1,16]{3,2,1,0:T(1,128)} %param.9) | copy-start | bytes 1540
  321.6 26.0 %copy-start.2 = (f32[128,8,8,256]{3,1,2,0:T(8,128)S(1)}, f32[128,8,8,256]{3,1,2,0:T(8,128)}, u32[]{:S(2)}) copy-start(f32[128,8,8,256]{3,1,2,0:T(8,128)} %copy.19) | copy-start | bytes 25165828
  412.5 46.3 %copy-start.1 = (f32[1,8,256,256]{3,2,1,0:T(8,128)S(1)}, f32[1,8,256,256]{3,2,1,0:T(8,128)}, u32[]{:S(2)}) copy-start(f32[1,8,256,256]{3,2,1,0:T(8,128)} %param.10) | copy-start | bytes 6291460
Sparse Core Ops, SparseCore 0:
  13.3 148.8 all-gather.3
  164.1 157.4 all-gather.5
  412.6 39.6 all-reduce.1
where the time goes:
time: 473 us; the launch traced here: 466 us
  waiting for transfers between devices  319 us (67%)
  matrix products  108 us (23%)
  local copies, waits for them, and re-layouts  18.4 us (4%)
  between operations  13.6 us (3%)
  other arithmetic  6.56 us (1%)
    all_gather x1, waiting for transfers between devices, body(): lax.all_gather(scaled, 'col', axis=1, tiled=True)  144 us
    all_gather x1, waiting for transfers between devices, body(): lax.all_gather(u_blocks, 'row', axis=1, tiled=True)  135 us
    dot_general x1, matrix products, body(): summed = lax.psum(jnp.dot(l_matrix, u_matrix, precision=highest), 'gz')  64.9 us
    psum x1, waiting for transfers between devices, body(): summed = lax.psum(jnp.dot(l_matrix, u_matrix, precision=highest), 'gz')  39.8 us
    dot_general x1, matrix products, place_columns(): return jnp.einsum('sak,skwb->swab', onehot, blocks, precision=highest)  26 us
    unnamed x12, local copies, waits for them, and re-layouts  13.6 us
    dot_general x1, matrix products, place_rows(): return jnp.einsum('sak,skbw->absw', onehot, blocks, precision=highest)  12.2 us
  transfers between devices with their start and end apart: 3, of which 3 were waited for; matrix products, arithmetic and copies ran while one was open for 6% of the time, Pallas kernels for 0%

commit v1 on v0

v1 whole, which is shorter than its diff:
```python
import functools

import jax
import jax.numpy as jnp
from jax import lax
from jax.experimental import pallas as pl
from jax.experimental.pallas import tpu as pltpu
from jax.sharding import PartitionSpec as P

W = 256
B = 128
AR = 8
AC = 16
HALF = AR * B // 2
F32 = jnp.float32
BF16 = jnp.bfloat16


def split(x):
    hi = x.astype(BF16)
    return hi, (x - hi.astype(F32)).astype(BF16)


def dot(a, b):
    return jnp.dot(a, b, preferred_element_type=F32)


def update_kernel(n_l, n_u, start, has_send, l_tgt, u_tgt, l_base, u_base, *refs):
    l_refs, refs = refs[:n_l], refs[n_l:]
    u_refs, refs = refs[:n_u], refs[n_u:]
    inv_ref, keep_in, refs = refs[0], refs[1], refs[2:]
    if has_send:
        send_in, refs = refs[0], refs[1:]
    send, keep, raw_h, raw_l, l_cat, u_cat = refs
    step = pl.program_id(0)
    node = start + step

    @pl.when(step == 0)
    def _():
        keep[...] = keep_in[...]
        send[...] = send_in[...] if has_send else jnp.zeros_like(send)

    raw_h[...] = jnp.zeros_like(raw_h)
    raw_l[...] = jnp.zeros_like(raw_l)
    for b, ref in enumerate(l_refs):
        base = l_base[b]
        for j in range(ref.shape[1]):
            tgt = jnp.where(base >= 0, l_tgt[node, jnp.maximum(base, 0) + j], -1)

            @pl.when(tgt >= 0)
            def _(ref=ref, j=j, tgt=tgt):
                rows = pl.ds(pl.multiple_of(tgt * B, B), B)
                hi, lo = split(ref[0, j])
                raw_h[rows, :] = hi
                raw_l[rows, :] = lo

    inv_h, inv_l = split(inv_ref[0])
    for m in range(0, AR * B, 256):
        rh, rl = raw_h[m : m + 256, :], raw_l[m : m + 256, :]
        hi, lo = split(dot(rh, inv_h) + dot(rh, inv_l) + dot(rl, inv_h))
        l_cat[m : m + 256, 0:W] = hi
        l_cat[m : m + 256, W : 2 * W] = lo
        l_cat[m : m + 256, 2 * W : 3 * W] = hi

    for b, ref in enumerate(u_refs):
        base = u_base[b]
        for j in range(0, ref.shape[1], 2):
            tgts = [u_tgt[node, base + j], u_tgt[node, base + j + 1]]

            @pl.when(jnp.maximum(tgts[0], tgts[1]) >= 0)
            def _(ref=ref, j=j, tgts=tgts):
                cols = []
                for i, tgt in enumerate(tgts):
                    hi, lo = split(jnp.where(tgt >= 0, ref[0, j + i], 0.0))
                    here = slice(i * B, (i + 1) * B)
                    u_cat[0:W, here] = hi
                    u_cat[W : 2 * W, here] = hi
                    u_cat[2 * W : 3 * W, here] = lo
                    cols.append(pl.ds(pl.multiple_of(jnp.maximum(tgt, 0) * B, B), B))
                part = dot(l_cat[0:HALF, :], u_cat[...])
                send[:, cols[0]] += part[:, :B]
                send[:, cols[1]] += part[:, B:]
                part = dot(l_cat[HALF : 2 * HALF, :], u_cat[...])
                keep[:, cols[0]] -= part[:, :B]
                keep[:, cols[1]] -= part[:, B:]


def apply_update(start, tables, l_bufs, u_bufs, u11_inv, send, keep):
    nodes = l_bufs[0].shape[0]
    width = keep.shape[1]

    def per_node(buf):
        return pl.BlockSpec((1,) + buf.shape[1:], lambda s, *_: (s, 0, 0, 0))

    whole = pl.BlockSpec((HALF, width), lambda s, *_: (0, 0), pipeline_mode=pl.Buffered(1))
    acc = jax.ShapeDtypeStruct((HALF, width), F32)
    sends = [] if send is None else [send]
    n_in = 4 + len(l_bufs) + len(u_bufs)
    return pl.pallas_call(
        functools.partial(update_kernel, len(l_bufs), len(u_bufs), start, bool(sends)),
        out_shape=(acc, acc),
        grid_spec=pltpu.PrefetchScalarGridSpec(
            num_scalar_prefetch=4,
            grid=(nodes,),
            in_specs=[per_node(b) for b in l_bufs]
            + [per_node(b) for b in u_bufs]
            + [pl.BlockSpec((1, W, W), lambda s, *_: (start + s, 0, 0))]
            + [whole] * (1 + len(sends)),
            out_specs=(whole, whole),
            scratch_shapes=[
                pltpu.VMEM((AR * B, W), BF16),
                pltpu.VMEM((AR * B, W), BF16),
                pltpu.VMEM((AR * B, 3 * W), BF16),
                pltpu.VMEM((3 * W, 2 * B), BF16),
            ],
        ),
        input_output_aliases={n_in + 1: 1, n_in + 2: 0} if sends else {},
        compiler_params=pltpu.CompilerParams(
            dimension_semantics=("arbitrary",), vmem_limit_bytes=48 << 20
        ),
    )(*tables, *l_bufs, *u_bufs, u11_inv, keep, *sends)


class Link:
    def __init__(self, axis):
        self.axis, self.last = axis, None

    def send(self, x, pairs):
        if self.last is not None:
            x, _ = lax.optimization_barrier((x, self.last))
        self.last = lax.ppermute(x, self.axis, pairs)
        return self.last


def up(hop):
    return [(z, z + 1) for z in range(hop - 1, 3)]


def down(hop):
    return [(z, z - 1) for z in range(1, 5 - hop)]


def side(mask):
    return [(r, r ^ mask) for r in range(4)]


def exchange(l_chunk, u_h0, u_h1, links):
    lx, ly, lu, ld = links
    x0, y1 = lx.send(u_h0, side(1)), ly.send(u_h1, side(2))
    up1, down1 = lu.send(l_chunk, up(1)), ld.send(l_chunk, down(1))
    x1, y0 = lx.send(u_h1, side(1)), ly.send(u_h0, side(2))
    up2, down2 = lu.send(up1, up(2)), ld.send(down1, down(2))
    d1, d0 = lx.send(y1, side(1)), ly.send(x0, side(2))
    up3, down3 = lu.send(up2, up(3)), ld.send(down2, down(3))
    l_bufs = [l_chunk, up1, down1, up2, down2, up3, down3]
    u_bufs = [u_h0, u_h1, x0, x1, y0, y1, d0, d1]
    return l_bufs, u_bufs


def body(rows, cols, l_panel, l_rows, u_panel, u_cols, u11_inv, ancestor):
    gz, row, col = (lax.axis_index(a) for a in ("gz", "row", "col"))
    l_own, u_own, inv = l_panel[0, :, 0], u_panel[0, :, 0], u11_inv[0]
    nodes, l_slots = l_own.shape[:2]
    u_slots = u_own.shape[1]
    l_tgt = l_rows[0, :, 0]
    l_tgt = jnp.where(l_tgt < 0, -1, (l_tgt + (AR // 2) * (1 - gz)) % AR)
    u_tgt = u_cols[0, :, 0]
    keep, send = ancestor[0], None

    if rows == 4 and cols == 4:
        half = u_slots // 2
        sources = jnp.stack([col, col - 1, col + 1, col - 2, col + 2, col - 3, col + 3])
        l_base = jnp.where((sources >= 0) & (sources < cols), sources * l_slots, -1)
        squares = jnp.stack([row, row, row ^ 1, row ^ 1, row ^ 2, row ^ 2, row ^ 3, row ^ 3])
        u_base = squares * u_slots + half * (jnp.arange(8, dtype=jnp.int32) % 2)
        tables = [t.astype(jnp.int32) for t in (l_tgt, u_tgt, l_base, u_base)]
        links = [Link("row"), Link("row"), Link("col"), Link("col")]
        size = nodes // 2
        for start in range(0, nodes, size):
            here = slice(start, start + size)
            l_bufs, u_bufs = exchange(l_own[here], u_own[here, :half], u_own[here, half:], links)
            send, keep = apply_update(start, tables, l_bufs, u_bufs, inv, send, keep)
    else:
        l_all = lax.all_gather(l_own, "col", axis=1, tiled=True)
        u_all = lax.all_gather(u_own, "row", axis=1, tiled=True)
        zero = jnp.zeros((1,), jnp.int32)
        tables = [t.astype(jnp.int32) for t in (l_tgt, u_tgt, zero, zero)]
        send, keep = apply_update(0, tables, [l_all], [u_all], inv, send, keep)

    other = lax.ppermute(send, "gz", [(0, 1), (1, 0)])
    return (keep - other)[None]


def solution(mesh):
    in_specs = (
        P("gz", None, "row", "col", None, None),
        P("gz", None, "row", None),
        P("gz", None, "col", "row", None, None),
        P("gz", None, "col", None),
        P("gz", None, None, None),
        P("row", "gz", "col"),
    )
    return jax.shard_map(
        functools.partial(body, mesh.shape["row"], mesh.shape["col"]),
        mesh=mesh,
        in_specs=in_specs,
        out_specs=P("row", "gz", "col"),
        check_vma=False,
    )
```

time: 473 us -> 222 us (0.47); the launches traced: 466 us -> 220 us
  waiting for transfers between devices: 319 us -> 77.4 us
  matrix products: 108 us -> 0 us
  Pallas kernels: 0 us -> 69.4 us
  starting transfers between devices: 0.09 us -> 56.6 us
  between operations: 13.6 us -> 0.37 us
  local copies, waits for them, and re-layouts: 18.4 us -> 11.6 us
    all_gather x2 -> x0, waiting for transfers between devices: 279 us -> none  [the longest x1 144 us: body(): lax.all_gather(scaled, 'col', axis=1, tiled=True)]
    dot_general x4 -> x0, matrix products: 108 us -> none  [the longest x1 64.9 us: body(): summed = lax.psum(jnp.dot(l_matrix, u_matrix, precision=highest), 'gz')]
    ppermute x0 -> x25, waiting for transfers between devices: none -> 77.4 us  [the longest x24 70.4 us: send(): self.last = lax.ppermute(x, self.axis, pairs)]
    pallas_call x0 -> x2, Pallas kernels: none -> 69.4 us  [apply_update(): pl.pallas_call(functools.partial(update_kernel, len(l_bufs), len(u_bufs),...]
    ppermute x0 -> x25, starting transfers between devices: none -> 56.6 us  [the longest x24 49.8 us: send(): self.last = lax.ppermute(x, self.axis, pairs)]
    psum x1 -> x0, waiting for transfers between devices: 39.8 us -> none  [body(): summed = lax.psum(jnp.dot(l_matrix, u_matrix, precision=highest), 'gz')]
    sub x1 -> x0, other arithmetic: 6.56 us -> none  [body(): return ancestor - own_share[None]]
    broadcast_in_dim x0 -> x1, other arithmetic: none -> 4.96 us  [body(): return (keep - other)[None]]
  transfers between devices with their start and end apart: 3 -> 25, of which waited for: 3 -> 13; matrix products, arithmetic and copies ran while one was open for 6% -> 0% of each run, Pallas kernels for 0% -> 15%
where the time goes in v1:
time: 222 us; the launch traced here: 220 us
  waiting for transfers between devices  77.4 us (35%)
  Pallas kernels  69.4 us (31%)
  starting transfers between devices  56.6 us (25%)
  local copies, waits for them, and re-layouts  11.6 us (5%)
  other arithmetic  4.99 us (2%)
    ppermute x24, waiting for transfers between devices, send(): self.last = lax.ppermute(x, self.axis, pairs)  70.4 us
    pallas_call x2, Pallas kernels, apply_update(): pl.pallas_call(functools.partial(update_kernel, len(l_bufs), len(u_bufs),...  69.4 us
    ppermute x24, starting transfers between devices, send(): self.last = lax.ppermute(x, self.axis, pairs)  49.8 us
    unnamed x54, local copies, waits for them, and re-layouts  8.66 us
    ppermute x1, waiting for transfers between devices, body(): other = lax.ppermute(send, 'gz', [(0, 1), (1, 0)])  7 us
    ppermute x1, starting transfers between devices, body(): other = lax.ppermute(send, 'gz', [(0, 1), (1, 0)])  6.78 us
    broadcast_in_dim x1, other arithmetic, body(): return (keep - other)[None]  4.96 us
  transfers between devices with their start and end apart: 25, of which 13 were waited for; matrix products, arithmetic and copies ran while one was open for 0% of the time, Pallas kernels for 15%

profile of v1, /device:TPU:17, one launch (start us, length us, event | category | flops | bytes accessed | tf_op | source)
XLA Modules:
  0.0 220.3 jit_solution(12252798611441519640)
XLA Ops:
  0.0 2.6 %fusion.4 = (f32[4,2,256,128]{3,2,1,0:T(8,128)S(1)}, f32[4,2,256,128]{3,2,1,0:T(8,128)S(1)}, f32[4,2,256,128]{3,2,1,0:T(8,128)S(1)}, f32[4,2,256,128]{3,2,1,0:T(8,128)S(1)}) fusion(f32[8,4,256,128]{3,2,1,0:T(8,128)} %bitcast.34), kind=kLoop, calls=%fused_computation.12 | loop fusion | bytes 8388608 | tf_op jit(solution)/shard_map/slice | solution.py:181
  2.7 1.3 collective-permute-start.13
  4.0 1.2 collective-permute-start.12
  5.4 2.1 collective-permute-start.4
  7.5 3.3 %collective-permute-start = (f32[4,2,128,256]{3,2,1,0:T(8,128)S(1)}, f32[4,2,128,256]{3,2,1,0:T(8,128)S(1)}, u32[]{:S(2)}, u32[]{:S(2)}) collective-permute-start(f32[4,2,128,256]{3,2,1,0:T(8,128)S(1)} %get-tuple-element.57.refs_0_), channel_id=1, source_target_pairs={{0,1},{1,2},{2,3},{4,5},{5,6},{6,7},{8,9},{9,10},{10,11},{12,13},{... | collective-permute-start | bytes 3145736 | tf_op jit(solution)/shard_map/ppermute | solution.py:131
  10.7 16.0 %collective-permute-done.13.refs_9_ = f32[4,2,256,128]{3,2,1,0:T(8,128)S(1)} collective-permute-done((f32[4,2,256,128]{3,2,1,0:T(8,128)S(1)}, f32[4,2,256,128]{3,2,1,0:T(8,128)S(1)}, u32[]{:S(2)}, u32[]{:S(2)}) %collective-permute-start.13) | collective-permute-done | bytes 1048608 | tf_op jit(solution)/shard_map/ppermute | solution.py:131
  28.0 1.2 collective-permute-start.18
  29.2 1.5 collective-permute-done.4.refs_2_
  30.7 2.1 collective-permute-start.5
  32.8 2.9 %collective-permute-start.1 = (f32[4,2,128,256]{3,2,1,0:T(8,128)S(1)}, f32[4,2,128,256]{3,2,1,0:T(8,128)S(1)}, u32[]{:S(2)}, u32[]{:S(2)}) collective-permute-start(f32[4,2,128,256]{3,2,1,0:T(8,128)S(1)} %collective-permute-done.refs_1_), channel_id=1, source_target_pairs={{1,2},{2,3},{5,6},{6,7},{9,10},{10,11},{13,14},{14,15},{17,18},{18... | collective-permute-start | bytes 3145736 | tf_op jit(solution)/shard_map/ppermute | solution.py:131
  36.7 13.1 %collective-permute-done.14.refs_10_ = f32[4,2,256,128]{3,2,1,0:T(8,128)S(1)} collective-permute-done((f32[4,2,256,128]{3,2,1,0:T(8,128)S(1)}, f32[4,2,256,128]{3,2,1,0:T(8,128)S(1)}, u32[]{:S(2)}, u32[]{:S(2)}) %collective-permute-start.14) | collective-permute-done | bytes 1048608 | tf_op jit(solution)/shard_map/ppermute | solution.py:131
  51.1 1.2 collective-permute-start.19
  54.7 2.2 %collective-permute-done.1.refs_3_ = f32[4,2,128,256]{3,2,1,0:T(8,128)S(1)} collective-permute-done((f32[4,2,128,256]{3,2,1,0:T(8,128)S(1)}, f32[4,2,128,256]{3,2,1,0:T(8,128)S(1)}, u32[]{:S(2)}, u32[]{:S(2)}) %collective-permute-start.1) | collective-permute-done | bytes 1048608 | tf_op jit(solution)/shard_map/ppermute | solution.py:131
  56.9 3.0 %collective-permute-start.2 = (f32[4,2,128,256]{3,2,1,0:T(8,128)S(1)}, f32[4,2,128,256]{3,2,1,0:T(8,128)S(1)}, u32[]{:S(2)}, u32[]{:S(2)}) collective-permute-start(f32[4,2,128,256]{3,2,1,0:T(8,128)S(1)} %collective-permute-done.1.refs_3_), channel_id=1, source_target_pairs={{2,3},{6,7},{10,11},{14,15},{18,19},{22,23},{26,27},{30,31}} | collective-permute-start | bytes 3145736 | tf_op jit(solution)/shard_map/ppermute | solution.py:131
  60.9 11.1 %collective-permute-done.15.refs_14_ = f32[4,2,256,128]{3,2,1,0:T(8,128)S(1)} collective-permute-done((f32[4,2,256,128]{3,2,1,0:T(8,128)S(1)}, f32[4,2,256,128]{3,2,1,0:T(8,128)S(1)}, u32[]{:S(2)}, u32[]{:S(2)}) %collective-permute-start.15) | collective-permute-done | bytes 1048608 | tf_op jit(solution)/shard_map/ppermute | solution.py:131
  73.3 1.2 collective-permute-start.20
  74.5 4.0 %collective-permute-start.7 = (f32[4,2,128,256]{3,2,1,0:T(8,128)S(1)}, f32[4,2,128,256]{3,2,1,0:T(8,128)S(1)}, u32[]{:S(2)}, u32[]{:S(2)}) collective-permute-start(f32[4,2,128,256]{3,2,1,0:T(8,128)S(1)} %get-tuple-element.34.refs_0_), channel_id=1, source_target_pairs={{1,0},{2,1},{3,2},{5,4},{6,5},{7,6},{9,8},{10,9},{11,10},{13,12},{... | collective-permute-start | bytes 3145736 | tf_op jit(solution)/shard_map/ppermute | solution.py:131
  78.9 4.2 %collective-permute-start.3 = (f32[4,2,128,256]{3,2,1,0:T(8,128)S(1)}, f32[4,2,128,256]{3,2,1,0:T(8,128)S(1)}, u32[]{:S(2)}, u32[]{:S(2)}) collective-permute-start(f32[4,2,128,256]{3,2,1,0:T(8,128)S(1)} %get-tuple-element.34.refs_0_), channel_id=1, source_target_pairs={{0,1},{1,2},{2,3},{4,5},{5,6},{6,7},{8,9},{9,10},{10,11},{12,13},{... | collective-permute-start | bytes 3145736 | tf_op jit(solution)/shard_map/ppermute | solution.py:131
  83.1 10.7 %collective-permute-done.16.refs_9_ = f32[4,2,256,128]{3,2,1,0:T(8,128)} collective-permute-done((f32[4,2,256,128]{3,2,1,0:T(8,128)S(1)}, f32[4,2,256,128]{3,2,1,0:T(8,128)}, u32[]{:S(2)}, u32[]{:S(2)}) %collective-permute-start.16) | collective-permute-done | bytes 1048608 | tf_op jit(solution)/shard_map/ppermute | solution.py:131
  95.0 1.2 collective-permute-start.21
  97.0 5.1 %collective-permute-start.9 = (f32[4,2,128,256]{3,2,1,0:T(8,128)S(1)}, f32[4,2,128,256]{3,2,1,0:T(8,128)}, u32[]{:S(2)}, u32[]{:S(2)}) collective-permute-start(f32[4,2,128,256]{3,2,1,0:T(8,128)S(1)} %collective-permute-done.7.refs_2_), channel_id=1, source_target_pairs={{1,0},{2,1},{5,4},{6,5},{9,8},{10,9},{13,12},{14,13},{17,16},{18,1... | collective-permute-start | bytes 3145736 | tf_op jit(solution)/shard_map/ppermute | solution.py:131
  103.1 2.4 %collective-permute-start.8 = (f32[4,2,128,256]{3,2,1,0:T(8,128)S(1)}, f32[4,2,128,256]{3,2,1,0:T(8,128)}, u32[]{:S(2)}, u32[]{:S(2)}) collective-permute-start(f32[4,2,128,256]{3,2,1,0:T(8,128)S(1)} %collective-permute-done.3.refs_1_), channel_id=1, source_target_pairs={{1,2},{2,3},{5,6},{6,7},{9,10},{10,11},{13,14},{14,15},{17,18},{18... | collective-permute-start | bytes 3145736 | tf_op jit(solution)/shard_map/ppermute | solution.py:131
  106.5 8.9 %collective-permute-done.17.refs_10_ = f32[4,2,256,128]{3,2,1,0:T(8,128)S(1)} collective-permute-done((f32[4,2,256,128]{3,2,1,0:T(8,128)S(1)}, f32[4,2,256,128]{3,2,1,0:T(8,128)S(1)}, u32[]{:S(2)}, u32[]{:S(2)}) %collective-permute-start.17) | collective-permute-done | bytes 1048608 | tf_op jit(solution)/shard_map/ppermute | solution.py:131
  116.6 1.2 collective-permute-start.22
  118.8 1.7 collective-permute-start.11
  120.5 4.1 %collective-permute-done.8.refs_3_ = f32[4,2,128,256]{3,2,1,0:T(8,128)} collective-permute-done((f32[4,2,128,256]{3,2,1,0:T(8,128)S(1)}, f32[4,2,128,256]{3,2,1,0:T(8,128)}, u32[]{:S(2)}, u32[]{:S(2)}) %collective-permute-start.8) | collective-permute-done | bytes 1048608 | tf_op jit(solution)/shard_map/ppermute | solution.py:131
  124.7 3.5 %collective-permute-start.10 = (f32[4,2,128,256]{3,2,1,0:T(8,128)}, f32[4,2,128,256]{3,2,1,0:T(8,128)}, u32[]{:S(2)}, u32[]{:S(2)}) collective-permute-start(f32[4,2,128,256]{3,2,1,0:T(8,128)} %collective-permute-done.8.refs_3_), channel_id=1, source_target_pairs={{2,3},{6,7},{10,11},{14,15},{18,19},{22,23},{26,27},{30,31}} | collective-permute-start | bytes 3145736 | tf_op jit(solution)/shard_map/ppermute | solution.py:131
  132.2 33.8 %shard_map.64 = (f32[512,2048]{1,0:T(8,128)}, f32[512,2048]{1,0:T(8,128)}) custom-call(s32[8,8]{1,0:T(8,128)S(1)} %fusion.1.l_tgt, s32[8,16]{1,0:T(8,128)S(1)} %bitcast.29, s32[7]{0:T(128)S(1)} %and_select_fusion.1.l_base, s32[8]{0:T(128)S(1)} %fusion.3.u_base, f32[4,2,128,256]{3,2,1,0:T(8,128)S(1)} %get-tuple-element.57.refs_0_, ...), custom_call_target="tpu_custom_call" | custom-call | tf_op jit(solution)/shard_map/pallas_call | solution.py:99
  166.1 35.6 %shard_map.65 = (f32[512,2048]{1,0:T(8,128)}, f32[512,2048]{1,0:T(8,128)}) custom-call(s32[8,8]{1,0:T(8,128)S(1)} %fusion.1.l_tgt, s32[8,16]{1,0:T(8,128)S(1)} %bitcast.30, s32[7]{0:T(128)S(1)} %and_select_fusion.1.l_base, s32[8]{0:T(128)S(1)} %fusion.3.u_base, ...), custom_call_target="tpu_custom_call", output_to_operand_aliasing={{1}: (20, {}), {0}: (21, {})} | custom-call | tf_op jit(solution)/shard_map/pallas_call | solution.py:99
  201.6 6.8 %collective-permute-start.24 = (f32[512,2048]{1,0:T(8,128)}, f32[512,2048]{1,0:T(8,128)S(1)}, u32[]{:S(2)}, u32[]{:S(2)}) collective-permute-start(f32[512,2048]{1,0:T(8,128)} %get-tuple-element.52), channel_id=1, source_target_pairs={{0,16},{16,0},{1,17},{17,1},{2,18},{18,2},{3,19},{19,3},{4,20},{20... | collective-permute-start | bytes 12582920 | tf_op jit(solution)/shard_map/ppermute | solution.py:190
  208.4 7.0 %collective-permute-done.24 = f32[512,2048]{1,0:T(8,128)S(1)} collective-permute-done((f32[512,2048]{1,0:T(8,128)}, f32[512,2048]{1,0:T(8,128)S(1)}, u32[]{:S(2)}, u32[]{:S(2)}) %collective-permute-start.24) | collective-permute-done | bytes 4194336 | tf_op jit(solution)/shard_map/ppermute | solution.py:190
  215.4 5.0 %subtract_bitcast_fusion = f32[1,512,2048]{2,1,0:T(8,128)} fusion(f32[512,2048]{1,0:T(8,128)} %get-tuple-element.51, f32[512,2048]{1,0:T(8,128)S(1)} %collective-permute-done.24), kind=kLoop, calls=%fused_computation | loop fusion | flops 1048576 | bytes 12582912 | tf_op jit(solution)/shard_map/broadcast_in_dim | solution.py:191
  (82 shorter events, 18.6 us)
Async XLA Ops:
  2.6 122.0 %copy-start.11 = (f32[4,2,256,128]{3,2,1,0:T(8,128)}, f32[4,2,256,128]{3,2,1,0:T(8,128)S(1)}, u32[]{:S(2)}) copy-start(f32[4,2,256,128]{3,2,1,0:T(8,128)S(1)} %get-tuple-element.45.refs_8_) | copy-start | bytes 3145732
  2.6 125.6 %copy-start.12 = (f32[4,2,256,128]{3,2,1,0:T(8,128)}, f32[4,2,256,128]{3,2,1,0:T(8,128)S(1)}, u32[]{:S(2)}) copy-start(f32[4,2,256,128]{3,2,1,0:T(8,128)S(1)} %get-tuple-element.46.refs_7_) | copy-start | bytes 3145732
  2.6 125.5 %copy-start.13 = (f32[4,2,256,128]{3,2,1,0:T(8,128)}, f32[4,2,256,128]{3,2,1,0:T(8,128)S(1)}, u32[]{:S(2)}) copy-start(f32[4,2,256,128]{3,2,1,0:T(8,128)S(1)} %get-tuple-element.43.refs_7_) | copy-start | bytes 3145732
  2.6 125.5 %copy-start.14 = (f32[4,2,256,128]{3,2,1,0:T(8,128)}, f32[4,2,256,128]{3,2,1,0:T(8,128)S(1)}, u32[]{:S(2)}) copy-start(f32[4,2,256,128]{3,2,1,0:T(8,128)S(1)} %get-tuple-element.39.refs_8_) | copy-start | bytes 3145732
  2.7 125.8 %copy-start.26 = (s32[1,8,1,8]{3,2,1,0:T(1,128)S(1)}, s32[1,8,1,8]{3,2,1,0:T(1,128)}, u32[]{:S(2)}) copy-start(s32[1,8,1,8]{3,2,1,0:T(1,128)} %param.7) | copy-start | bytes 772
  2.7 125.8 %copy-start.10 = (s32[1,8,1,16]{3,2,1,0:T(1,128)S(1)}, s32[1,8,1,16]{3,2,1,0:T(1,128)}, u32[]{:S(2)}) copy-start(s32[1,8,1,16]{3,2,1,0:T(1,128)} %param.9) | copy-start | bytes 1540
  2.7 24.1 %collective-permute-start.13 = (f32[4,2,256,128]{3,2,1,0:T(8,128)S(1)}, f32[4,2,256,128]{3,2,1,0:T(8,128)S(1)}, u32[]{:S(2)}, u32[]{:S(2)}) collective-permute-start(f32[4,2,256,128]{3,2,1,0:T(8,128)S(1)} %get-tuple-element.43.refs_7_), channel_id=1, source_target_pairs={{0,4},{4,0},{8,12},{12,8},{1,5},{5,1},{9,13},{13,9},{2,6},{6,2},{1... | collective-permute-start | bytes 3145736 | tf_op jit(solution)/shard_map/ppermute | solution.py:131
  4.0 24.0 %collective-permute-start.12 = (f32[4,2,256,128]{3,2,1,0:T(8,128)S(1)}, f32[4,2,256,128]{3,2,1,0:T(8,128)S(1)}, u32[]{:S(2)}, u32[]{:S(2)}) collective-permute-start(f32[4,2,256,128]{3,2,1,0:T(8,128)S(1)} %get-tuple-element.39.refs_8_), channel_id=1, source_target_pairs={{0,8},{4,12},{8,0},{12,4},{1,9},{5,13},{9,1},{13,5},{2,10},{6,14},... | collective-permute-start | bytes 3145736 | tf_op jit(solution)/shard_map/ppermute | solution.py:131
  5.4 25.3 %collective-permute-start.4 = (f32[4,2,128,256]{3,2,1,0:T(8,128)S(1)}, f32[4,2,128,256]{3,2,1,0:T(8,128)S(1)}, u32[]{:S(2)}, u32[]{:S(2)}) collective-permute-start(f32[4,2,128,256]{3,2,1,0:T(8,128)S(1)} %get-tuple-element.57.refs_0_), channel_id=1, source_target_pairs={{1,0},{2,1},{3,2},{5,4},{6,5},{7,6},{9,8},{10,9},{11,10},{13,12},{... | collective-permute-start | bytes 3145736 | tf_op jit(solution)/shard_map/ppermute | solution.py:131
  7.5 25.4 %collective-permute-start = (f32[4,2,128,256]{3,2,1,0:T(8,128)S(1)}, f32[4,2,128,256]{3,2,1,0:T(8,128)S(1)}, u32[]{:S(2)}, u32[]{:S(2)}) collective-permute-start(f32[4,2,128,256]{3,2,1,0:T(8,128)S(1)} %get-tuple-element.57.refs_0_), channel_id=1, source_target_pairs={{0,1},{1,2},{2,3},{4,5},{5,6},{6,7},{8,9},{9,10},{10,11},{12,13},{... | collective-permute-start | bytes 3145736 | tf_op jit(solution)/shard_map/ppermute | solution.py:131
  26.8 101.4 %copy-start.16 = (f32[4,2,256,128]{3,2,1,0:T(8,128)}, f32[4,2,256,128]{3,2,1,0:T(8,128)S(1)}, u32[]{:S(2)}) copy-start(f32[4,2,256,128]{3,2,1,0:T(8,128)S(1)} %collective-permute-done.13.refs_9_) | copy-start | bytes 3145732
  26.8 23.1 %collective-permute-start.14 = (f32[4,2,256,128]{3,2,1,0:T(8,128)S(1)}, f32[4,2,256,128]{3,2,1,0:T(8,128)S(1)}, u32[]{:S(2)}, u32[]{:S(2)}) collective-permute-start(f32[4,2,256,128]{3,2,1,0:T(8,128)S(1)} %get-tuple-element.39.refs_8_), channel_id=1, source_target_pairs={{0,4},{4,0},{8,12},{12,8},{1,5},{5,1},{9,13},{13,9},{2,6},{6,2},{1... | collective-permute-start | bytes 3145736 | tf_op jit(solution)/shard_map/ppermute | solution.py:131
  28.0 23.1 %collective-permute-start.18 = (f32[4,2,256,128]{3,2,1,0:T(8,128)S(1)}, f32[4,2,256,128]{3,2,1,0:T(8,128)S(1)}, u32[]{:S(2)}, u32[]{:S(2)}) collective-permute-start(f32[4,2,256,128]{3,2,1,0:T(8,128)S(1)} %get-tuple-element.43.refs_7_), channel_id=1, source_target_pairs={{0,8},{4,12},{8,0},{12,4},{1,9},{5,13},{9,1},{13,5},{2,10},{6,14},... | collective-permute-start | bytes 3145736 | tf_op jit(solution)/shard_map/ppermute | solution.py:131
  30.7 22.3 %collective-permute-start.5 = (f32[4,2,128,256]{3,2,1,0:T(8,128)S(1)}, f32[4,2,128,256]{3,2,1,0:T(8,128)S(1)}, u32[]{:S(2)}, u32[]{:S(2)}) collective-permute-start(f32[4,2,128,256]{3,2,1,0:T(8,128)S(1)} %collective-permute-done.4.refs_2_), channel_id=1, source_target_pairs={{1,0},{2,1},{5,4},{6,5},{9,8},{10,9},{13,12},{14,13},{17,16},{18,1... | collective-permute-start | bytes 3145736 | tf_op jit(solution)/shard_map/ppermute | solution.py:131
  32.8 24.1 %collective-permute-start.1 = (f32[4,2,128,256]{3,2,1,0:T(8,128)S(1)}, f32[4,2,128,256]{3,2,1,0:T(8,128)S(1)}, u32[]{:S(2)}, u32[]{:S(2)}) collective-permute-start(f32[4,2,128,256]{3,2,1,0:T(8,128)S(1)} %collective-permute-done.refs_1_), channel_id=1, source_target_pairs={{1,2},{2,3},{5,6},{6,7},{9,10},{10,11},{13,14},{14,15},{17,18},{18... | collective-permute-start | bytes 3145736 | tf_op jit(solution)/shard_map/ppermute | solution.py:131
  49.9 22.2 %collective-permute-start.15 = (f32[4,2,256,128]{3,2,1,0:T(8,128)S(1)}, f32[4,2,256,128]{3,2,1,0:T(8,128)S(1)}, u32[]{:S(2)}, u32[]{:S(2)}) collective-permute-start(f32[4,2,256,128]{3,2,1,0:T(8,128)S(1)} %collective-permute-done.12.refs_12_), channel_id=1, source_target_pairs={{0,4},{4,0},{8,12},{12,8},{1,5},{5,1},{9,13},{13,9},{2,6},{6,2},{1... | collective-permute-start | bytes 3145736 | tf_op jit(solution)/shard_map/ppermute | solution.py:131
  51.1 22.2 %collective-permute-start.19 = (f32[4,2,256,128]{3,2,1,0:T(8,128)S(1)}, f32[4,2,256,128]{3,2,1,0:T(8,128)S(1)}, u32[]{:S(2)}, u32[]{:S(2)}) collective-permute-start(f32[4,2,256,128]{3,2,1,0:T(8,128)S(1)} %collective-permute-done.13.refs_9_), channel_id=1, source_target_pairs={{0,8},{4,12},{8,0},{12,4},{1,9},{5,13},{9,1},{13,5},{2,10},{6,14},... | collective-permute-start | bytes 3145736 | tf_op jit(solution)/shard_map/ppermute | solution.py:131
  53.0 21.5 %collective-permute-start.6 = (f32[4,2,128,256]{3,2,1,0:T(8,128)S(1)}, f32[4,2,128,256]{3,2,1,0:T(8,128)S(1)}, u32[]{:S(2)}, u32[]{:S(2)}) collective-permute-start(f32[4,2,128,256]{3,2,1,0:T(8,128)S(1)} %collective-permute-done.5.refs_4_), channel_id=1, source_target_pairs={{1,0},{5,4},{9,8},{13,12},{17,16},{21,20},{25,24},{29,28}} | collective-permute-start | bytes 3145736 | tf_op jit(solution)/shard_map/ppermute | solution.py:131
  56.9 22.0 %collective-permute-start.2 = (f32[4,2,128,256]{3,2,1,0:T(8,128)S(1)}, f32[4,2,128,256]{3,2,1,0:T(8,128)S(1)}, u32[]{:S(2)}, u32[]{:S(2)}) collective-permute-start(f32[4,2,128,256]{3,2,1,0:T(8,128)S(1)} %collective-permute-done.1.refs_3_), channel_id=1, source_target_pairs={{2,3},{6,7},{10,11},{14,15},{18,19},{22,23},{26,27},{30,31}} | collective-permute-start | bytes 3145736 | tf_op jit(solution)/shard_map/ppermute | solution.py:131
  72.1 21.7 %collective-permute-start.16 = (f32[4,2,256,128]{3,2,1,0:T(8,128)S(1)}, f32[4,2,256,128]{3,2,1,0:T(8,128)}, u32[]{:S(2)}, u32[]{:S(2)}) collective-permute-start(f32[4,2,256,128]{3,2,1,0:T(8,128)S(1)} %get-tuple-element.46.refs_7_), channel_id=1, source_target_pairs={{0,4},{4,0},{8,12},{12,8},{1,5},{5,1},{9,13},{13,9},{2,6},{6,2},{1... | collective-permute-start | bytes 3145736 | tf_op jit(solution)/shard_map/ppermute | solution.py:131
  73.3 21.7 %collective-permute-start.20 = (f32[4,2,256,128]{3,2,1,0:T(8,128)S(1)}, f32[4,2,256,128]{3,2,1,0:T(8,128)}, u32[]{:S(2)}, u32[]{:S(2)}) collective-permute-start(f32[4,2,256,128]{3,2,1,0:T(8,128)S(1)} %get-tuple-element.45.refs_8_), channel_id=1, source_target_pairs={{0,8},{4,12},{8,0},{12,4},{1,9},{5,13},{9,1},{13,5},{2,10},{6,14},... | collective-permute-start | bytes 3145736 | tf_op jit(solution)/shard_map/ppermute | solution.py:131
  74.5 22.5 %collective-permute-start.7 = (f32[4,2,128,256]{3,2,1,0:T(8,128)S(1)}, f32[4,2,128,256]{3,2,1,0:T(8,128)S(1)}, u32[]{:S(2)}, u32[]{:S(2)}) collective-permute-start(f32[4,2,128,256]{3,2,1,0:T(8,128)S(1)} %get-tuple-element.34.refs_0_), channel_id=1, source_target_pairs={{1,0},{2,1},{3,2},{5,4},{6,5},{7,6},{9,8},{10,9},{11,10},{13,12},{... | collective-permute-start | bytes 3145736 | tf_op jit(solution)/shard_map/ppermute | solution.py:131
  78.9 24.2 %collective-permute-start.3 = (f32[4,2,128,256]{3,2,1,0:T(8,128)S(1)}, f32[4,2,128,256]{3,2,1,0:T(8,128)S(1)}, u32[]{:S(2)}, u32[]{:S(2)}) collective-permute-start(f32[4,2,128,256]{3,2,1,0:T(8,128)S(1)} %get-tuple-element.34.refs_0_), channel_id=1, source_target_pairs={{0,1},{1,2},{2,3},{4,5},{5,6},{6,7},{8,9},{9,10},{10,11},{12,13},{... | collective-permute-start | bytes 3145736 | tf_op jit(solution)/shard_map/ppermute | solution.py:131
  93.8 21.6 %collective-permute-start.17 = (f32[4,2,256,128]{3,2,1,0:T(8,128)S(1)}, f32[4,2,256,128]{3,2,1,0:T(8,128)S(1)}, u32[]{:S(2)}, u32[]{:S(2)}) collective-permute-start(f32[4,2,256,128]{3,2,1,0:T(8,128)S(1)} %get-tuple-element.45.refs_8_), channel_id=1, source_target_pairs={{0,4},{4,0},{8,12},{12,8},{1,5},{5,1},{9,13},{13,9},{2,6},{6,2},{1... | collective-permute-start | bytes 3145736 | tf_op jit(solution)/shard_map/ppermute | solution.py:131
  95.0 21.6 %collective-permute-start.21 = (f32[4,2,256,128]{3,2,1,0:T(8,128)S(1)}, f32[4,2,256,128]{3,2,1,0:T(8,128)S(1)}, u32[]{:S(2)}, u32[]{:S(2)}) collective-permute-start(f32[4,2,256,128]{3,2,1,0:T(8,128)S(1)} %get-tuple-element.46.refs_7_), channel_id=1, source_target_pairs={{0,8},{4,12},{8,0},{12,4},{1,9},{5,13},{9,1},{13,5},{2,10},{6,14},... | collective-permute-start | bytes 3145736 | tf_op jit(solution)/shard_map/ppermute | solution.py:131
  97.0 21.8 %collective-permute-start.9 = (f32[4,2,128,256]{3,2,1,0:T(8,128)S(1)}, f32[4,2,128,256]{3,2,1,0:T(8,128)}, u32[]{:S(2)}, u32[]{:S(2)}) collective-permute-start(f32[4,2,128,256]{3,2,1,0:T(8,128)S(1)} %collective-permute-done.7.refs_2_), channel_id=1, source_target_pairs={{1,0},{2,1},{5,4},{6,5},{9,8},{10,9},{13,12},{14,13},{17,16},{18,1... | collective-permute-start | bytes 3145736 | tf_op jit(solution)/shard_map/ppermute | solution.py:131
  103.1 21.5 %collective-permute-start.8 = (f32[4,2,128,256]{3,2,1,0:T(8,128)S(1)}, f32[4,2,128,256]{3,2,1,0:T(8,128)}, u32[]{:S(2)}, u32[]{:S(2)}) collective-permute-start(f32[4,2,128,256]{3,2,1,0:T(8,128)S(1)} %collective-permute-done.3.refs_1_), channel_id=1, source_target_pairs={{1,2},{2,3},{5,6},{6,7},{9,10},{10,11},{13,14},{14,15},{17,18},{18... | collective-permute-start | bytes 3145736 | tf_op jit(solution)/shard_map/ppermute | solution.py:131
  115.4 50.6 %collective-permute-start.23 = (f32[4,2,256,128]{3,2,1,0:T(8,128)}, f32[4,2,256,128]{3,2,1,0:T(8,128)}, u32[]{:S(2)}, u32[]{:S(2)}) collective-permute-start(f32[4,2,256,128]{3,2,1,0:T(8,128)} %collective-permute-done.20.refs_12_), channel_id=1, source_target_pairs={{0,4},{4,0},{8,12},{12,8},{1,5},{5,1},{9,13},{13,9},{2,6},{6,2},{1... | collective-permute-start | bytes 3145736 | tf_op jit(solution)/shard_map/ppermute | solution.py:131
  116.6 49.4 %collective-permute-start.22 = (f32[4,2,256,128]{3,2,1,0:T(8,128)}, f32[4,2,256,128]{3,2,1,0:T(8,128)}, u32[]{:S(2)}, u32[]{:S(2)}) collective-permute-start(f32[4,2,256,128]{3,2,1,0:T(8,128)} %collective-permute-done.16.refs_9_), channel_id=1, source_target_pairs={{0,8},{4,12},{8,0},{12,4},{1,9},{5,13},{9,1},{13,5},{2,10},{6,14},... | collective-permute-start | bytes 3145736 | tf_op jit(solution)/shard_map/ppermute | solution.py:131
  118.8 47.2 %collective-permute-start.11 = (f32[4,2,128,256]{3,2,1,0:T(8,128)}, f32[4,2,128,256]{3,2,1,0:T(8,128)}, u32[]{:S(2)}, u32[]{:S(2)}) collective-permute-start(f32[4,2,128,256]{3,2,1,0:T(8,128)} %collective-permute-done.9.refs_4_), channel_id=1, source_target_pairs={{1,0},{5,4},{9,8},{13,12},{17,16},{21,20},{25,24},{29,28}} | collective-permute-start | bytes 3145736 | tf_op jit(solution)/shard_map/ppermute | solution.py:131
  124.7 41.4 %collective-permute-start.10 = (f32[4,2,128,256]{3,2,1,0:T(8,128)}, f32[4,2,128,256]{3,2,1,0:T(8,128)}, u32[]{:S(2)}, u32[]{:S(2)}) collective-permute-start(f32[4,2,128,256]{3,2,1,0:T(8,128)} %collective-permute-done.8.refs_3_), channel_id=1, source_target_pairs={{2,3},{6,7},{10,11},{14,15},{18,19},{22,23},{26,27},{30,31}} | collective-permute-start | bytes 3145736 | tf_op jit(solution)/shard_map/ppermute | solution.py:131
  201.6 13.8 %collective-permute-start.24 = (f32[512,2048]{1,0:T(8,128)}, f32[512,2048]{1,0:T(8,128)S(1)}, u32[]{:S(2)}, u32[]{:S(2)}) collective-permute-start(f32[512,2048]{1,0:T(8,128)} %get-tuple-element.52), channel_id=1, source_target_pairs={{0,16},{16,0},{1,17},{17,1},{2,18},{18,2},{3,19},{19,3},{4,20},{20... | collective-permute-start | bytes 12582920 | tf_op jit(solution)/shard_map/ppermute | solution.py:190
  (20 other events, 575.8 us)

commit v2 on v1

v2 whole, which is shorter than its diff:
```python
import functools

import jax
import jax.numpy as jnp
from jax import lax
from jax.experimental import pallas as pl
from jax.experimental.pallas import tpu as pltpu
from jax.sharding import PartitionSpec as P

W = 256
B = 128
AR = 8
AC = 16
HALF = AR * B // 2
F32 = jnp.float32
BF16 = jnp.bfloat16


def split(x):
    hi = x.astype(BF16)
    return hi, (x - hi.astype(F32)).astype(BF16)


def dot(a, b):
    return jnp.dot(a, b, preferred_element_type=F32)


def update_kernel(n_l, n_u, start, first, l_tgt, u_tgt, l_base, u_base, *refs):
    l_refs, refs = refs[:n_l], refs[n_l:]
    u_refs, refs = refs[:n_u], refs[n_u:]
    inv_ref, keep_in, _, send, keep, token, raw_h, raw_l, l_cat, u_cat = refs
    step = pl.program_id(0)
    node = start + step

    @pl.when(step == 0)
    def _():
        token[...] = jnp.zeros_like(token)
        if first:
            keep[...] = keep_in[...]
            send[...] = jnp.zeros_like(send)

    raw_h[...] = jnp.zeros_like(raw_h)
    raw_l[...] = jnp.zeros_like(raw_l)
    for b, ref in enumerate(l_refs):
        base = l_base[b]
        for j in range(ref.shape[1]):
            tgt = jnp.where(base >= 0, l_tgt[node, jnp.maximum(base, 0) + j], -1)

            @pl.when(tgt >= 0)
            def _(ref=ref, j=j, tgt=tgt):
                rows = pl.ds(pl.multiple_of(tgt * B, B), B)
                hi, lo = split(ref[0, j])
                raw_h[rows, :] = hi
                raw_l[rows, :] = lo

    inv_h, inv_l = split(inv_ref[0])
    for m in range(0, AR * B, 256):
        rh, rl = raw_h[m : m + 256, :], raw_l[m : m + 256, :]
        hi, lo = split(dot(rh, inv_h) + dot(rh, inv_l) + dot(rl, inv_h))
        l_cat[m : m + 256, 0:W] = hi
        l_cat[m : m + 256, W : 2 * W] = lo

    u_cat[...] = jnp.zeros_like(u_cat)
    for b, ref in enumerate(u_refs):
        base = u_base[b]
        for j in range(ref.shape[1]):
            tgt = u_tgt[node, base + j]

            @pl.when(tgt >= 0)
            def _(ref=ref, j=j, tgt=tgt):
                cols = pl.ds(pl.multiple_of(tgt * B, B), B)
                hi, lo = split(ref[0, j])
                u_cat[0:W, cols] = hi
                u_cat[W : 2 * W, cols] = lo

    uh, ul = u_cat[0:W, :], u_cat[W : 2 * W, :]

    def product(rows):
        lh, ll = l_cat[rows, 0:W], l_cat[rows, W : 2 * W]
        return dot(lh, uh) + dot(ll, uh) + dot(lh, ul)

    send[...] += product(slice(0, HALF))
    keep[...] -= product(slice(HALF, 2 * HALF))


def apply_update(nodes, offsets, tables, l_bufs, u_bufs, u11_inv, send, keep):
    start, stop = nodes
    width = keep.shape[1]
    first = send is None

    def per_node(buf, offset):
        return pl.BlockSpec((1,) + buf.shape[1:], lambda s, *_: (offset + s, 0, 0, 0))

    vmem = pl.BlockSpec(memory_space=pltpu.VMEM)
    acc = pltpu.VMEM((HALF, width), F32)
    n_in = 4 + len(l_bufs) + len(u_bufs)
    last = jnp.zeros((8, 128), F32) if first else send
    l_bufs, u_bufs = ([pltpu.with_memory_space_constraint(b, pltpu.HBM) for b in bufs] for bufs in (l_bufs, u_bufs))
    return pl.pallas_call(
        functools.partial(update_kernel, len(l_bufs), len(u_bufs), start, first),
        out_shape=(acc, acc, jax.ShapeDtypeStruct((8, 128), F32)),
        grid_spec=pltpu.PrefetchScalarGridSpec(
            num_scalar_prefetch=4,
            grid=(stop - start,),
            in_specs=[per_node(b, o) for b, o in zip([*l_bufs, *u_bufs], offsets)]
            + [pl.BlockSpec((1, W, W), lambda s, *_: (start + s, 0, 0)), vmem, vmem],
            out_specs=(vmem, vmem, vmem),
            scratch_shapes=[
                pltpu.VMEM((AR * B, W), BF16),
                pltpu.VMEM((AR * B, W), BF16),
                pltpu.VMEM((AR * B, 2 * W), BF16),
                pltpu.VMEM((2 * W, AC * B), BF16),
            ],
        ),
        input_output_aliases={} if first else {n_in + 1: 1, n_in + 2: 0},
        compiler_params=pltpu.CompilerParams(
            dimension_semantics=("arbitrary",), vmem_limit_bytes=32 << 20
        ),
    )(*tables, *l_bufs, *u_bufs, u11_inv, keep, last)


class Link:
    def __init__(self, axis):
        self.axis, self.after = axis, []

    def send(self, x, pairs):
        if self.after:
            x = lax.optimization_barrier((x, *self.after))[0]
        out = lax.ppermute(x, self.axis, pairs)
        self.after = [out]
        return out


def up(hop):
    return [(z, z + 1) for z in range(hop - 1, 3)]


def down(hop):
    return [(z, z - 1) for z in range(1, 5 - hop)]


def side(mask):
    return [(r, r ^ mask) for r in range(4)]


def hold(links, token):
    for link in links:
        link.after.append(token)


class Exchange:
    def __init__(self, links, l_chunk, u_h0, u_h1):
        self.links = links
        self.l, self.h = l_chunk, (u_h0, u_h1)

    def first(self):
        lx, ly, lu, ld = self.links
        self.u1, self.d1 = lu.send(self.l, up(1)), ld.send(self.l, down(1))
        self.x0, self.y1 = lx.send(self.h[0], side(1)), ly.send(self.h[1], side(2))

    def second(self):
        lx, ly, lu, ld = self.links
        self.u2, self.d2 = lu.send(self.u1, up(2)), ld.send(self.d1, down(2))
        self.x1, self.y0 = lx.send(self.h[1], side(1)), ly.send(self.h[0], side(2))

    def third(self, here):
        lx, ly, lu, ld = self.links
        u3, d3 = lu.send(self.u2[here], up(3)), ld.send(self.d2[here], down(3))
        f1, f0 = lx.send(self.y1[here], side(1)), ly.send(self.x0[here], side(2))
        return (u3, d3), (f0, f1)

    def buffers(self, third):
        l_bufs = [self.l, self.u1, self.d1, self.u2, self.d2, *third[0]]
        u_bufs = [*self.h, self.x0, self.x1, self.y0, self.y1, *third[1]]
        return l_bufs, u_bufs


def body(rows, cols, l_panel, l_rows, u_panel, u_cols, u11_inv, ancestor):
    gz, row, col = (lax.axis_index(a) for a in ("gz", "row", "col"))
    l_own, u_own, inv = l_panel[0, :, 0], u_panel[0, :, 0], u11_inv[0]
    nodes, l_slots = l_own.shape[:2]
    u_slots = u_own.shape[1]
    l_tgt = l_rows[0, :, 0]
    l_tgt = jnp.where(l_tgt < 0, -1, (l_tgt + (AR // 2) * (1 - gz)) % AR)
    u_tgt = u_cols[0, :, 0]
    keep, send = ancestor[0], None

    if rows == 4 and cols == 4:
        half = u_slots // 2
        sources = jnp.stack([col, col - 1, col + 1, col - 2, col + 2, col - 3, col + 3])
        l_base = jnp.where((sources >= 0) & (sources < cols), sources * l_slots, -1)
        squares = jnp.stack([row, row, row ^ 1, row ^ 1, row ^ 2, row ^ 2, row ^ 3, row ^ 3])
        u_base = squares * u_slots + half * (jnp.arange(8, dtype=jnp.int32) % 2)
        tables = [t.astype(jnp.int32) for t in (l_tgt, u_tgt, l_base, u_base)]
        links = [Link("row"), Link("row"), Link("col"), Link("col")]
        size, part = nodes // 2, nodes // 4
        chunks = []
        for start in (0, size):
            here = slice(start, start + size)
            chunks.append(Exchange(links, l_own[here], u_own[here, :half], u_own[here, half:]))
        one, two = chunks

        one.first()
        one.second()
        bufs = one.buffers(one.third(slice(0, size)))
        two.first()
        send, keep, token = apply_update((0, part), [0] * 15, tables, *bufs, inv, send, keep)
        hold(links, token)
        two.second()
        send, keep, token = apply_update((part, size), [part] * 15, tables, *bufs, inv, send, keep)
        hold(links, token)
        for k in range(2):
            bufs = two.buffers(two.third(slice(k * part, (k + 1) * part)))
            at = [k * part] * 5 + [0] * 2 + [k * part] * 6 + [0] * 2
            nodes_now = (size + k * part, size + (k + 1) * part)
            send, keep, token = apply_update(nodes_now, at, tables, *bufs, inv, send, keep)
    else:
        l_all = lax.all_gather(l_own, "col", axis=1, tiled=True)
        u_all = lax.all_gather(u_own, "row", axis=1, tiled=True)
        zero = jnp.zeros((1,), jnp.int32)
        tables = [t.astype(jnp.int32) for t in (l_tgt, u_tgt, zero, zero)]
        send, keep, _ = apply_update((0, nodes), [0, 0], tables, [l_all], [u_all], inv, send, keep)

    other = lax.ppermute(send, "gz", [(0, 1), (1, 0)])
    return (keep - other)[None]


def solution(mesh):
    in_specs = (
        P("gz", None, "row", "col", None, None),
        P("gz", None, "row", None),
        P("gz", None, "col", "row", None, None),
        P("gz", None, "col", None),
        P("gz", None, None, None),
        P("row", "gz", "col"),
    )
    return jax.shard_map(
        functools.partial(body, mesh.shape["row"], mesh.shape["col"]),
        mesh=mesh,
        in_specs=in_specs,
        out_specs=P("row", "gz", "col"),
        check_vma=False,
    )
```

time: 222 us -> 188 us (0.85)
  Pallas kernels: 69.4 us -> 53.8 us
  waiting for transfers between devices: 77.4 us -> 64.1 us
    pallas_call x2 -> x4, Pallas kernels: 69.4 us -> 53.8 us  [apply_update(): pl.pallas_call(functools.partial(update_kernel, len(l_bufs), len(u_bufs),...]
    ppermute x24 -> x28, waiting for transfers between devices: 70.4 us -> 57.3 us  [send(): out = lax.ppermute(x, self.axis, pairs)]
    unnamed x54 -> x66, local copies, waits for them, and re-layouts: 8.66 us -> 3.53 us
    slice x1 -> x5, local copies, waits for them, and re-layouts: 2.6 us -> 5.51 us  [the longest x1 4.03 us: body(): u_own[here, half:]]
    ppermute x24 -> x28, starting transfers between devices: 49.8 us -> 47.2 us  [send(): out = lax.ppermute(x, self.axis, pairs)]
    ppermute x1, starting transfers between devices: 6.78 us -> 9.23 us  [body(): other = lax.ppermute(send, 'gz', [(0, 1), (1, 0)])]
  transfers between devices with their start and end apart: 25 -> 29, of which waited for: 13 -> 11; matrix products, arithmetic and copies ran while one was open for 0% -> 2% of each run, Pallas kernels for 15% -> 22%
where the time goes in v2:
time: 188 us
  waiting for transfers between devices  64.1 us (34%)
  starting transfers between devices  56.4 us (30%)
  Pallas kernels  53.8 us (29%)
  local copies, waits for them, and re-layouts  10.4 us (6%)
  other arithmetic  2.8 us (1%)
    ppermute x28, waiting for transfers between devices, send(): out = lax.ppermute(x, self.axis, pairs)  57.3 us
    pallas_call x4, Pallas kernels, apply_update(): pl.pallas_call(functools.partial(update_kernel, len(l_bufs), len(u_bufs),...  53.8 us
    ppermute x28, starting transfers between devices, send(): out = lax.ppermute(x, self.axis, pairs)  47.2 us
    ppermute x1, starting transfers between devices, body(): other = lax.ppermute(send, 'gz', [(0, 1), (1, 0)])  9.23 us
    ppermute x1, waiting for transfers between devices, body(): other = lax.ppermute(send, 'gz', [(0, 1), (1, 0)])  6.79 us
    slice x1, local copies, waits for them, and re-layouts, body(): u_own[here, half:]  4.03 us
  transfers between devices with their start and end apart: 29, of which 11 were waited for; matrix products, arithmetic and copies ran while one was open for 2% of the time, Pallas kernels for 22%

profile of v2, /device:TPU:17, one launch (start us, length us, event | category | flops | bytes accessed | tf_op | source)
XLA Modules:
  0.0 188.0 jit_solution(16534813494514259742)
XLA Ops:
  0.0 4.0 %fusion.4 = (f32[4,2,256,128]{3,2,1,0:T(8,128)}, f32[4,2,256,128]{3,2,1,0:T(8,128)}, f32[4,2,256,128]{3,2,1,0:T(8,128)S(1)}, f32[4,2,256,128]{3,2,1,0:T(8,128)S(1)}) fusion(f32[8,4,256,128]{3,2,1,0:T(8,128)} %bitcast.38), kind=kLoop, calls=%fused_computation.12 | loop fusion | bytes 8388608 | tf_op jit(solution)/shard_map/slice | solution.py:200
  4.1 1.3 collective-permute-start.10
  7.7 2.1 %collective-permute-start.4 = (f32[4,2,128,256]{3,2,1,0:T(8,128)S(1)}, f32[4,2,128,256]{3,2,1,0:T(8,128)S(1)}, u32[]{:S(2)}, u32[]{:S(2)}) collective-permute-start(f32[4,2,128,256]{3,2,1,0:T(8,128)S(1)} %get-tuple-element.77.refs_0_), channel_id=1, source_target_pairs={{1,0},{2,1},{3,2},{5,4},{6,5},{7,6},{9,8},{10,9},{11,10},{13,12},{... | collective-permute-start | bytes 3145736 | tf_op jit(solution)/shard_map/ppermute | solution.py:129
  9.8 3.3 %collective-permute-start = (f32[4,2,128,256]{3,2,1,0:T(8,128)S(1)}, f32[4,2,128,256]{3,2,1,0:T(8,128)S(1)}, u32[]{:S(2)}, u32[]{:S(2)}) collective-permute-start(f32[4,2,128,256]{3,2,1,0:T(8,128)S(1)} %get-tuple-element.77.refs_0_), channel_id=1, source_target_pairs={{0,1},{1,2},{2,3},{4,5},{5,6},{6,7},{8,9},{9,10},{10,11},{12,13},{... | collective-permute-start | bytes 3145736 | tf_op jit(solution)/shard_map/ppermute | solution.py:129
  13.1 16.0 %collective-permute-done.8.refs_9_ = f32[4,2,256,128]{3,2,1,0:T(8,128)S(1)} collective-permute-done((f32[4,2,256,128]{3,2,1,0:T(8,128)S(1)}, f32[4,2,256,128]{3,2,1,0:T(8,128)S(1)}, u32[]{:S(2)}, u32[]{:S(2)}) %collective-permute-start.8) | collective-permute-done | bytes 1048608 | tf_op jit(solution)/shard_map/ppermute | solution.py:129
  30.5 2.5 %collective-permute-done.4.refs_2_ = f32[4,2,128,256]{3,2,1,0:T(8,128)S(1)} collective-permute-done((f32[4,2,128,256]{3,2,1,0:T(8,128)S(1)}, f32[4,2,128,256]{3,2,1,0:T(8,128)S(1)}, u32[]{:S(2)}, u32[]{:S(2)}) %collective-permute-start.4) | collective-permute-done | bytes 1048608 | tf_op jit(solution)/shard_map/ppermute | solution.py:129
  33.0 2.1 %collective-permute-start.5 = (f32[4,2,128,256]{3,2,1,0:T(8,128)S(1)}, f32[4,2,128,256]{3,2,1,0:T(8,128)S(1)}, u32[]{:S(2)}, u32[]{:S(2)}) collective-permute-start(f32[4,2,128,256]{3,2,1,0:T(8,128)S(1)} %collective-permute-done.4.refs_2_), channel_id=1, source_target_pairs={{1,0},{2,1},{5,4},{6,5},{9,8},{10,9},{13,12},{14,13},{17,16},{18,1... | collective-permute-start | bytes 3145736 | tf_op jit(solution)/shard_map/ppermute | solution.py:129
  35.2 2.9 %collective-permute-start.1 = (f32[4,2,128,256]{3,2,1,0:T(8,128)S(1)}, f32[4,2,128,256]{3,2,1,0:T(8,128)S(1)}, u32[]{:S(2)}, u32[]{:S(2)}) collective-permute-start(f32[4,2,128,256]{3,2,1,0:T(8,128)S(1)} %collective-permute-done.refs_1_), channel_id=1, source_target_pairs={{1,2},{2,3},{5,6},{6,7},{9,10},{10,11},{13,14},{14,15},{17,18},{18... | collective-permute-start | bytes 3145736 | tf_op jit(solution)/shard_map/ppermute | solution.py:129
  38.1 13.8 %collective-permute-done.9.refs_10_ = f32[4,2,256,128]{3,2,1,0:T(8,128)S(1)} collective-permute-done((f32[4,2,256,128]{3,2,1,0:T(8,128)S(1)}, f32[4,2,256,128]{3,2,1,0:T(8,128)S(1)}, u32[]{:S(2)}, u32[]{:S(2)}) %collective-permute-start.9) | collective-permute-done | bytes 1048608 | tf_op jit(solution)/shard_map/ppermute | solution.py:129
  53.3 2.1 %collective-permute-done.5.refs_4_ = f32[4,2,128,256]{3,2,1,0:T(8,128)S(1)} collective-permute-done((f32[4,2,128,256]{3,2,1,0:T(8,128)S(1)}, f32[4,2,128,256]{3,2,1,0:T(8,128)S(1)}, u32[]{:S(2)}, u32[]{:S(2)}) %collective-permute-start.5) | collective-permute-done | bytes 1048608 | tf_op jit(solution)/shard_map/ppermute | solution.py:129
  56.1 3.2 %collective-permute-done.1.refs_3_ = f32[4,2,128,256]{3,2,1,0:T(8,128)S(1)} collective-permute-done((f32[4,2,128,256]{3,2,1,0:T(8,128)S(1)}, f32[4,2,128,256]{3,2,1,0:T(8,128)S(1)}, u32[]{:S(2)}, u32[]{:S(2)}) %collective-permute-start.1) | collective-permute-done | bytes 1048608 | tf_op jit(solution)/shard_map/ppermute | solution.py:129
  59.3 3.0 %collective-permute-start.2 = (f32[4,2,128,256]{3,2,1,0:T(8,128)S(1)}, f32[4,2,128,256]{3,2,1,0:T(8,128)S(1)}, u32[]{:S(2)}, u32[]{:S(2)}) collective-permute-start(f32[4,2,128,256]{3,2,1,0:T(8,128)S(1)} %collective-permute-done.1.refs_3_), channel_id=1, source_target_pairs={{2,3},{6,7},{10,11},{14,15},{18,19},{22,23},{26,27},{30,31}} | collective-permute-start | bytes 3145736 | tf_op jit(solution)/shard_map/ppermute | solution.py:129
  62.3 11.5 %collective-permute-done.13.refs_14_ = f32[4,2,256,128]{3,2,1,0:T(8,128)S(1)} collective-permute-done((f32[4,2,256,128]{3,2,1,0:T(8,128)S(1)}, f32[4,2,256,128]{3,2,1,0:T(8,128)S(1)}, u32[]{:S(2)}, u32[]{:S(2)}) %collective-permute-start.13) | collective-permute-done | bytes 1048608 | tf_op jit(solution)/shard_map/ppermute | solution.py:129
  73.7 1.3 collective-permute-start.20
  75.4 5.5 %collective-permute-start.7 = (f32[4,2,128,256]{3,2,1,0:T(8,128)}, f32[4,2,128,256]{3,2,1,0:T(8,128)}, u32[]{:S(2)}, u32[]{:S(2)}) collective-permute-start(f32[4,2,128,256]{3,2,1,0:T(8,128)} %get-tuple-element.44.refs_0_), channel_id=1, source_target_pairs={{1,0},{2,1},{3,2},{5,4},{6,5},{7,6},{9,8},{10,9},{11,10},{13,12},{... | collective-permute-start | bytes 3145736 | tf_op jit(solution)/shard_map/ppermute | solution.py:129
  81.3 4.1 %collective-permute-start.3 = (f32[4,2,128,256]{3,2,1,0:T(8,128)}, f32[4,2,128,256]{3,2,1,0:T(8,128)}, u32[]{:S(2)}, u32[]{:S(2)}) collective-permute-start(f32[4,2,128,256]{3,2,1,0:T(8,128)} %get-tuple-element.44.refs_0_), channel_id=1, source_target_pairs={{0,1},{1,2},{2,3},{4,5},{5,6},{6,7},{8,9},{9,10},{10,11},{12,13},{... | collective-permute-start | bytes 3145736 | tf_op jit(solution)/shard_map/ppermute | solution.py:129
  85.7 2.2 %copy-done.1 = f32[1,512,2048]{2,1,0:T(8,128)S(1)} copy-done((f32[1,512,2048]{2,1,0:T(8,128)S(1)}, f32[1,512,2048]{2,1,0:T(8,128)}, u32[]{:S(2)}) %copy-start.1) | copy-done | bytes 4194328
  87.9 13.8 %shard_map.64 = (f32[512,2048]{1,0:T(8,128)S(1)}, f32[512,2048]{1,0:T(8,128)S(1)}, f32[8,128]{1,0:T(8,128)}) custom-call(s32[8,8]{1,0:T(8,128)S(1)} %fusion.1.l_tgt, s32[8,16]{1,0:T(8,128)S(1)} %bitcast.34, s32[7]{0:T(128)S(1)} %and_select_fusion.1.l_base, s32[8]{0:T(128)S(1)} %fusion.3.u_base, f32[4,2,128,256]{3,2,1,0:T(8,128)} %copy-done.6, ...), custom_call_target="tpu_custom_call" | custom-call | tf_op jit(solution)/shard_map/pallas_call | solution.py:99
  102.7 2.7 %collective-permute-start.15 = (f32[4,2,128,256]{3,2,1,0:T(8,128)}, f32[4,2,128,256]{3,2,1,0:T(8,128)S(1)}, u32[]{:S(2)}, u32[]{:S(2)}) collective-permute-start(f32[4,2,128,256]{3,2,1,0:T(8,128)} %collective-permute-done.7.refs_2_), channel_id=1, source_target_pairs={{1,0},{2,1},{5,4},{6,5},{9,8},{10,9},{13,12},{14,13},{17,16},{18,1... | collective-permute-start | bytes 3145736 | tf_op jit(solution)/shard_map/ppermute | solution.py:129
  105.4 2.7 %collective-permute-start.14 = (f32[4,2,128,256]{3,2,1,0:T(8,128)}, f32[4,2,128,256]{3,2,1,0:T(8,128)S(1)}, u32[]{:S(2)}, u32[]{:S(2)}) collective-permute-start(f32[4,2,128,256]{3,2,1,0:T(8,128)} %collective-permute-done.3.refs_1_), channel_id=1, source_target_pairs={{1,2},{2,3},{5,6},{6,7},{9,10},{10,11},{13,14},{14,15},{17,18},{18... | collective-permute-start | bytes 3145736 | tf_op jit(solution)/shard_map/ppermute | solution.py:129
  108.1 13.3 %shard_map.65 = (f32[512,2048]{1,0:T(8,128)S(1)}, f32[512,2048]{1,0:T(8,128)S(1)}, f32[8,128]{1,0:T(8,128)}) custom-call(s32[8,8]{1,0:T(8,128)S(1)} %fusion.1.l_tgt, s32[8,16]{1,0:T(8,128)S(1)} %bitcast.35, s32[7]{0:T(128)S(1)} %and_select_fusion.1.l_base, s32[8]{0:T(128)S(1)} %fusion.3.u_base, ...), custom_call_target="tpu_custom_call", output_to_operand_aliasing={{1}: (20, {}), {0}: (21, {})} | custom-call | tf_op jit(solution)/shard_map/pallas_call | solution.py:99
  121.5 1.3 fusion.5
  124.9 2.7 %collective-permute-done.14.refs_3_ = f32[4,2,128,256]{3,2,1,0:T(8,128)S(1)} collective-permute-done((f32[4,2,128,256]{3,2,1,0:T(8,128)}, f32[4,2,128,256]{3,2,1,0:T(8,128)S(1)}, u32[]{:S(2)}, u32[]{:S(2)}) %collective-permute-start.14) | collective-permute-done | bytes 1048608 | tf_op jit(solution)/shard_map/ppermute | solution.py:129
  127.7 1.9 %collective-permute-start.16 = (f32[2,2,128,256]{3,2,1,0:T(8,128)S(1)}, f32[2,2,128,256]{3,2,1,0:T(8,128)S(1)}, u32[]{:S(2)}, u32[]{:S(2)}) collective-permute-start(f32[2,2,128,256]{3,2,1,0:T(8,128)S(1)} %get-tuple-element.55), channel_id=1, source_target_pairs={{2,3},{6,7},{10,11},{14,15},{18,19},{22,23},{26,27},{30,31}} | collective-permute-start | bytes 1572872 | tf_op jit(solution)/shard_map/ppermute | solution.py:129
  129.6 3.7 %collective-permute-done.26.refs_14_ = f32[2,2,256,128]{3,2,1,0:T(8,128)S(1)} collective-permute-done((f32[2,2,256,128]{3,2,1,0:T(8,128)S(1)}, f32[2,2,256,128]{3,2,1,0:T(8,128)S(1)}, u32[]{:S(2)}, u32[]{:S(2)}) %collective-permute-start.26) | collective-permute-done | bytes 524320 | tf_op jit(solution)/shard_map/ppermute | solution.py:129
  135.2 1.5 collective-permute-done.16.refs_5_
  136.7 4.3 %collective-permute-start.17 = (f32[2,2,128,256]{3,2,1,0:T(8,128)S(1)}, f32[2,2,128,256]{3,2,1,0:T(8,128)S(1)}, u32[]{:S(2)}, u32[]{:S(2)}) collective-permute-start(f32[2,2,128,256]{3,2,1,0:T(8,128)S(1)} %get-tuple-element.56), channel_id=1, source_target_pairs={{2,3},{6,7},{10,11},{14,15},{18,19},{22,23},{26,27},{30,31}} | collective-permute-start | bytes 1572872 | tf_op jit(solution)/shard_map/ppermute | solution.py:129
  141.2 13.4 %shard_map.66 = (f32[512,2048]{1,0:T(8,128)S(1)}, f32[512,2048]{1,0:T(8,128)S(1)}, f32[8,128]{1,0:T(8,128)}) custom-call(s32[8,8]{1,0:T(8,128)S(1)} %fusion.1.l_tgt, s32[8,16]{1,0:T(8,128)S(1)} %bitcast.36, s32[7]{0:T(128)S(1)} %and_select_fusion.1.l_base, s32[8]{0:T(128)S(1)} %fusion.3.u_base, ...), custom_call_target="tpu_custom_call", output_to_operand_aliasing={{1}: (20, {}), {0}: (21, {})} | custom-call | tf_op jit(solution)/shard_map/pallas_call | solution.py:99
  155.9 13.3 %shard_map.67 = (f32[512,2048]{1,0:T(8,128)S(1)}, f32[512,2048]{1,0:T(8,128)S(1)}, f32[8,128]{1,0:T(8,128)}) custom-call(s32[8,8]{1,0:T(8,128)S(1)} %fusion.1.l_tgt, s32[8,16]{1,0:T(8,128)S(1)} %bitcast.37, s32[7]{0:T(128)S(1)} %and_select_fusion.1.l_base, s32[8]{0:T(128)S(1)} %fusion.3.u_base, ...), custom_call_target="tpu_custom_call", output_to_operand_aliasing={{1}: (20, {}), {0}: (21, {})} | custom-call | tf_op jit(solution)/shard_map/pallas_call | solution.py:99
  169.2 9.2 %collective-permute-start.28 = (f32[512,2048]{1,0:T(8,128)S(1)}, f32[512,2048]{1,0:T(8,128)S(1)}, u32[]{:S(2)}, u32[]{:S(2)}) collective-permute-start(f32[512,2048]{1,0:T(8,128)S(1)} %get-tuple-element.72), channel_id=1, source_target_pairs={{0,16},{16,0},{1,17},{17,1},{2,18},{18,2},{3,19},{19,3},{4,20},{20... | collective-permute-start | bytes 12582920 | tf_op jit(solution)/shard_map/ppermute | solution.py:224
  178.4 6.8 %collective-permute-done.28 = f32[512,2048]{1,0:T(8,128)S(1)} collective-permute-done((f32[512,2048]{1,0:T(8,128)S(1)}, f32[512,2048]{1,0:T(8,128)S(1)}, u32[]{:S(2)}, u32[]{:S(2)}) %collective-permute-start.28) | collective-permute-done | bytes 4194336 | tf_op jit(solution)/shard_map/ppermute | solution.py:224
  185.2 2.8 %subtract_bitcast_fusion = f32[1,512,2048]{2,1,0:T(8,128)} fusion(f32[512,2048]{1,0:T(8,128)S(1)} %get-tuple-element.71, f32[512,2048]{1,0:T(8,128)S(1)} %collective-permute-done.28), kind=kLoop, calls=%fused_computation | loop fusion | flops 1048576 | bytes 12582912 | tf_op jit(solution)/shard_map/broadcast_in_dim | solution.py:225
  (109 shorter events, 13.3 us)
Async XLA Ops:
  4.0 81.6 %copy-start.32 = (s32[1,8,1,8]{3,2,1,0:T(1,128)S(1)}, s32[1,8,1,8]{3,2,1,0:T(1,128)}, u32[]{:S(2)}) copy-start(s32[1,8,1,8]{3,2,1,0:T(1,128)} %param.7) | copy-start | bytes 772
  4.0 81.6 %copy-start = (f32[1,8,256,256]{3,2,1,0:T(8,128)S(1)}, f32[1,8,256,256]{3,2,1,0:T(8,128)}, u32[]{:S(2)}) copy-start(f32[1,8,256,256]{3,2,1,0:T(8,128)} %param.10) | copy-start | bytes 6291460
  4.0 81.6 %copy-start.2 = (s32[1,8,1,16]{3,2,1,0:T(1,128)S(1)}, s32[1,8,1,16]{3,2,1,0:T(1,128)}, u32[]{:S(2)}) copy-start(s32[1,8,1,16]{3,2,1,0:T(1,128)} %param.9) | copy-start | bytes 1540
  4.1 26.2 %collective-permute-start.10 = (f32[4,2,256,128]{3,2,1,0:T(8,128)S(1)}, f32[4,2,256,128]{3,2,1,0:T(8,128)S(1)}, u32[]{:S(2)}, u32[]{:S(2)}) collective-permute-start(f32[4,2,256,128]{3,2,1,0:T(8,128)S(1)} %get-tuple-element.45.refs_8_), channel_id=1, source_target_pairs={{0,8},{4,12},{8,0},{12,4},{1,9},{5,13},{9,1},{13,5},{2,10},{6,14},... | collective-permute-start | bytes 3145736 | tf_op jit(solution)/shard_map/ppermute | solution.py:129
  5.4 23.7 %collective-permute-start.8 = (f32[4,2,256,128]{3,2,1,0:T(8,128)S(1)}, f32[4,2,256,128]{3,2,1,0:T(8,128)S(1)}, u32[]{:S(2)}, u32[]{:S(2)}) collective-permute-start(f32[4,2,256,128]{3,2,1,0:T(8,128)S(1)} %get-tuple-element.46.refs_7_), channel_id=1, source_target_pairs={{0,4},{4,0},{8,12},{12,8},{1,5},{5,1},{9,13},{13,9},{2,6},{6,2},{1... | collective-permute-start | bytes 3145736 | tf_op jit(solution)/shard_map/ppermute | solution.py:129
  7.7 25.3 %collective-permute-start.4 = (f32[4,2,128,256]{3,2,1,0:T(8,128)S(1)}, f32[4,2,128,256]{3,2,1,0:T(8,128)S(1)}, u32[]{:S(2)}, u32[]{:S(2)}) collective-permute-start(f32[4,2,128,256]{3,2,1,0:T(8,128)S(1)} %get-tuple-element.77.refs_0_), channel_id=1, source_target_pairs={{1,0},{2,1},{3,2},{5,4},{6,5},{7,6},{9,8},{10,9},{11,10},{13,12},{... | collective-permute-start | bytes 3145736 | tf_op jit(solution)/shard_map/ppermute | solution.py:129
  9.8 25.4 %collective-permute-start = (f32[4,2,128,256]{3,2,1,0:T(8,128)S(1)}, f32[4,2,128,256]{3,2,1,0:T(8,128)S(1)}, u32[]{:S(2)}, u32[]{:S(2)}) collective-permute-start(f32[4,2,128,256]{3,2,1,0:T(8,128)S(1)} %get-tuple-element.77.refs_0_), channel_id=1, source_target_pairs={{0,1},{1,2},{2,3},{4,5},{5,6},{6,7},{8,9},{9,10},{10,11},{12,13},{... | collective-permute-start | bytes 3145736 | tf_op jit(solution)/shard_map/ppermute | solution.py:129
  29.1 22.8 %collective-permute-start.9 = (f32[4,2,256,128]{3,2,1,0:T(8,128)S(1)}, f32[4,2,256,128]{3,2,1,0:T(8,128)S(1)}, u32[]{:S(2)}, u32[]{:S(2)}) collective-permute-start(f32[4,2,256,128]{3,2,1,0:T(8,128)S(1)} %get-tuple-element.45.refs_8_), channel_id=1, source_target_pairs={{0,4},{4,0},{8,12},{12,8},{1,5},{5,1},{9,13},{13,9},{2,6},{6,2},{1... | collective-permute-start | bytes 3145736 | tf_op jit(solution)/shard_map/ppermute | solution.py:129
  30.3 22.8 %collective-permute-start.11 = (f32[4,2,256,128]{3,2,1,0:T(8,128)S(1)}, f32[4,2,256,128]{3,2,1,0:T(8,128)S(1)}, u32[]{:S(2)}, u32[]{:S(2)}) collective-permute-start(f32[4,2,256,128]{3,2,1,0:T(8,128)S(1)} %get-tuple-element.46.refs_7_), channel_id=1, source_target_pairs={{0,8},{4,12},{8,0},{12,4},{1,9},{5,13},{9,1},{13,5},{2,10},{6,14},... | collective-permute-start | bytes 3145736 | tf_op jit(solution)/shard_map/ppermute | solution.py:129
  33.0 22.3 %collective-permute-start.5 = (f32[4,2,128,256]{3,2,1,0:T(8,128)S(1)}, f32[4,2,128,256]{3,2,1,0:T(8,128)S(1)}, u32[]{:S(2)}, u32[]{:S(2)}) collective-permute-start(f32[4,2,128,256]{3,2,1,0:T(8,128)S(1)} %collective-permute-done.4.refs_2_), channel_id=1, source_target_pairs={{1,0},{2,1},{5,4},{6,5},{9,8},{10,9},{13,12},{14,13},{17,16},{18,1... | collective-permute-start | bytes 3145736 | tf_op jit(solution)/shard_map/ppermute | solution.py:129
  35.2 24.1 %collective-permute-start.1 = (f32[4,2,128,256]{3,2,1,0:T(8,128)S(1)}, f32[4,2,128,256]{3,2,1,0:T(8,128)S(1)}, u32[]{:S(2)}, u32[]{:S(2)}) collective-permute-start(f32[4,2,128,256]{3,2,1,0:T(8,128)S(1)} %collective-permute-done.refs_1_), channel_id=1, source_target_pairs={{1,2},{2,3},{5,6},{6,7},{9,10},{10,11},{13,14},{14,15},{17,18},{18... | collective-permute-start | bytes 3145736 | tf_op jit(solution)/shard_map/ppermute | solution.py:129
  51.9 21.9 %collective-permute-start.13 = (f32[4,2,256,128]{3,2,1,0:T(8,128)S(1)}, f32[4,2,256,128]{3,2,1,0:T(8,128)S(1)}, u32[]{:S(2)}, u32[]{:S(2)}) collective-permute-start(f32[4,2,256,128]{3,2,1,0:T(8,128)S(1)} %collective-permute-done.10.refs_12_), channel_id=1, source_target_pairs={{0,4},{4,0},{8,12},{12,8},{1,5},{5,1},{9,13},{13,9},{2,6},{6,2},{1... | collective-permute-start | bytes 3145736 | tf_op jit(solution)/shard_map/ppermute | solution.py:129
  53.1 21.9 %collective-permute-start.12 = (f32[4,2,256,128]{3,2,1,0:T(8,128)S(1)}, f32[4,2,256,128]{3,2,1,0:T(8,128)S(1)}, u32[]{:S(2)}, u32[]{:S(2)}) collective-permute-start(f32[4,2,256,128]{3,2,1,0:T(8,128)S(1)} %collective-permute-done.8.refs_9_), channel_id=1, source_target_pairs={{0,8},{4,12},{8,0},{12,4},{1,9},{5,13},{9,1},{13,5},{2,10},{6,14},... | collective-permute-start | bytes 3145736 | tf_op jit(solution)/shard_map/ppermute | solution.py:129
  55.4 20.0 %collective-permute-start.6 = (f32[4,2,128,256]{3,2,1,0:T(8,128)S(1)}, f32[4,2,128,256]{3,2,1,0:T(8,128)S(1)}, u32[]{:S(2)}, u32[]{:S(2)}) collective-permute-start(f32[4,2,128,256]{3,2,1,0:T(8,128)S(1)} %collective-permute-done.5.refs_4_), channel_id=1, source_target_pairs={{1,0},{5,4},{9,8},{13,12},{17,16},{21,20},{25,24},{29,28}} | collective-permute-start | bytes 3145736 | tf_op jit(solution)/shard_map/ppermute | solution.py:129
  59.3 22.0 %collective-permute-start.2 = (f32[4,2,128,256]{3,2,1,0:T(8,128)S(1)}, f32[4,2,128,256]{3,2,1,0:T(8,128)S(1)}, u32[]{:S(2)}, u32[]{:S(2)}) collective-permute-start(f32[4,2,128,256]{3,2,1,0:T(8,128)S(1)} %collective-permute-done.1.refs_3_), channel_id=1, source_target_pairs={{2,3},{6,7},{10,11},{14,15},{18,19},{22,23},{26,27},{30,31}} | collective-permute-start | bytes 3145736 | tf_op jit(solution)/shard_map/ppermute | solution.py:129
  73.7 27.9 %collective-permute-start.20 = (f32[4,2,256,128]{3,2,1,0:T(8,128)}, f32[4,2,256,128]{3,2,1,0:T(8,128)S(1)}, u32[]{:S(2)}, u32[]{:S(2)}) collective-permute-start(f32[4,2,256,128]{3,2,1,0:T(8,128)} %get-tuple-element.62.refs_7_), channel_id=1, source_target_pairs={{0,4},{4,0},{8,12},{12,8},{1,5},{5,1},{9,13},{13,9},{2,6},{6,2},{1... | collective-permute-start | bytes 3145736 | tf_op jit(solution)/shard_map/ppermute | solution.py:129
  75.0 26.9 %collective-permute-start.22 = (f32[4,2,256,128]{3,2,1,0:T(8,128)}, f32[4,2,256,128]{3,2,1,0:T(8,128)}, u32[]{:S(2)}, u32[]{:S(2)}) collective-permute-start(f32[4,2,256,128]{3,2,1,0:T(8,128)} %get-tuple-element.61.refs_8_), channel_id=1, source_target_pairs={{0,8},{4,12},{8,0},{12,4},{1,9},{5,13},{9,1},{13,5},{2,10},{6,14},... | collective-permute-start | bytes 3145736 | tf_op jit(solution)/shard_map/ppermute | solution.py:129
  75.4 27.3 %collective-permute-start.7 = (f32[4,2,128,256]{3,2,1,0:T(8,128)}, f32[4,2,128,256]{3,2,1,0:T(8,128)}, u32[]{:S(2)}, u32[]{:S(2)}) collective-permute-start(f32[4,2,128,256]{3,2,1,0:T(8,128)} %get-tuple-element.44.refs_0_), channel_id=1, source_target_pairs={{1,0},{2,1},{3,2},{5,4},{6,5},{7,6},{9,8},{10,9},{11,10},{13,12},{... | collective-permute-start | bytes 3145736 | tf_op jit(solution)/shard_map/ppermute | solution.py:129
  81.3 24.1 %collective-permute-start.3 = (f32[4,2,128,256]{3,2,1,0:T(8,128)}, f32[4,2,128,256]{3,2,1,0:T(8,128)}, u32[]{:S(2)}, u32[]{:S(2)}) collective-permute-start(f32[4,2,128,256]{3,2,1,0:T(8,128)} %get-tuple-element.44.refs_0_), channel_id=1, source_target_pairs={{0,1},{1,2},{2,3},{4,5},{5,6},{6,7},{8,9},{9,10},{10,11},{12,13},{... | collective-permute-start | bytes 3145736 | tf_op jit(solution)/shard_map/ppermute | solution.py:129
  101.7 21.2 %collective-permute-start.21 = (f32[4,2,256,128]{3,2,1,0:T(8,128)}, f32[4,2,256,128]{3,2,1,0:T(8,128)S(1)}, u32[]{:S(2)}, u32[]{:S(2)}) collective-permute-start(f32[4,2,256,128]{3,2,1,0:T(8,128)} %get-tuple-element.61.refs_8_), channel_id=1, source_target_pairs={{0,4},{4,0},{8,12},{12,8},{1,5},{5,1},{9,13},{13,9},{2,6},{6,2},{1... | collective-permute-start | bytes 3145736 | tf_op jit(solution)/shard_map/ppermute | solution.py:129
  102.0 21.2 %collective-permute-start.23 = (f32[4,2,256,128]{3,2,1,0:T(8,128)}, f32[4,2,256,128]{3,2,1,0:T(8,128)S(1)}, u32[]{:S(2)}, u32[]{:S(2)}) collective-permute-start(f32[4,2,256,128]{3,2,1,0:T(8,128)} %get-tuple-element.62.refs_7_), channel_id=1, source_target_pairs={{0,8},{4,12},{8,0},{12,4},{1,9},{5,13},{9,1},{13,5},{2,10},{6,14},... | collective-permute-start | bytes 3145736 | tf_op jit(solution)/shard_map/ppermute | solution.py:129
  102.7 21.5 %collective-permute-start.15 = (f32[4,2,128,256]{3,2,1,0:T(8,128)}, f32[4,2,128,256]{3,2,1,0:T(8,128)S(1)}, u32[]{:S(2)}, u32[]{:S(2)}) collective-permute-start(f32[4,2,128,256]{3,2,1,0:T(8,128)} %collective-permute-done.7.refs_2_), channel_id=1, source_target_pairs={{1,0},{2,1},{5,4},{6,5},{9,8},{10,9},{13,12},{14,13},{17,16},{18,1... | collective-permute-start | bytes 3145736 | tf_op jit(solution)/shard_map/ppermute | solution.py:129
  105.4 22.2 %collective-permute-start.14 = (f32[4,2,128,256]{3,2,1,0:T(8,128)}, f32[4,2,128,256]{3,2,1,0:T(8,128)S(1)}, u32[]{:S(2)}, u32[]{:S(2)}) collective-permute-start(f32[4,2,128,256]{3,2,1,0:T(8,128)} %collective-permute-done.3.refs_1_), channel_id=1, source_target_pairs={{1,2},{2,3},{5,6},{6,7},{9,10},{10,11},{13,14},{14,15},{17,18},{18... | collective-permute-start | bytes 3145736 | tf_op jit(solution)/shard_map/ppermute | solution.py:129
  122.8 10.4 %collective-permute-start.26 = (f32[2,2,256,128]{3,2,1,0:T(8,128)S(1)}, f32[2,2,256,128]{3,2,1,0:T(8,128)S(1)}, u32[]{:S(2)}, u32[]{:S(2)}) collective-permute-start(f32[2,2,256,128]{3,2,1,0:T(8,128)S(1)} %get-tuple-element.65), channel_id=1, source_target_pairs={{0,4},{4,0},{8,12},{12,8},{1,5},{5,1},{9,13},{13,9},{2,6},{6,2},{1... | collective-permute-start | bytes 1572872 | tf_op jit(solution)/shard_map/ppermute | solution.py:129
  123.2 10.4 %collective-permute-start.24 = (f32[2,2,256,128]{3,2,1,0:T(8,128)S(1)}, f32[2,2,256,128]{3,2,1,0:T(8,128)S(1)}, u32[]{:S(2)}, u32[]{:S(2)}) collective-permute-start(f32[2,2,256,128]{3,2,1,0:T(8,128)S(1)} %get-tuple-element.63), channel_id=1, source_target_pairs={{0,8},{4,12},{8,0},{12,4},{1,9},{5,13},{9,1},{13,5},{2,10},{6,14},... | collective-permute-start | bytes 1572872 | tf_op jit(solution)/shard_map/ppermute | solution.py:129
  124.2 10.3 %collective-permute-start.18 = (f32[2,2,128,256]{3,2,1,0:T(8,128)S(1)}, f32[2,2,128,256]{3,2,1,0:T(8,128)S(1)}, u32[]{:S(2)}, u32[]{:S(2)}) collective-permute-start(f32[2,2,128,256]{3,2,1,0:T(8,128)S(1)} %get-tuple-element.57), channel_id=1, source_target_pairs={{1,0},{5,4},{9,8},{13,12},{17,16},{21,20},{25,24},{29,28}} | collective-permute-start | bytes 1572872 | tf_op jit(solution)/shard_map/ppermute | solution.py:129
  127.7 9.0 %collective-permute-start.16 = (f32[2,2,128,256]{3,2,1,0:T(8,128)S(1)}, f32[2,2,128,256]{3,2,1,0:T(8,128)S(1)}, u32[]{:S(2)}, u32[]{:S(2)}) collective-permute-start(f32[2,2,128,256]{3,2,1,0:T(8,128)S(1)} %get-tuple-element.55), channel_id=1, source_target_pairs={{2,3},{6,7},{10,11},{14,15},{18,19},{22,23},{26,27},{30,31}} | collective-permute-start | bytes 1572872 | tf_op jit(solution)/shard_map/ppermute | solution.py:129
  133.3 21.3 %collective-permute-start.27 = (f32[2,2,256,128]{3,2,1,0:T(8,128)S(1)}, f32[2,2,256,128]{3,2,1,0:T(8,128)S(1)}, u32[]{:S(2)}, u32[]{:S(2)}) collective-permute-start(f32[2,2,256,128]{3,2,1,0:T(8,128)S(1)} %get-tuple-element.66), channel_id=1, source_target_pairs={{0,4},{4,0},{8,12},{12,8},{1,5},{5,1},{9,13},{13,9},{2,6},{6,2},{1... | collective-permute-start | bytes 1572872 | tf_op jit(solution)/shard_map/ppermute | solution.py:129
  133.6 21.0 %collective-permute-start.25 = (f32[2,2,256,128]{3,2,1,0:T(8,128)S(1)}, f32[2,2,256,128]{3,2,1,0:T(8,128)S(1)}, u32[]{:S(2)}, u32[]{:S(2)}) collective-permute-start(f32[2,2,256,128]{3,2,1,0:T(8,128)S(1)} %get-tuple-element.64), channel_id=1, source_target_pairs={{0,8},{4,12},{8,0},{12,4},{1,9},{5,13},{9,1},{13,5},{2,10},{6,14},... | collective-permute-start | bytes 1572872 | tf_op jit(solution)/shard_map/ppermute | solution.py:129
  134.5 20.1 %collective-permute-start.19 = (f32[2,2,128,256]{3,2,1,0:T(8,128)S(1)}, f32[2,2,128,256]{3,2,1,0:T(8,128)S(1)}, u32[]{:S(2)}, u32[]{:S(2)}) collective-permute-start(f32[2,2,128,256]{3,2,1,0:T(8,128)S(1)} %get-tuple-element.58), channel_id=1, source_target_pairs={{1,0},{5,4},{9,8},{13,12},{17,16},{21,20},{25,24},{29,28}} | collective-permute-start | bytes 1572872 | tf_op jit(solution)/shard_map/ppermute | solution.py:129
  136.7 17.9 %collective-permute-start.17 = (f32[2,2,128,256]{3,2,1,0:T(8,128)S(1)}, f32[2,2,128,256]{3,2,1,0:T(8,128)S(1)}, u32[]{:S(2)}, u32[]{:S(2)}) collective-permute-start(f32[2,2,128,256]{3,2,1,0:T(8,128)S(1)} %get-tuple-element.56), channel_id=1, source_target_pairs={{2,3},{6,7},{10,11},{14,15},{18,19},{22,23},{26,27},{30,31}} | collective-permute-start | bytes 1572872 | tf_op jit(solution)/shard_map/ppermute | solution.py:129
  169.2 16.0 %collective-permute-start.28 = (f32[512,2048]{1,0:T(8,128)S(1)}, f32[512,2048]{1,0:T(8,128)S(1)}, u32[]{:S(2)}, u32[]{:S(2)}) collective-permute-start(f32[512,2048]{1,0:T(8,128)S(1)} %get-tuple-element.72), channel_id=1, source_target_pairs={{0,16},{16,0},{1,17},{17,1},{2,18},{18,2},{3,19},{19,3},{4,20},{20... | collective-permute-start | bytes 12582920 | tf_op jit(solution)/shard_map/ppermute | solution.py:224
  (30 other events, 646.4 us)

commit v3 on v2

v3 whole, which is shorter than its diff:
```python
import functools

import jax
import jax.numpy as jnp
from jax import lax
from jax.experimental import pallas as pl
from jax.experimental.pallas import tpu as pltpu
from jax.sharding import PartitionSpec as P

W = 256
B = 128
AR = 8
AC = 16
HALF = AR * B // 2
F32 = jnp.float32
BF16 = jnp.bfloat16


def split(x):
    hi = x.astype(BF16)
    return hi, (x - hi.astype(F32)).astype(BF16)


def dot(a, b):
    return jnp.dot(a, b, preferred_element_type=F32)


def slot_rows(l_tgt, l_base, node, b, j):
    base = l_base[b]
    return jnp.where(base >= 0, l_tgt[node, jnp.maximum(base, 0) + j], -1)


def block(tgt):
    return pl.ds(pl.multiple_of(tgt * B, B), B)


def scale(hi, lo, inv):
    return split(dot(hi, inv[0]) + dot(hi, inv[1]) + dot(lo, inv[0]))


def place_l(l_refs, targets, raw_h, raw_l, inv, l_cat):
    raw_h[...] = jnp.zeros_like(raw_h)
    raw_l[...] = jnp.zeros_like(raw_l)
    for b, ref in enumerate(l_refs):
        for j in range(ref.shape[1]):
            tgt = targets(b, j)

            @pl.when(tgt >= 0)
            def _(ref=ref, j=j, tgt=tgt):
                raw_h[block(tgt), :], raw_l[block(tgt), :] = split(ref[0, j])

    for m in range(0, AR * B, 256):
        hi, lo = scale(raw_h[m : m + 256, :], raw_l[m : m + 256, :], inv)
        l_cat[m : m + 256, 0:W] = hi
        l_cat[m : m + 256, W : 2 * W] = lo


def place_u(u_refs, targets, u_cat):
    for b, ref in enumerate(u_refs):
        for j in range(ref.shape[1]):
            tgt = targets(b, j)

            @pl.when(tgt >= 0)
            def _(ref=ref, j=j, tgt=tgt):
                hi, lo = split(ref[0, j])
                u_cat[0:W, block(tgt)] = hi
                u_cat[W : 2 * W, block(tgt)] = lo


def product(l_cat, u_cat, half):
    rows = slice(half * HALF, (half + 1) * HALF)
    lh, ll = l_cat[rows, 0:W], l_cat[rows, W : 2 * W]
    uh, ul = u_cat[0:W, :], u_cat[W : 2 * W, :]
    return dot(lh, uh) + dot(ll, uh) + dot(lh, ul)


def update_kernel(n_l, n_u, start, first, l_tgt, u_tgt, l_base, u_base, *refs):
    l_refs, u_refs, refs = refs[:n_l], refs[n_l : n_l + n_u], refs[n_l + n_u :]
    inv_ref, _, send_in, keep_in, send, keep, token, raw_h, raw_l, l_cat, u_cat = refs
    step = pl.program_id(0)
    node = start + step

    @pl.when(step == 0)
    def _():
        token[...] = jnp.zeros_like(token)
        if first:
            send[...] = jnp.zeros_like(send)
            keep[...] = keep_in[...]

    rows = lambda b, j: slot_rows(l_tgt, l_base, node, b, j)
    place_l(l_refs, rows, raw_h, raw_l, split(inv_ref[0]), l_cat)
    u_cat[...] = jnp.zeros_like(u_cat)
    place_u(u_refs, lambda b, j: u_tgt[node, u_base[b] + j], u_cat)
    send[...] += product(l_cat, u_cat, 0)
    keep[...] -= product(l_cat, u_cat, 1)


def prepare_kernel(n_l, n_u, start, l_tgt, u_tgt, l_base, u_base, *refs):
    l_refs, u_refs, refs = refs[:n_l], refs[n_l : n_l + n_u], refs[n_l + n_u :]
    inv_ref, _, l_cats, u_cats, token, raw_h, raw_l = refs
    step = pl.program_id(0)
    node = start + step
    token[...] = jnp.zeros_like(token)
    rows = lambda b, j: slot_rows(l_tgt, l_base, node, b, j)
    place_l(l_refs, rows, raw_h, raw_l, split(inv_ref[0]), l_cats.at[step])
    u_cats[step] = jnp.zeros(u_cats.shape[1:], BF16)
    place_u(u_refs, lambda b, j: u_tgt[node, u_base[b] + j], u_cats.at[step])


def finish_kernel(n_l, n_u, start, l_tgt, u_tgt, l_base, u_base, *refs):
    l_refs, u_refs, refs = refs[:n_l], refs[n_l : n_l + n_u], refs[n_l + n_u :]
    inv_ref, _, _, _, _, l_cats, u_cats, send, token = refs
    step = pl.program_id(0)
    node = start + step
    token[...] = jnp.zeros_like(token)
    l_cat, u_cat = l_cats.at[step], u_cats.at[step]
    inv = split(inv_ref[0])
    for b, ref in enumerate(l_refs):
        for j in range(ref.shape[1]):
            tgt = slot_rows(l_tgt, l_base, node, b, j)

            @pl.when(tgt >= 0)
            def _(ref=ref, j=j, tgt=tgt):
                hi, lo = scale(*split(ref[0, j]), inv)
                l_cat[block(tgt), 0:W] = hi
                l_cat[block(tgt), W : 2 * W] = lo

    place_u(u_refs, lambda b, j: u_tgt[node, u_base[b] + j], u_cat)
    send[...] += product(l_cat, u_cat, 0)


def keep_kernel(l_cats, u_cats, _, keep_in, keep):
    step = pl.program_id(0)
    keep[...] -= product(l_cats.at[step], u_cats.at[step], 1)


RAW = pltpu.VMEM((AR * B, W), BF16)
L_CAT = (AR * B, 2 * W)
U_CAT = (2 * W, AC * B)
PARAMS = pltpu.CompilerParams(dimension_semantics=("arbitrary",), vmem_limit_bytes=32 << 20)


def call(kernel, nodes, offsets, tables, l_bufs, u_bufs, u11_inv, token, held, out, fixed, scratch):
    start, stop = nodes

    def per_node(buf, offset):
        return pl.BlockSpec((1,) + buf.shape[1:], lambda s, *_: (offset + s, 0, 0, 0))

    vmem, anywhere = pl.BlockSpec(memory_space=pltpu.VMEM), pl.BlockSpec(memory_space=pl.ANY)
    bufs = [pltpu.with_memory_space_constraint(b, pltpu.HBM) for b in (*l_bufs, *u_bufs)]
    n_in = 6 + len(bufs)
    return pl.pallas_call(
        functools.partial(kernel, len(l_bufs), len(u_bufs), start),
        out_shape=(*out, jax.ShapeDtypeStruct((8, 128), F32)),
        grid_spec=pltpu.PrefetchScalarGridSpec(
            num_scalar_prefetch=4,
            grid=(stop - start,),
            in_specs=[per_node(b, o) for b, o in zip(bufs, offsets)]
            + [pl.BlockSpec((1, W, W), lambda s, *_: (start + s, 0, 0)), anywhere]
            + [vmem] * len(held),
            out_specs=(vmem,) * (len(out) + 1),
            scratch_shapes=scratch,
        ),
        input_output_aliases={n_in + i: i for i in range(len(held))} if fixed else {},
        compiler_params=PARAMS,
    )(*tables, *bufs, u11_inv, token, *held)


def apply_update(nodes, offsets, tables, l_bufs, u_bufs, inv, token, accs, first=False):
    kernel = lambda n_l, n_u, start, *refs: update_kernel(n_l, n_u, start, first, *refs)
    out = [pltpu.VMEM((HALF, AC * B), F32)] * 2
    scratch = [RAW, RAW, pltpu.VMEM(L_CAT, BF16), pltpu.VMEM(U_CAT, BF16)]
    *accs, token = call(
        kernel, nodes, offsets, tables, l_bufs, u_bufs, inv, token, accs, out, not first, scratch
    )
    return token, accs


class Box:
    def __init__(self, value):
        self.value = value


def after(x, boxes):
    if not boxes:
        return x
    x, *values = lax.optimization_barrier((x, *[b.value for b in boxes]))
    for box, value in zip(boxes, values):
        box.value = value
    return x


class Link:
    def __init__(self, axis, wait=()):
        self.axis, self.wait = axis, list(wait)

    def send(self, x, pairs):
        out = Box(lax.ppermute(after(x, self.wait), self.axis, pairs))
        self.wait = [out]
        return out


def up(hop):
    return [(z, z + 1) for z in range(hop - 1, 3)]


def down(hop):
    return [(z, z - 1) for z in range(1, 5 - hop)]


def side(mask):
    return [(r, r ^ mask) for r in range(4)]


def hold(links, box):
    for link in links:
        link.wait.append(box)


class Exchange:
    def __init__(self, links, l_chunk, u_h0, u_h1):
        self.links = links
        self.l, self.h = l_chunk, (u_h0, u_h1)

    def first(self):
        lx, ly, lu, ld = self.links
        self.u1, self.d1 = lu.send(self.l, up(1)), ld.send(self.l, down(1))
        self.x0, self.y1 = lx.send(self.h[0], side(1)), ly.send(self.h[1], side(2))

    def second(self):
        lx, ly, lu, ld = self.links
        self.u2, self.d2 = lu.send(self.u1.value, up(2)), ld.send(self.d1.value, down(2))
        self.x1, self.y0 = lx.send(self.h[1], side(1)), ly.send(self.h[0], side(2))

    def third(self, here):
        lx, ly, lu, ld = self.links
        u3, d3 = lu.send(self.u2.value[here], up(3)), ld.send(self.d2.value[here], down(3))
        f1, f0 = lx.send(self.y1.value[here], side(1)), ly.send(self.x0.value[here], side(2))
        return u3, d3, f0, f1

    def buffers(self, third):
        u3, d3, f0, f1 = third
        l_bufs = [self.l] + [b.value for b in (self.u1, self.d1, self.u2, self.d2, u3, d3)]
        u_bufs = [*self.h] + [b.value for b in (self.x0, self.x1, self.y0, self.y1, f0, f1)]
        return l_bufs, u_bufs


def body(rows, cols, l_panel, l_rows, u_panel, u_cols, u11_inv, ancestor):
    gz, row, col = (lax.axis_index(a) for a in ("gz", "row", "col"))
    l_own, u_own, inv = l_panel[0, :, 0], u_panel[0, :, 0], u11_inv[0]
    nodes, l_slots = l_own.shape[:2]
    u_slots = u_own.shape[1]
    l_tgt = l_rows[0, :, 0]
    l_tgt = jnp.where(l_tgt < 0, -1, (l_tgt + (AR // 2) * (1 - gz)) % AR)
    u_tgt = u_cols[0, :, 0]
    keep = ancestor[0]

    if rows == 4 and cols == 4:
        half = u_slots // 2
        sources = jnp.stack([col, col - 1, col + 1, col - 2, col + 2, col - 3, col + 3])
        l_base = jnp.where((sources >= 0) & (sources < cols), sources * l_slots, -1)
        squares = jnp.stack([row, row, row ^ 1, row ^ 1, row ^ 2, row ^ 2, row ^ 3, row ^ 3])
        u_base = squares * u_slots + half * (jnp.arange(8, dtype=jnp.int32) % 2)
        tables = [t.astype(jnp.int32) for t in (l_tgt, u_tgt, l_base, u_base)]
        links = [Link("row"), Link("row"), Link("col"), Link("col")]
        size, part = nodes // 2, nodes // 4
        chunks = []
        for start in (0, size):
            here = slice(start, start + size)
            chunks.append(Exchange(links, l_own[here], u_own[here, :half], u_own[here, half:]))
        one, two = chunks

        one.first()
        one.second()
        third = one.third(slice(0, size))
        two.first()
        zero = jnp.zeros((8, 128), F32)
        token, accs = apply_update(
            (0, part), [0] * 15, tables, *one.buffers(third), inv, zero, (zero, keep), True
        )
        token = Box(token)
        hold(links, token)
        two.second()
        token, accs = apply_update(
            (part, size), [part] * 15, tables, *one.buffers(third), inv, token.value, accs
        )
        token = Box(token)
        hold(links, token)
        third = two.third(slice(0, size))
        l_bufs, u_bufs = two.buffers(third)
        late = (size, nodes), [0] * 15
        cats = [pltpu.VMEM((size,) + shape, BF16) for shape in (L_CAT, U_CAT)]
        l_cats, u_cats, token = call(
            prepare_kernel, *late, tables, l_bufs[:5], u_bufs[:6], inv, token.value, (), cats, True, [RAW, RAW]
        )
        send, keep = accs
        tables = [l_tgt, u_tgt, l_base[5:], u_base[6:]]
        tables = [t.astype(jnp.int32) for t in tables]
        l_cats, u_cats, send, token = call(
            finish_kernel,
            *late,
            tables,
            l_bufs[5:],
            u_bufs[6:],
            inv,
            token,
            (l_cats, u_cats, send),
            (*cats, pltpu.VMEM((HALF, AC * B), F32)),
            True,
            [],
        )
        vmem = pl.BlockSpec(memory_space=pltpu.VMEM)
        keep = pl.pallas_call(
            keep_kernel,
            grid=(size,),
            out_shape=pltpu.VMEM((HALF, AC * B), F32),
            in_specs=[vmem, vmem, pl.BlockSpec(memory_space=pl.ANY), vmem],
            out_specs=vmem,
            input_output_aliases={3: 0},
            compiler_params=PARAMS,
        )(l_cats, u_cats, token, keep)
    else:
        l_all = lax.all_gather(l_own, "col", axis=1, tiled=True)
        u_all = lax.all_gather(u_own, "row", axis=1, tiled=True)
        base, zero = jnp.zeros((1,), jnp.int32), jnp.zeros((8, 128), F32)
        tables = [t.astype(jnp.int32) for t in (l_tgt, u_tgt, base, base)]
        _, (send, keep) = apply_update(
            (0, nodes), [0, 0], tables, [l_all], [u_all], inv, zero, (zero, keep), True
        )

    other = lax.ppermute(send, "gz", [(0, 1), (1, 0)])
    return (keep - other)[None]


def solution(mesh):
    in_specs = (
        P("gz", None, "row", "col", None, None),
        P("gz", None, "row", None),
        P("gz", None, "col", "row", None, None),
        P("gz", None, "col", None),
        P("gz", None, None, None),
        P("row", "gz", "col"),
    )
    return jax.shard_map(
        functools.partial(body, mesh.shape["row"], mesh.shape["col"]),
        mesh=mesh,
        in_specs=in_specs,
        out_specs=P("row", "gz", "col"),
        check_vma=False,
    )
```

time: 188 us -> 186 us (0.989)
  starting transfers between devices: 56.4 us -> 50.2 us
    ppermute x28 -> x24, waiting for transfers between devices: 57.3 us -> 64.3 us  [send(): out = Box(lax.ppermute(after(x, self.wait), self.axis, pairs))]
    ppermute x1, waiting for transfers between devices: 6.79 us -> 0.01 us  [body(): other = lax.ppermute(send, 'gz', [(0, 1), (1, 0)])]
    ppermute x28 -> x24, starting transfers between devices: 47.2 us -> 42.7 us  [send(): out = Box(lax.ppermute(after(x, self.wait), self.axis, pairs))]
    slice x5 -> x3, local copies, waits for them, and re-layouts: 5.51 us -> 1.81 us  [the longest x1 1.67 us: body(): u_own[here, :half]]
    unnamed x66 -> x62, local copies, waits for them, and re-layouts: 3.53 us -> 6.25 us
    pallas_call x4 -> x5, Pallas kernels: 53.8 us -> 55.4 us  [the longest x4 47.3 us: call(): pl.pallas_call(functools.partial(kernel, len(l_bufs), len(u_bufs), start)...]
  transfers between devices with their start and end apart: 29 -> 25, of which waited for: 11 -> 7; matrix products, arithmetic and copies ran while one was open for 2% -> 1% of each run, Pallas kernels for 22% -> 24%
where the time goes in v3:
time: 186 us; the launch traced here: 184 us
  waiting for transfers between devices  64.3 us (35%)
  Pallas kernels  55.4 us (30%)
  starting transfers between devices  50.2 us (27%)
  local copies, waits for them, and re-layouts  11.1 us (6%)
  other arithmetic  2.8 us (2%)
    ppermute x24, waiting for transfers between devices, send(): out = Box(lax.ppermute(after(x, self.wait), self.axis, pairs))  64.3 us
    pallas_call x4, Pallas kernels, call(): pl.pallas_call(functools.partial(kernel, len(l_bufs), len(u_bufs), start)...  47.3 us
    ppermute x24, starting transfers between devices, send(): out = Box(lax.ppermute(after(x, self.wait), self.axis, pairs))  42.7 us
    pallas_call x1, Pallas kernels, body(): pl.pallas_call(keep_kernel, grid=(size,), out_shape=pltpu.VMEM((HALF, AC...  8.11 us
    ppermute x1, starting transfers between devices, body(): other = lax.ppermute(send, 'gz', [(0, 1), (1, 0)])  7.51 us
    unnamed x62, local copies, waits for them, and re-layouts  6.25 us
  transfers between devices with their start and end apart: 25, of which 7 were waited for; matrix products, arithmetic and copies ran while one was open for 1% of the time, Pallas kernels for 24%

profile of v3, /device:TPU:17, one launch (start us, length us, event | category | flops | bytes accessed | tf_op | source)
XLA Modules:
  0.0 184.2 jit_solution(9431197183412448569)
XLA Ops:
  0.0 2.9 %slice_bitcast_fusion = (f32[4,2,128,256]{3,2,1,0:T(8,128)S(1)}, f32[4,2,128,256]{3,2,1,0:T(8,128)}) fusion(f32[1,8,1,2,128,256]{5,4,3,1,2,0:T(8,128)} %bitcast.39), kind=kLoop, calls=%fused_computation.1 | loop fusion | bytes 4194304 | tf_op jit(solution)/shard_map/slice | solution.py:270
  2.9 2.1 %collective-permute-start.4 = (f32[4,2,128,256]{3,2,1,0:T(8,128)S(1)}, f32[4,2,128,256]{3,2,1,0:T(8,128)S(1)}, u32[]{:S(2)}, u32[]{:S(2)}) collective-permute-start(f32[4,2,128,256]{3,2,1,0:T(8,128)S(1)} %get-tuple-element.131.refs_4_), channel_id=1, source_target_pairs={{1,0},{2,1},{3,2},{5,4},{6,5},{7,6},{9,8},{10,9},{11,10},{13,12},{... | collective-permute-start | bytes 3145736 | tf_op jit(solution)/shard_map/ppermute | solution.py:198
  4.9 3.3 %collective-permute-start = (f32[4,2,128,256]{3,2,1,0:T(8,128)S(1)}, f32[4,2,128,256]{3,2,1,0:T(8,128)S(1)}, u32[]{:S(2)}, u32[]{:S(2)}) collective-permute-start(f32[4,2,128,256]{3,2,1,0:T(8,128)S(1)} %get-tuple-element.131.refs_4_), channel_id=1, source_target_pairs={{0,1},{1,2},{2,3},{4,5},{5,6},{6,7},{8,9},{9,10},{10,11},{12,13},{... | collective-permute-start | bytes 3145736 | tf_op jit(solution)/shard_map/ppermute | solution.py:198
  8.3 1.7 fusion.4
  12.4 18.2 %collective-permute-done.refs_5_ = f32[4,2,128,256]{3,2,1,0:T(8,128)S(1)} collective-permute-done((f32[4,2,128,256]{3,2,1,0:T(8,128)S(1)}, f32[4,2,128,256]{3,2,1,0:T(8,128)S(1)}, u32[]{:S(2)}, u32[]{:S(2)}) %collective-permute-start) | collective-permute-done | bytes 1048608 | tf_op jit(solution)/shard_map/ppermute | solution.py:198
  30.5 3.3 %collective-permute-start.1 = (f32[4,2,128,256]{3,2,1,0:T(8,128)S(1)}, f32[4,2,128,256]{3,2,1,0:T(8,128)S(1)}, u32[]{:S(2)}, u32[]{:S(2)}) collective-permute-start(f32[4,2,128,256]{3,2,1,0:T(8,128)S(1)} %collective-permute-done.refs_5_), channel_id=1, source_target_pairs={{1,2},{2,3},{5,6},{6,7},{9,10},{10,11},{13,14},{14,15},{17,18},{18... | collective-permute-start | bytes 3145736 | tf_op jit(solution)/shard_map/ppermute | solution.py:198
  33.8 2.1 %collective-permute-start.5 = (f32[4,2,128,256]{3,2,1,0:T(8,128)S(1)}, f32[4,2,128,256]{3,2,1,0:T(8,128)S(1)}, u32[]{:S(2)}, u32[]{:S(2)}) collective-permute-start(f32[4,2,128,256]{3,2,1,0:T(8,128)S(1)} %collective-permute-done.4.refs_6_), channel_id=1, source_target_pairs={{1,0},{2,1},{5,4},{6,5},{9,8},{10,9},{13,12},{14,13},{17,16},{18,1... | collective-permute-start | bytes 3145736 | tf_op jit(solution)/shard_map/ppermute | solution.py:198
  36.0 1.3 collective-permute-start.9
  38.5 16.7 %collective-permute-done.1.refs_7_ = f32[4,2,128,256]{3,2,1,0:T(8,128)S(1)} collective-permute-done((f32[4,2,128,256]{3,2,1,0:T(8,128)S(1)}, f32[4,2,128,256]{3,2,1,0:T(8,128)S(1)}, u32[]{:S(2)}, u32[]{:S(2)}) %collective-permute-start.1) | collective-permute-done | bytes 1048608 | tf_op jit(solution)/shard_map/ppermute | solution.py:198
  55.2 3.3 %collective-permute-start.2 = (f32[4,2,128,256]{3,2,1,0:T(8,128)S(1)}, f32[4,2,128,256]{3,2,1,0:T(8,128)S(1)}, u32[]{:S(2)}, u32[]{:S(2)}) collective-permute-start(f32[4,2,128,256]{3,2,1,0:T(8,128)S(1)} %collective-permute-done.1.refs_7_), channel_id=1, source_target_pairs={{2,3},{6,7},{10,11},{14,15},{18,19},{22,23},{26,27},{30,31}} | collective-permute-start | bytes 3145736 | tf_op jit(solution)/shard_map/ppermute | solution.py:198
  59.3 1.3 collective-permute-start.12
  60.6 1.3 collective-permute-start.11
  61.9 16.2 %collective-permute-done.2.refs_9_ = f32[4,2,128,256]{3,2,1,0:T(8,128)S(1)} collective-permute-done((f32[4,2,128,256]{3,2,1,0:T(8,128)S(1)}, f32[4,2,128,256]{3,2,1,0:T(8,128)S(1)}, u32[]{:S(2)}, u32[]{:S(2)}) %collective-permute-start.2) | collective-permute-done | bytes 1048608 | tf_op jit(solution)/shard_map/ppermute | solution.py:198
  78.1 4.1 %collective-permute-start.3 = (f32[4,2,128,256]{3,2,1,0:T(8,128)}, f32[4,2,128,256]{3,2,1,0:T(8,128)}, u32[]{:S(2)}, u32[]{:S(2)}) collective-permute-start(f32[4,2,128,256]{3,2,1,0:T(8,128)} %get-tuple-element.91.refs_0_), channel_id=1, source_target_pairs={{0,1},{1,2},{2,3},{4,5},{5,6},{6,7},{8,9},{9,10},{10,11},{12,13},{... | collective-permute-start | bytes 3145736 | tf_op jit(solution)/shard_map/ppermute | solution.py:198
  82.3 1.9 %collective-permute-start.16 = (f32[4,2,128,256]{3,2,1,0:T(8,128)}, f32[4,2,128,256]{3,2,1,0:T(8,128)}, u32[]{:S(2)}, u32[]{:S(2)}) collective-permute-start(f32[4,2,128,256]{3,2,1,0:T(8,128)} %get-tuple-element.91.refs_0_), channel_id=1, source_target_pairs={{1,0},{2,1},{3,2},{5,4},{6,5},{7,6},{9,8},{10,9},{11,10},{13,12},{... | collective-permute-start | bytes 3145736 | tf_op jit(solution)/shard_map/ppermute | solution.py:198
  85.5 1.3 collective-permute-start.14
  87.1 2.2 %copy-done.4 = f32[1,512,2048]{2,1,0:T(8,128)S(1)} copy-done((f32[1,512,2048]{2,1,0:T(8,128)S(1)}, f32[1,512,2048]{2,1,0:T(8,128)}, u32[]{:S(2)}) %copy-start.4) | copy-done | bytes 4194328
  89.3 14.0 %shard_map.64 = (f32[512,2048]{1,0:T(8,128)S(1)}, f32[512,2048]{1,0:T(8,128)S(1)}, f32[8,128]{1,0:T(8,128)S(1)}) custom-call(s32[8,8]{1,0:T(8,128)S(1)} %fusion.1.refs_0_.l_tgt, s32[8,16]{1,0:T(8,128)S(1)} %bitcast.34, s32[7]{0:T(128)S(1)} %and_select_fusion.1.refs_2_.l_base, s32[8]{0:T(128)S(1)} %fusion.3.refs_3_.u_base, f32[4,2,128,256]{3,2,1,0:T(8,128)} %copy-done.6, ...), custom_call_target="tpu_custom_call" | custom-call | tf_op jit(solution)/shard_map/pallas_call | solution.py:152
  103.3 1.8 collective-permute-done.16.refs_2_
  105.1 2.3 %collective-permute-start.13 = (f32[4,2,128,256]{3,2,1,0:T(8,128)}, f32[4,2,128,256]{3,2,1,0:T(8,128)S(1)}, u32[]{:S(2)}, u32[]{:S(2)}) collective-permute-start(f32[4,2,128,256]{3,2,1,0:T(8,128)} %collective-permute-done.3.refs_1_), channel_id=1, source_target_pairs={{1,2},{2,3},{5,6},{6,7},{9,10},{10,11},{13,14},{14,15},{17,18},{18... | collective-permute-start | bytes 3145736 | tf_op jit(solution)/shard_map/ppermute | solution.py:198
  107.4 3.3 %collective-permute-start.18 = (f32[4,2,128,256]{3,2,1,0:T(8,128)}, f32[4,2,128,256]{3,2,1,0:T(8,128)S(1)}, u32[]{:S(2)}, u32[]{:S(2)}) collective-permute-start(f32[4,2,128,256]{3,2,1,0:T(8,128)} %collective-permute-done.16.refs_2_), channel_id=1, source_target_pairs={{1,0},{2,1},{5,4},{6,5},{9,8},{10,9},{13,12},{14,13},{17,16},{18,1... | collective-permute-start | bytes 3145736 | tf_op jit(solution)/shard_map/ppermute | solution.py:198
  110.7 1.3 collective-permute-start.21
  113.3 13.5 %shard_map.65 = (f32[512,2048]{1,0:T(8,128)S(1)}, f32[512,2048]{1,0:T(8,128)S(1)}, f32[8,128]{1,0:T(8,128)S(1)}) custom-call(s32[8,8]{1,0:T(8,128)S(1)} %fusion.1.refs_0_.l_tgt, s32[8,16]{1,0:T(8,128)S(1)} %bitcast.35, s32[7]{0:T(128)S(1)} %and_select_fusion.1.refs_2_.l_base, ...), custom_call_target="tpu_custom_call", output_to_operand_aliasing={{0}: (21, {}), {1}: (22, {})} | custom-call | tf_op jit(solution)/shard_map/pallas_call | solution.py:152
  126.7 2.0 %copy-done.2 = f32[512,2048]{1,0:T(8,128)} copy-done((f32[512,2048]{1,0:T(8,128)}, f32[512,2048]{1,0:T(8,128)S(1)}, u32[]{:S(2)}) %copy-start.2) | copy-done | bytes 4194328
  128.8 1.4 collective-permute-done.21.refs_8_
  133.4 1.4 collective-permute-start.17
  135.0 8.7 %shard_map.66 = (bf16[4,1024,512]{2,1,0:T(8,128)(2,1)S(1)}, bf16[4,512,2048]{2,1,0:T(8,128)(2,1)S(1)}, f32[8,128]{1,0:T(8,128)S(1)}) custom-call(s32[8,8]{1,0:T(8,128)S(1)} %fusion.1.refs_0_.l_tgt, s32[8,16]{1,0:T(8,128)S(1)} %bitcast.36, s32[7]{0:T(128)S(1)} %and_select_fusion.1.refs_2_.l_base, s32[8]{0:T(128)S(1)} %fusion.3.refs_3_.u_base, ...), custom_call_target="tpu_custom_call" | custom-call | tf_op jit(solution)/shard_map/pallas_call | solution.py:152
  143.7 9.0 %collective-permute-done.22.refs_2_ = f32[4,2,256,128]{3,2,1,0:T(8,128)S(1)} collective-permute-done((f32[4,2,256,128]{3,2,1,0:T(8,128)}, f32[4,2,256,128]{3,2,1,0:T(8,128)S(1)}, u32[]{:S(2)}, u32[]{:S(2)}) %collective-permute-start.22) | collective-permute-done | bytes 1048608 | tf_op jit(solution)/shard_map/ppermute | solution.py:198
  154.7 11.0 %shard_map.67 = (bf16[4,1024,512]{2,1,0:T(8,128)(2,1)S(1)}, bf16[4,512,2048]{2,1,0:T(8,128)(2,1)S(1)}, f32[512,2048]{1,0:T(8,128)S(1)}, f32[8,128]{1,0:T(8,128)S(1)}) custom-call(s32[8,8]{1,0:T(8,128)S(1)} %fusion.1.refs_0_.l_tgt, s32[8,16]{1,0:T(8,128)S(1)} %bitcast.37, ...), custom_call_target="tpu_custom_call", output_to_operand_aliasing={{0}: (10, {}), {1}: (11, {}), {2}: (12, {})} | custom-call | tf_op jit(solution)/shard_map/pallas_call | solution.py:152
  165.8 7.5 %collective-permute-start.24 = (f32[512,2048]{1,0:T(8,128)S(1)}, f32[512,2048]{1,0:T(8,128)S(1)}, u32[]{:S(2)}, u32[]{:S(2)}) collective-permute-start(f32[512,2048]{1,0:T(8,128)S(1)} %get-tuple-element.126), channel_id=1, source_target_pairs={{0,16},{16,0},{1,17},{17,1},{2,18},{18,2},{3,19},{19,3},{4,20},{20... | collective-permute-start | bytes 12582920 | tf_op jit(solution)/shard_map/ppermute | solution.py:331
  173.3 8.1 %shard_map.68 = f32[512,2048]{1,0:T(8,128)S(1)} custom-call(bf16[4,1024,512]{2,1,0:T(8,128)(2,1)S(1)} %get-tuple-element.122.l_cats, bf16[4,512,2048]{2,1,0:T(8,128)(2,1)S(1)} %get-tuple-element.123.u_cats, f32[8,128]{1,0:T(8,128)S(1)} %get-tuple-element.124._, f32[512,2048]{1,0:T(8,128)S(1)} %get-tuple-element.125.keep_in), custom_call_target="tpu_custom_call", output_to_operand_aliasing={{}: (3, {})} | custom-call | tf_op jit(solution)/shard_map/pallas_call | solution.py:313
  181.4 2.8 %subtract_bitcast_fusion = f32[1,512,2048]{2,1,0:T(8,128)} fusion(f32[512,2048]{1,0:T(8,128)S(1)} %shard_map.68, f32[512,2048]{1,0:T(8,128)S(1)} %collective-permute-done.24), kind=kLoop, calls=%fused_computation | loop fusion | flops 1048576 | bytes 12582912 | tf_op jit(solution)/shard_map/broadcast_in_dim | solution.py:332
  (96 shorter events, 12.6 us)
Async XLA Ops:
  2.9 30.9 %collective-permute-start.4 = (f32[4,2,128,256]{3,2,1,0:T(8,128)S(1)}, f32[4,2,128,256]{3,2,1,0:T(8,128)S(1)}, u32[]{:S(2)}, u32[]{:S(2)}) collective-permute-start(f32[4,2,128,256]{3,2,1,0:T(8,128)S(1)} %get-tuple-element.131.refs_4_), channel_id=1, source_target_pairs={{1,0},{2,1},{3,2},{5,4},{6,5},{7,6},{9,8},{10,9},{11,10},{13,12},{... | collective-permute-start | bytes 3145736 | tf_op jit(solution)/shard_map/ppermute | solution.py:198
  4.9 25.6 %collective-permute-start = (f32[4,2,128,256]{3,2,1,0:T(8,128)S(1)}, f32[4,2,128,256]{3,2,1,0:T(8,128)S(1)}, u32[]{:S(2)}, u32[]{:S(2)}) collective-permute-start(f32[4,2,128,256]{3,2,1,0:T(8,128)S(1)} %get-tuple-element.131.refs_4_), channel_id=1, source_target_pairs={{0,1},{1,2},{2,3},{4,5},{5,6},{6,7},{8,9},{9,10},{10,11},{12,13},{... | collective-permute-start | bytes 3145736 | tf_op jit(solution)/shard_map/ppermute | solution.py:198
  8.2 78.8 %copy-start.30 = (s32[1,8,1,8]{3,2,1,0:T(1,128)S(1)}, s32[1,8,1,8]{3,2,1,0:T(1,128)}, u32[]{:S(2)}) copy-start(s32[1,8,1,8]{3,2,1,0:T(1,128)} %param.7) | copy-start | bytes 772
  8.2 78.8 %copy-start = (f32[1,8,256,256]{3,2,1,0:T(8,128)S(1)}, f32[1,8,256,256]{3,2,1,0:T(8,128)}, u32[]{:S(2)}) copy-start(f32[1,8,256,256]{3,2,1,0:T(8,128)} %param.10) | copy-start | bytes 6291460
  8.2 78.8 %copy-start.5 = (s32[1,8,1,16]{3,2,1,0:T(1,128)S(1)}, s32[1,8,1,16]{3,2,1,0:T(1,128)}, u32[]{:S(2)}) copy-start(s32[1,8,1,16]{3,2,1,0:T(1,128)} %param.9) | copy-start | bytes 1540
  9.9 49.4 %copy-start.8 = (f32[4,2,256,128]{3,2,1,0:T(8,128)}, f32[4,2,256,128]{3,2,1,0:T(8,128)S(1)}, u32[]{:S(2)}) copy-start(f32[4,2,256,128]{3,2,1,0:T(8,128)S(1)} %get-tuple-element.81.refs_11_) | copy-start | bytes 3145732
  9.9 26.0 %collective-permute-start.7 = (f32[4,2,256,128]{3,2,1,0:T(8,128)S(1)}, f32[4,2,256,128]{3,2,1,0:T(8,128)S(1)}, u32[]{:S(2)}, u32[]{:S(2)}) collective-permute-start(f32[4,2,256,128]{3,2,1,0:T(8,128)S(1)} %get-tuple-element.81.refs_11_), channel_id=1, source_target_pairs={{0,4},{4,0},{8,12},{12,8},{1,5},{5,1},{9,13},{13,9},{2,6},{6,2},{1... | collective-permute-start | bytes 3145736 | tf_op jit(solution)/shard_map/ppermute | solution.py:198
  11.1 26.1 %collective-permute-start.8 = (f32[4,2,256,128]{3,2,1,0:T(8,128)S(1)}, f32[4,2,256,128]{3,2,1,0:T(8,128)S(1)}, u32[]{:S(2)}, u32[]{:S(2)}) collective-permute-start(f32[4,2,256,128]{3,2,1,0:T(8,128)S(1)} %get-tuple-element.79.refs_12_), channel_id=1, source_target_pairs={{0,8},{4,12},{8,0},{12,4},{1,9},{5,13},{9,1},{13,5},{2,10},{6,14},... | collective-permute-start | bytes 3145736 | tf_op jit(solution)/shard_map/ppermute | solution.py:198
  30.5 31.4 %copy-start.11 = (f32[4,2,128,256]{3,2,1,0:T(8,128)}, f32[4,2,128,256]{3,2,1,0:T(8,128)S(1)}, u32[]{:S(2)}) copy-start(f32[4,2,128,256]{3,2,1,0:T(8,128)S(1)} %collective-permute-done.refs_5_) | copy-start | bytes 3145732
  30.5 24.7 %collective-permute-start.1 = (f32[4,2,128,256]{3,2,1,0:T(8,128)S(1)}, f32[4,2,128,256]{3,2,1,0:T(8,128)S(1)}, u32[]{:S(2)}, u32[]{:S(2)}) collective-permute-start(f32[4,2,128,256]{3,2,1,0:T(8,128)S(1)} %collective-permute-done.refs_5_), channel_id=1, source_target_pairs={{1,2},{2,3},{5,6},{6,7},{9,10},{10,11},{13,14},{14,15},{17,18},{18... | collective-permute-start | bytes 3145736 | tf_op jit(solution)/shard_map/ppermute | solution.py:198
  33.8 24.7 %collective-permute-start.5 = (f32[4,2,128,256]{3,2,1,0:T(8,128)S(1)}, f32[4,2,128,256]{3,2,1,0:T(8,128)S(1)}, u32[]{:S(2)}, u32[]{:S(2)}) collective-permute-start(f32[4,2,128,256]{3,2,1,0:T(8,128)S(1)} %collective-permute-done.4.refs_6_), channel_id=1, source_target_pairs={{1,0},{2,1},{5,4},{6,5},{9,8},{10,9},{13,12},{14,13},{17,16},{18,1... | collective-permute-start | bytes 3145736 | tf_op jit(solution)/shard_map/ppermute | solution.py:198
  36.0 42.1 %copy-start.12 = (f32[4,2,256,128]{3,2,1,0:T(8,128)}, f32[4,2,256,128]{3,2,1,0:T(8,128)S(1)}, u32[]{:S(2)}) copy-start(f32[4,2,256,128]{3,2,1,0:T(8,128)S(1)} %collective-permute-done.7.refs_13_) | copy-start | bytes 3145732
  36.0 23.3 %collective-permute-start.9 = (f32[4,2,256,128]{3,2,1,0:T(8,128)S(1)}, f32[4,2,256,128]{3,2,1,0:T(8,128)S(1)}, u32[]{:S(2)}, u32[]{:S(2)}) collective-permute-start(f32[4,2,256,128]{3,2,1,0:T(8,128)S(1)} %get-tuple-element.79.refs_12_), channel_id=1, source_target_pairs={{0,4},{4,0},{8,12},{12,8},{1,5},{5,1},{9,13},{13,9},{2,6},{6,2},{1... | collective-permute-start | bytes 3145736 | tf_op jit(solution)/shard_map/ppermute | solution.py:198
  37.3 48.2 %copy-start.13 = (f32[4,2,256,128]{3,2,1,0:T(8,128)}, f32[4,2,256,128]{3,2,1,0:T(8,128)S(1)}, u32[]{:S(2)}) copy-start(f32[4,2,256,128]{3,2,1,0:T(8,128)S(1)} %collective-permute-done.8.refs_16_) | copy-start | bytes 3145732
  37.3 23.3 %collective-permute-start.10 = (f32[4,2,256,128]{3,2,1,0:T(8,128)S(1)}, f32[4,2,256,128]{3,2,1,0:T(8,128)S(1)}, u32[]{:S(2)}, u32[]{:S(2)}) collective-permute-start(f32[4,2,256,128]{3,2,1,0:T(8,128)S(1)} %get-tuple-element.81.refs_11_), channel_id=1, source_target_pairs={{0,8},{4,12},{8,0},{12,4},{1,9},{5,13},{9,1},{13,5},{2,10},{6,14},... | collective-permute-start | bytes 3145736 | tf_op jit(solution)/shard_map/ppermute | solution.py:198
  55.2 22.9 %collective-permute-start.2 = (f32[4,2,128,256]{3,2,1,0:T(8,128)S(1)}, f32[4,2,128,256]{3,2,1,0:T(8,128)S(1)}, u32[]{:S(2)}, u32[]{:S(2)}) collective-permute-start(f32[4,2,128,256]{3,2,1,0:T(8,128)S(1)} %collective-permute-done.1.refs_7_), channel_id=1, source_target_pairs={{2,3},{6,7},{10,11},{14,15},{18,19},{22,23},{26,27},{30,31}} | collective-permute-start | bytes 3145736 | tf_op jit(solution)/shard_map/ppermute | solution.py:198
  58.6 23.7 %collective-permute-start.6 = (f32[4,2,128,256]{3,2,1,0:T(8,128)S(1)}, f32[4,2,128,256]{3,2,1,0:T(8,128)S(1)}, u32[]{:S(2)}, u32[]{:S(2)}) collective-permute-start(f32[4,2,128,256]{3,2,1,0:T(8,128)S(1)} %collective-permute-done.5.refs_8_), channel_id=1, source_target_pairs={{1,0},{5,4},{9,8},{13,12},{17,16},{21,20},{25,24},{29,28}} | collective-permute-start | bytes 3145736 | tf_op jit(solution)/shard_map/ppermute | solution.py:198
  59.3 24.9 %collective-permute-start.12 = (f32[4,2,256,128]{3,2,1,0:T(8,128)S(1)}, f32[4,2,256,128]{3,2,1,0:T(8,128)S(1)}, u32[]{:S(2)}, u32[]{:S(2)}) collective-permute-start(f32[4,2,256,128]{3,2,1,0:T(8,128)S(1)} %collective-permute-done.8.refs_16_), channel_id=1, source_target_pairs={{0,4},{4,0},{8,12},{12,8},{1,5},{5,1},{9,13},{13,9},{2,6},{6,2},{1... | collective-permute-start | bytes 3145736 | tf_op jit(solution)/shard_map/ppermute | solution.py:198
  60.6 24.9 %collective-permute-start.11 = (f32[4,2,256,128]{3,2,1,0:T(8,128)S(1)}, f32[4,2,256,128]{3,2,1,0:T(8,128)S(1)}, u32[]{:S(2)}, u32[]{:S(2)}) collective-permute-start(f32[4,2,256,128]{3,2,1,0:T(8,128)S(1)} %collective-permute-done.7.refs_13_), channel_id=1, source_target_pairs={{0,8},{4,12},{8,0},{12,4},{1,9},{5,13},{9,1},{13,5},{2,10},{6,14},... | collective-permute-start | bytes 3145736 | tf_op jit(solution)/shard_map/ppermute | solution.py:198
  78.1 25.2 %collective-permute-start.3 = (f32[4,2,128,256]{3,2,1,0:T(8,128)}, f32[4,2,128,256]{3,2,1,0:T(8,128)}, u32[]{:S(2)}, u32[]{:S(2)}) collective-permute-start(f32[4,2,128,256]{3,2,1,0:T(8,128)} %get-tuple-element.91.refs_0_), channel_id=1, source_target_pairs={{0,1},{1,2},{2,3},{4,5},{5,6},{6,7},{8,9},{9,10},{10,11},{12,13},{... | collective-permute-start | bytes 3145736 | tf_op jit(solution)/shard_map/ppermute | solution.py:198
  82.3 22.9 %collective-permute-start.16 = (f32[4,2,128,256]{3,2,1,0:T(8,128)}, f32[4,2,128,256]{3,2,1,0:T(8,128)}, u32[]{:S(2)}, u32[]{:S(2)}) collective-permute-start(f32[4,2,128,256]{3,2,1,0:T(8,128)} %get-tuple-element.91.refs_0_), channel_id=1, source_target_pairs={{1,0},{2,1},{3,2},{5,4},{6,5},{7,6},{9,8},{10,9},{11,10},{13,12},{... | collective-permute-start | bytes 3145736 | tf_op jit(solution)/shard_map/ppermute | solution.py:198
  84.2 26.5 %collective-permute-start.15 = (f32[4,2,256,128]{3,2,1,0:T(8,128)}, f32[4,2,256,128]{3,2,1,0:T(8,128)}, u32[]{:S(2)}, u32[]{:S(2)}) collective-permute-start(f32[4,2,256,128]{3,2,1,0:T(8,128)} %get-tuple-element.104.refs_5_), channel_id=1, source_target_pairs={{0,4},{4,0},{8,12},{12,8},{1,5},{5,1},{9,13},{13,9},{2,6},{6,2},{1... | collective-permute-start | bytes 3145736 | tf_op jit(solution)/shard_map/ppermute | solution.py:198
  85.5 26.5 %collective-permute-start.14 = (f32[4,2,256,128]{3,2,1,0:T(8,128)}, f32[4,2,256,128]{3,2,1,0:T(8,128)}, u32[]{:S(2)}, u32[]{:S(2)}) collective-permute-start(f32[4,2,256,128]{3,2,1,0:T(8,128)} %get-tuple-element.106.refs_6_), channel_id=1, source_target_pairs={{0,8},{4,12},{8,0},{12,4},{1,9},{5,13},{9,1},{13,5},{2,10},{6,14},... | collective-permute-start | bytes 3145736 | tf_op jit(solution)/shard_map/ppermute | solution.py:198
  105.1 23.6 %collective-permute-start.13 = (f32[4,2,128,256]{3,2,1,0:T(8,128)}, f32[4,2,128,256]{3,2,1,0:T(8,128)S(1)}, u32[]{:S(2)}, u32[]{:S(2)}) collective-permute-start(f32[4,2,128,256]{3,2,1,0:T(8,128)} %collective-permute-done.3.refs_1_), channel_id=1, source_target_pairs={{1,2},{2,3},{5,6},{6,7},{9,10},{10,11},{13,14},{14,15},{17,18},{18... | collective-permute-start | bytes 3145736 | tf_op jit(solution)/shard_map/ppermute | solution.py:198
  107.4 21.4 %collective-permute-start.18 = (f32[4,2,128,256]{3,2,1,0:T(8,128)}, f32[4,2,128,256]{3,2,1,0:T(8,128)S(1)}, u32[]{:S(2)}, u32[]{:S(2)}) collective-permute-start(f32[4,2,128,256]{3,2,1,0:T(8,128)} %collective-permute-done.16.refs_2_), channel_id=1, source_target_pairs={{1,0},{2,1},{5,4},{6,5},{9,8},{10,9},{13,12},{14,13},{17,16},{18,1... | collective-permute-start | bytes 3145736 | tf_op jit(solution)/shard_map/ppermute | solution.py:198
  110.7 19.5 %collective-permute-start.21 = (f32[4,2,256,128]{3,2,1,0:T(8,128)}, f32[4,2,256,128]{3,2,1,0:T(8,128)S(1)}, u32[]{:S(2)}, u32[]{:S(2)}) collective-permute-start(f32[4,2,256,128]{3,2,1,0:T(8,128)} %get-tuple-element.106.refs_6_), channel_id=1, source_target_pairs={{0,4},{4,0},{8,12},{12,8},{1,5},{5,1},{9,13},{13,9},{2,6},{6,2},{1... | collective-permute-start | bytes 3145736 | tf_op jit(solution)/shard_map/ppermute | solution.py:198
  112.0 19.1 %collective-permute-start.20 = (f32[4,2,256,128]{3,2,1,0:T(8,128)}, f32[4,2,256,128]{3,2,1,0:T(8,128)S(1)}, u32[]{:S(2)}, u32[]{:S(2)}) collective-permute-start(f32[4,2,256,128]{3,2,1,0:T(8,128)} %get-tuple-element.104.refs_5_), channel_id=1, source_target_pairs={{0,8},{4,12},{8,0},{12,4},{1,9},{5,13},{9,1},{13,5},{2,10},{6,14},... | collective-permute-start | bytes 3145736 | tf_op jit(solution)/shard_map/ppermute | solution.py:198
  131.1 21.6 %collective-permute-start.22 = (f32[4,2,256,128]{3,2,1,0:T(8,128)}, f32[4,2,256,128]{3,2,1,0:T(8,128)S(1)}, u32[]{:S(2)}, u32[]{:S(2)}) collective-permute-start(f32[4,2,256,128]{3,2,1,0:T(8,128)} %collective-permute-done.15.refs_7_), channel_id=1, source_target_pairs={{0,8},{4,12},{8,0},{12,4},{1,9},{5,13},{9,1},{13,5},{2,10},{6,14},... | collective-permute-start | bytes 3145736 | tf_op jit(solution)/shard_map/ppermute | solution.py:198
  132.4 20.4 %collective-permute-start.23 = (f32[4,2,256,128]{3,2,1,0:T(8,128)}, f32[4,2,256,128]{3,2,1,0:T(8,128)S(1)}, u32[]{:S(2)}, u32[]{:S(2)}) collective-permute-start(f32[4,2,256,128]{3,2,1,0:T(8,128)} %collective-permute-done.14.refs_10_), channel_id=1, source_target_pairs={{0,4},{4,0},{8,12},{12,8},{1,5},{5,1},{9,13},{13,9},{2,6},{6,2},{1... | collective-permute-start | bytes 3145736 | tf_op jit(solution)/shard_map/ppermute | solution.py:198
  132.7 20.0 %collective-permute-start.19 = (f32[4,2,128,256]{3,2,1,0:T(8,128)S(1)}, f32[4,2,128,256]{3,2,1,0:T(8,128)S(1)}, u32[]{:S(2)}, u32[]{:S(2)}) collective-permute-start(f32[4,2,128,256]{3,2,1,0:T(8,128)S(1)} %collective-permute-done.18.refs_4_), channel_id=1, source_target_pairs={{1,0},{5,4},{9,8},{13,12},{17,16},{21,20},{25,24},{29,28}} | collective-permute-start | bytes 3145736 | tf_op jit(solution)/shard_map/ppermute | solution.py:198
  133.4 19.3 %collective-permute-start.17 = (f32[4,2,128,256]{3,2,1,0:T(8,128)S(1)}, f32[4,2,128,256]{3,2,1,0:T(8,128)S(1)}, u32[]{:S(2)}, u32[]{:S(2)}) collective-permute-start(f32[4,2,128,256]{3,2,1,0:T(8,128)S(1)} %collective-permute-done.13.refs_3_), channel_id=1, source_target_pairs={{2,3},{6,7},{10,11},{14,15},{18,19},{22,23},{26,27},{30,31}} | collective-permute-start | bytes 3145736 | tf_op jit(solution)/shard_map/ppermute | solution.py:198
  165.8 15.6 %collective-permute-start.24 = (f32[512,2048]{1,0:T(8,128)S(1)}, f32[512,2048]{1,0:T(8,128)S(1)}, u32[]{:S(2)}, u32[]{:S(2)}) collective-permute-start(f32[512,2048]{1,0:T(8,128)S(1)} %get-tuple-element.126), channel_id=1, source_target_pairs={{0,16},{16,0},{1,17},{17,1},{2,18},{18,2},{3,19},{19,3},{4,20},{20... | collective-permute-start | bytes 12582920 | tf_op jit(solution)/shard_map/ppermute | solution.py:331
  (24 other events, 270.5 us)

commit v4 on v3

--- a/solution.py
+++ b/solution.py
@@ -107,17 +107,39 @@
     place_u(u_refs, lambda b, j: u_tgt[node, u_base[b] + j], u_cats.at[step])
 
 
-def finish_kernel(n_l, n_u, start, l_tgt, u_tgt, l_base, u_base, *refs):
+def finish_kernel(first, halves, n_l, n_u, start, l_tgt, u_tgt, l_base, u_base, *refs):
     l_refs, u_refs, refs = refs[:n_l], refs[n_l : n_l + n_u], refs[n_l + n_u :]
-    inv_ref, _, _, _, _, l_cats, u_cats, send, token = refs
+    n = len(halves)
+    inv_ref, _, refs = refs[0], refs[1], refs[2:]
+    ins, (l_cats, u_cats), accs, token = refs[2 : 2 + n], refs[2 + n : 4 + n], refs[4 + n : 4 + 2 * n], refs[-1]
     step = pl.program_id(0)
     node = start + step
     token[...] = jnp.zeros_like(token)
+    if first:
+
+        @pl.when(step == 0)
+        def _():
+            for half, src, acc in zip(halves, ins, accs):
+                acc[...] = src[...] if half else jnp.zeros_like(acc)
+
     l_cat, u_cat = l_cats.at[step], u_cats.at[step]
+    add_l(l_refs, lambda b, j: slot_rows(l_tgt, l_base, node, b, j), inv_ref, l_cat)
+    place_u(u_refs, lambda b, j: u_tgt[node, u_base[b] + j], u_cat)
+    for half, acc in zip(halves, accs):
+        part = product(l_cat, u_cat, half)
+        acc[...] = acc[...] - part if half else acc[...] + part
+
+
+def keep_kernel(l_cats, u_cats, _, keep_in, keep):
+    step = pl.program_id(0)
+    keep[...] -= product(l_cats.at[step], u_cats.at[step], 1)
+
+
+def add_l(l_refs, targets, inv_ref, l_cat):
     inv = split(inv_ref[0])
     for b, ref in enumerate(l_refs):
         for j in range(ref.shape[1]):
-            tgt = slot_rows(l_tgt, l_base, node, b, j)
+            tgt = targets(b, j)
 
             @pl.when(tgt >= 0)
             def _(ref=ref, j=j, tgt=tgt):
@@ -125,29 +147,23 @@
                 l_cat[block(tgt), 0:W] = hi
                 l_cat[block(tgt), W : 2 * W] = lo
 
-    place_u(u_refs, lambda b, j: u_tgt[node, u_base[b] + j], u_cat)
-    send[...] += product(l_cat, u_cat, 0)
-
-
-def keep_kernel(l_cats, u_cats, _, keep_in, keep):
-    step = pl.program_id(0)
-    keep[...] -= product(l_cats.at[step], u_cats.at[step], 1)
-
 
 RAW = pltpu.VMEM((AR * B, W), BF16)
 L_CAT = (AR * B, 2 * W)
 U_CAT = (2 * W, AC * B)
-PARAMS = pltpu.CompilerParams(dimension_semantics=("arbitrary",), vmem_limit_bytes=32 << 20)
-
-
-def call(kernel, nodes, offsets, tables, l_bufs, u_bufs, u11_inv, token, held, out, fixed, scratch):
+PARAMS = pltpu.CompilerParams(dimension_semantics=("arbitrary",), vmem_limit_bytes=20 << 20)
+
+
+def call(kernel, nodes, offsets, tables, l_bufs, u_bufs, u11_inv, token, held, out, aliases, scratch, pin=True):
     start, stop = nodes
 
     def per_node(buf, offset):
         return pl.BlockSpec((1,) + buf.shape[1:], lambda s, *_: (offset + s, 0, 0, 0))
 
     vmem, anywhere = pl.BlockSpec(memory_space=pltpu.VMEM), pl.BlockSpec(memory_space=pl.ANY)
-    bufs = [pltpu.with_memory_space_constraint(b, pltpu.HBM) for b in (*l_bufs, *u_bufs)]
+    bufs = [*l_bufs, *u_bufs]
+    if pin:
+        bufs = [pltpu.with_memory_space_constraint(b, pltpu.HBM) for b in bufs]
     n_in = 6 + len(bufs)
     return pl.pallas_call(
         functools.partial(kernel, len(l_bufs), len(u_bufs), start),
@@ -161,19 +177,22 @@
             out_specs=(vmem,) * (len(out) + 1),
             scratch_shapes=scratch,
         ),
-        input_output_aliases={n_in + i: i for i in range(len(held))} if fixed else {},
+        input_output_aliases={n_in + i: o for i, o in aliases.items()},
         compiler_params=PARAMS,
     )(*tables, *bufs, u11_inv, token, *held)
 
 
-def apply_update(nodes, offsets, tables, l_bufs, u_bufs, inv, token, accs, first=False):
-    kernel = lambda n_l, n_u, start, *refs: update_kernel(n_l, n_u, start, first, *refs)
-    out = [pltpu.VMEM((HALF, AC * B), F32)] * 2
+ACC = pltpu.VMEM((HALF, AC * B), F32)
+
+
+def apply_update(nodes, tables, l_bufs, u_bufs, inv, token, keep):
+    kernel = lambda n_l, n_u, start, *refs: update_kernel(n_l, n_u, start, True, *refs)
     scratch = [RAW, RAW, pltpu.VMEM(L_CAT, BF16), pltpu.VMEM(U_CAT, BF16)]
-    *accs, token = call(
-        kernel, nodes, offsets, tables, l_bufs, u_bufs, inv, token, accs, out, not first, scratch
+    offsets = [0] * (len(l_bufs) + len(u_bufs))
+    send, keep, _ = call(
+        kernel, nodes, offsets, tables, l_bufs, u_bufs, inv, token, (token, keep), [ACC] * 2, {}, scratch
     )
-    return token, accs
+    return send, keep
 
 
 class Box:
@@ -239,9 +258,11 @@
         return u3, d3, f0, f1
 
     def buffers(self, third):
-        u3, d3, f0, f1 = third
-        l_bufs = [self.l] + [b.value for b in (self.u1, self.d1, self.u2, self.d2, u3, d3)]
-        u_bufs = [*self.h] + [b.value for b in (self.x0, self.x1, self.y0, self.y1, f0, f1)]
+        names = ("u1", "d1", "u2", "d2", "x0", "x1", "y0", "y1")
+        v = {n: getattr(self, n).value if hasattr(self, n) else None for n in names}
+        u3, d3, f0, f1 = (b.value for b in third)
+        l_bufs = [self.l, v["u1"], v["d1"], v["u2"], v["d2"], u3, d3]
+        u_bufs = [*self.h, v["x0"], v["y1"], v["x1"], v["y0"], f0, f1]
         return l_bufs, u_bufs
 
 
@@ -259,74 +280,91 @@
         half = u_slots // 2
         sources = jnp.stack([col, col - 1, col + 1, col - 2, col + 2, col - 3, col + 3])
         l_base = jnp.where((sources >= 0) & (sources < cols), sources * l_slots, -1)
-        squares = jnp.stack([row, row, row ^ 1, row ^ 1, row ^ 2, row ^ 2, row ^ 3, row ^ 3])
-        u_base = squares * u_slots + half * (jnp.arange(8, dtype=jnp.int32) % 2)
-        tables = [t.astype(jnp.int32) for t in (l_tgt, u_tgt, l_base, u_base)]
+        squares = jnp.stack([row, row, row ^ 1, row ^ 2, row ^ 1, row ^ 2, row ^ 3, row ^ 3])
+        u_base = squares * u_slots + half * jnp.array([0, 1, 0, 1, 1, 0, 0, 1], jnp.int32)
         links = [Link("row"), Link("row"), Link("col"), Link("col")]
-        size, part = nodes // 2, nodes // 4
+        size = 5
         chunks = []
-        for start in (0, size):
-            here = slice(start, start + size)
+        for here in (slice(0, size), slice(size, nodes)):
             chunks.append(Exchange(links, l_own[here], u_own[here, :half], u_own[here, half:]))
         one, two = chunks
-
         one.first()
         one.second()
         third = one.third(slice(0, size))
-        two.first()
         zero = jnp.zeros((8, 128), F32)
-        token, accs = apply_update(
-            (0, part), [0] * 15, tables, *one.buffers(third), inv, zero, (zero, keep), True
-        )
+
+        def run(kernel, chunk, third, here, ls, us, token, held, out, aliases, scratch=(), pin=True):
+            l_bufs, u_bufs = chunk.buffers(third)
+            tables = [t.astype(jnp.int32) for t in (l_tgt, u_tgt, l_base[ls], u_base[us])]
+            l_bufs, u_bufs = l_bufs[ls], u_bufs[us]
+            offsets = [here[0] - (0 if chunk is one else size)] * (len(l_bufs) + len(u_bufs))
+            return call(
+                kernel, here, offsets, tables, l_bufs, u_bufs, inv, token, held, out, aliases, list(scratch), pin
+            )
+
+        def cats(count):
+            return [pltpu.VMEM((count,) + shape, BF16) for shape in (L_CAT, U_CAT)]
+
+        early, late = (slice(0, 5), slice(0, 6)), (slice(5, 7), slice(6, 8))
+        parts = ((0, 3), (3, size))
+        held = []
+        token = zero
+        for here in parts:
+            *cat, token = run(
+                prepare_kernel, one, third, here, *early, token, (), cats(here[1] - here[0]), {}, (RAW, RAW)
+            )
+            held.append(cat)
         token = Box(token)
         hold(links, token)
-        two.second()
-        token, accs = apply_update(
-            (part, size), [part] * 15, tables, *one.buffers(third), inv, token.value, accs
+        accs, first = (zero, keep), True
+        for stage, here, cat in zip((two.first, two.second), parts, held):
+            stage()
+            *_, send, keep, token = run(
+                functools.partial(finish_kernel, first, (0, 1)),
+                one,
+                third,
+                here,
+                *late,
+                token.value,
+                (*cat, *accs),
+                [*cats(here[1] - here[0]), ACC, ACC],
+                {0: 0, 1: 1} if first else {0: 0, 1: 1, 2: 2, 3: 3},
+            )
+            accs, first, token = (send, keep), False, Box(token)
+            hold(links, token)
+        last = two.third(slice(0, nodes - size))
+        here = (size, nodes)
+        *cat, token = run(
+            prepare_kernel, two, last, here, *early, token.value, (), cats(nodes - size), {}, (RAW, RAW)
         )
-        token = Box(token)
-        hold(links, token)
-        third = two.third(slice(0, size))
-        l_bufs, u_bufs = two.buffers(third)
-        late = (size, nodes), [0] * 15
-        cats = [pltpu.VMEM((size,) + shape, BF16) for shape in (L_CAT, U_CAT)]
-        l_cats, u_cats, token = call(
-            prepare_kernel, *late, tables, l_bufs[:5], u_bufs[:6], inv, token.value, (), cats, True, [RAW, RAW]
-        )
-        send, keep = accs
-        tables = [l_tgt, u_tgt, l_base[5:], u_base[6:]]
-        tables = [t.astype(jnp.int32) for t in tables]
-        l_cats, u_cats, send, token = call(
-            finish_kernel,
+        *cat, send, token = run(
+            functools.partial(finish_kernel, False, (0,)),
+            two,
+            last,
+            here,
             *late,
-            tables,
-            l_bufs[5:],
-            u_bufs[6:],
-            inv,
             token,
-            (l_cats, u_cats, send),
-            (*cats, pltpu.VMEM((HALF, AC * B), F32)),
-            True,
-            [],
+            (*cat, send),
+            [*cats(nodes - size), ACC],
+            {0: 0, 1: 1, 2: 2},
+            pin=False,
         )
         vmem = pl.BlockSpec(memory_space=pltpu.VMEM)
         keep = pl.pallas_call(
             keep_kernel,
-            grid=(size,),
-            out_shape=pltpu.VMEM((HALF, AC * B), F32),
+            grid=(nodes - size,),
+            out_shape=ACC,
             in_specs=[vmem, vmem, pl.BlockSpec(memory_space=pl.ANY), vmem],
             out_specs=vmem,
             input_output_aliases={3: 0},
             compiler_params=PARAMS,
-        )(l_cats, u_cats, token, keep)
+        )(*cat, token, keep)
     else:
         l_all = lax.all_gather(l_own, "col", axis=1, tiled=True)
         u_all = lax.all_gather(u_own, "row", axis=1, tiled=True)
         base, zero = jnp.zeros((1,), jnp.int32), jnp.zeros((8, 128), F32)
         tables = [t.astype(jnp.int32) for t in (l_tgt, u_tgt, base, base)]
-        _, (send, keep) = apply_update(
-            (0, nodes), [0, 0], tables, [l_all], [u_all], inv, zero, (zero, keep), True
-        )
+        send, keep = apply_update((0, nodes), tables, [l_all], [u_all], inv, zero, keep)
 
     other = lax.ppermute(send, "gz", [(0, 1), (1, 0)])
     return (keep - other)[None]

time: 186 us -> 179 us (0.962)
  waiting for transfers between devices: 64.3 us -> 58.5 us
  local copies, waits for them, and re-layouts: 11.1 us -> 6.71 us
    ppermute x24, waiting for transfers between devices: 64.3 us -> 57.7 us  [send(): out = Box(lax.ppermute(after(x, self.wait), self.axis, pairs))]
    unnamed x62 -> x46, local copies, waits for them, and re-layouts: 6.25 us -> 0.11 us
    pallas_call x4 -> x6, Pallas kernels: 47.3 us -> 50.7 us  [call(): pl.pallas_call(functools.partial(kernel, len(l_bufs), len(u_bufs), start)...]
    ppermute x24, starting transfers between devices: 42.7 us -> 44.9 us  [send(): out = Box(lax.ppermute(after(x, self.wait), self.axis, pairs))]
    pallas_call x1, Pallas kernels: 8.11 us -> 5.91 us  [body(): pl.pallas_call(keep_kernel, grid=(nodes - size,), out_shape=ACC, in_specs...]
    slice x2 -> x3, local copies, waits for them, and re-layouts: 0.14 us -> 2.03 us  [the longest x1 1.89 us: body(): u_own[here, half:]]
  transfers between devices with their start and end apart: 25 -> 25, of which waited for: 7 -> 9; matrix products, arithmetic and copies ran while one was open for 1% -> 3% of each run, Pallas kernels for 24% -> 28%
where the time goes in v4:
time: 179 us; the launch traced here: 177 us
  waiting for transfers between devices  58.5 us (33%)
  Pallas kernels  56.6 us (32%)
  starting transfers between devices  51.6 us (29%)
  local copies, waits for them, and re-layouts  6.71 us (4%)
  other arithmetic  2.8 us (2%)
    ppermute x24, waiting for transfers between devices, send(): out = Box(lax.ppermute(after(x, self.wait), self.axis, pairs))  57.7 us
    pallas_call x6, Pallas kernels, call(): pl.pallas_call(functools.partial(kernel, len(l_bufs), len(u_bufs), start)...  50.7 us
    ppermute x24, starting transfers between devices, send(): out = Box(lax.ppermute(after(x, self.wait), self.axis, pairs))  44.9 us
    ppermute x1, starting transfers between devices, body(): other = lax.ppermute(send, 'gz', [(0, 1), (1, 0)])  6.72 us
    pallas_call x1, Pallas kernels, body(): pl.pallas_call(keep_kernel, grid=(nodes - size,), out_shape=ACC, in_specs...  5.91 us
  transfers between devices with their start and end apart: 25, of which 9 were waited for; matrix products, arithmetic and copies ran while one was open for 3% of the time, Pallas kernels for 28%

profile of v4, /device:TPU:17, one launch (start us, length us, event | category | flops | bytes accessed | tf_op | source)
XLA Modules:
  0.0 176.7 jit_solution(2638163703366651115)
XLA Ops:
  0.0 1.4 slice_bitcast_fusion.refs_0_
  1.5 3.3 %collective-permute-start = (f32[5,2,128,256]{3,2,1,0:T(8,128)S(1)}, f32[5,2,128,256]{3,2,1,0:T(8,128)S(1)}, u32[]{:S(2)}, u32[]{:S(2)}) collective-permute-start(f32[5,2,128,256]{3,2,1,0:T(8,128)S(1)} %slice_bitcast_fusion.refs_0_), channel_id=1, source_target_pairs={{0,1},{1,2},{2,3},{4,5},{5,6},{6,7},{8,9},{9,10},{10,11},{12,13},{... | collective-permute-start | bytes 3932168 | tf_op jit(solution)/shard_map/ppermute | solution.py:217
  4.8 2.1 %collective-permute-start.3 = (f32[5,2,128,256]{3,2,1,0:T(8,128)S(1)}, f32[5,2,128,256]{3,2,1,0:T(8,128)S(1)}, u32[]{:S(2)}, u32[]{:S(2)}) collective-permute-start(f32[5,2,128,256]{3,2,1,0:T(8,128)S(1)} %slice_bitcast_fusion.refs_0_), channel_id=1, source_target_pairs={{1,0},{2,1},{3,2},{5,4},{6,5},{7,6},{9,8},{10,9},{11,10},{13,12},{... | collective-permute-start | bytes 3932168 | tf_op jit(solution)/shard_map/ppermute | solution.py:217
  6.9 1.9 %fusion.3 = (f32[5,2,256,128]{3,2,1,0:T(8,128)S(1)}, f32[5,2,256,128]{3,2,1,0:T(8,128)S(1)}) fusion(f32[8,4,256,128]{3,2,1,0:T(8,128)} %bitcast.50), kind=kLoop, calls=%fused_computation.11 | loop fusion | bytes 5242880 | tf_op jit(solution)/shard_map/slice | solution.py:289
  8.9 1.3 collective-permute-start.5
  11.4 21.9 %collective-permute-done.refs_1_ = f32[5,2,128,256]{3,2,1,0:T(8,128)S(1)} collective-permute-done((f32[5,2,128,256]{3,2,1,0:T(8,128)S(1)}, f32[5,2,128,256]{3,2,1,0:T(8,128)S(1)}, u32[]{:S(2)}, u32[]{:S(2)}) %collective-permute-start) | collective-permute-done | bytes 1310752 | tf_op jit(solution)/shard_map/ppermute | solution.py:217
  33.3 3.2 %collective-permute-start.1 = (f32[5,2,128,256]{3,2,1,0:T(8,128)S(1)}, f32[5,2,128,256]{3,2,1,0:T(8,128)}, u32[]{:S(2)}, u32[]{:S(2)}) collective-permute-start(f32[5,2,128,256]{3,2,1,0:T(8,128)S(1)} %collective-permute-done.refs_1_), channel_id=1, source_target_pairs={{1,2},{2,3},{5,6},{6,7},{9,10},{10,11},{13,14},{14,15},{17,18},{18... | collective-permute-start | bytes 3932168 | tf_op jit(solution)/shard_map/ppermute | solution.py:217
  36.5 4.2 %collective-permute-start.4 = (f32[5,2,128,256]{3,2,1,0:T(8,128)S(1)}, f32[5,2,128,256]{3,2,1,0:T(8,128)}, u32[]{:S(2)}, u32[]{:S(2)}) collective-permute-start(f32[5,2,128,256]{3,2,1,0:T(8,128)S(1)} %collective-permute-done.3.refs_2_), channel_id=1, source_target_pairs={{1,0},{2,1},{5,4},{6,5},{9,8},{10,9},{13,12},{14,13},{17,16},{18,1... | collective-permute-start | bytes 3932168 | tf_op jit(solution)/shard_map/ppermute | solution.py:217
  43.2 20.9 %collective-permute-done.1.refs_3_ = f32[5,2,128,256]{3,2,1,0:T(8,128)} collective-permute-done((f32[5,2,128,256]{3,2,1,0:T(8,128)S(1)}, f32[5,2,128,256]{3,2,1,0:T(8,128)}, u32[]{:S(2)}, u32[]{:S(2)}) %collective-permute-start.1) | collective-permute-done | bytes 1310752 | tf_op jit(solution)/shard_map/ppermute | solution.py:217
  64.1 4.3 %collective-permute-start.2 = (f32[5,2,128,256]{3,2,1,0:T(8,128)}, f32[5,2,128,256]{3,2,1,0:T(8,128)}, u32[]{:S(2)}, u32[]{:S(2)}) collective-permute-start(f32[5,2,128,256]{3,2,1,0:T(8,128)} %collective-permute-done.1.refs_3_), channel_id=1, source_target_pairs={{2,3},{6,7},{10,11},{14,15},{18,19},{22,23},{26,27},{30,31}} | collective-permute-start | bytes 3932168 | tf_op jit(solution)/shard_map/ppermute | solution.py:217
  68.3 1.7 collective-permute-start.10
  71.3 1.3 collective-permute-start.11
  74.0 1.8 fusion.2
  75.9 7.0 %shard_map.73 = (bf16[3,1024,512]{2,1,0:T(8,128)(2,1)S(1)}, bf16[3,512,2048]{2,1,0:T(8,128)(2,1)S(1)}, f32[8,128]{1,0:T(8,128)S(1)}) custom-call(s32[8,8]{1,0:T(8,128)S(1)} %fusion.1.l_tgt, s32[8,16]{1,0:T(8,128)S(1)} %bitcast.38, s32[5]{0:T(128)S(1)} %bitcast.44, s32[6]{0:T(128)S(1)} %bitcast.47, f32[5,2,128,256]{3,2,1,0:T(8,128)} %copy-done.5, ...), custom_call_target="tpu_custom_call" | custom-call | tf_op jit(solution)/shard_map/pallas_call | solution.py:168
  82.9 5.5 %shard_map.74 = (bf16[2,1024,512]{2,1,0:T(8,128)(2,1)S(1)}, bf16[2,512,2048]{2,1,0:T(8,128)(2,1)S(1)}, f32[8,128]{1,0:T(8,128)S(1)}) custom-call(s32[8,8]{1,0:T(8,128)S(1)} %fusion.1.l_tgt, s32[8,16]{1,0:T(8,128)S(1)} %bitcast.39, s32[5]{0:T(128)S(1)} %bitcast.45, s32[6]{0:T(128)S(1)} %bitcast.48, f32[5,2,128,256]{3,2,1,0:T(8,128)} %copy-done.5, ...), custom_call_target="tpu_custom_call" | custom-call | tf_op jit(solution)/shard_map/pallas_call | solution.py:168
  88.4 4.9 %collective-permute-done.2.refs_0_ = f32[5,2,128,256]{3,2,1,0:T(8,128)} collective-permute-done((f32[5,2,128,256]{3,2,1,0:T(8,128)}, f32[5,2,128,256]{3,2,1,0:T(8,128)}, u32[]{:S(2)}, u32[]{:S(2)}) %collective-permute-start.2) | collective-permute-done | bytes 1310752 | tf_op jit(solution)/shard_map/ppermute | solution.py:217
  93.3 4.1 %collective-permute-start.9 = (f32[3,2,128,256]{3,2,1,0:T(8,128)S(1)}, f32[3,2,128,256]{3,2,1,0:T(8,128)S(1)}, u32[]{:S(2)}, u32[]{:S(2)}) collective-permute-start(f32[3,2,128,256]{3,2,1,0:T(8,128)S(1)} %slice_bitcast_fusion.1.refs_0_), channel_id=1, source_target_pairs={{0,1},{1,2},{2,3},{4,5},{5,6},{6,7},{8,9},{9,10},{10,11},{12,13},{... | collective-permute-start | bytes 2359304 | tf_op jit(solution)/shard_map/ppermute | solution.py:217
  97.4 1.9 %collective-permute-start.16 = (f32[3,2,128,256]{3,2,1,0:T(8,128)S(1)}, f32[3,2,128,256]{3,2,1,0:T(8,128)S(1)}, u32[]{:S(2)}, u32[]{:S(2)}) collective-permute-start(f32[3,2,128,256]{3,2,1,0:T(8,128)S(1)} %slice_bitcast_fusion.1.refs_0_), channel_id=1, source_target_pairs={{1,0},{2,1},{3,2},{5,4},{6,5},{7,6},{9,8},{10,9},{11,10},{13,12},{... | collective-permute-start | bytes 2359304 | tf_op jit(solution)/shard_map/ppermute | solution.py:217
  99.4 1.3 collective-permute-start.15
  102.0 14.4 %shard_map.75 = (bf16[3,1024,512]{2,1,0:T(8,128)(2,1)S(1)}, bf16[3,512,2048]{2,1,0:T(8,128)(2,1)S(1)}, f32[512,2048]{1,0:T(8,128)S(1)}, f32[512,2048]{1,0:T(8,128)S(1)}, f32[8,128]{1,0:T(8,128)S(1)}) custom-call(s32[8,8]{1,0:T(8,128)S(1)} %fusion.1.l_tgt, s32[8,16]{1,0:T(8,128)S(1)} %bitcast.40, ...), custom_call_target="tpu_custom_call", output_to_operand_aliasing={{0}: (10, {}), {1}: (11, {})} | custom-call | tf_op jit(solution)/shard_map/pallas_call | solution.py:168
  116.5 4.5 %collective-permute-start.13 = (f32[3,2,128,256]{3,2,1,0:T(8,128)S(1)}, f32[3,2,128,256]{3,2,1,0:T(8,128)S(1)}, u32[]{:S(2)}, u32[]{:S(2)}) collective-permute-start(f32[3,2,128,256]{3,2,1,0:T(8,128)S(1)} %collective-permute-done.9.refs_1_), channel_id=1, source_target_pairs={{1,2},{2,3},{5,6},{6,7},{9,10},{10,11},{13,14},{14,15},{17,18},{18... | collective-permute-start | bytes 2359304 | tf_op jit(solution)/shard_map/ppermute | solution.py:217
  120.9 1.5 collective-permute-start.18
  123.4 9.7 %shard_map.76 = (bf16[2,1024,512]{2,1,0:T(8,128)(2,1)S(1)}, bf16[2,512,2048]{2,1,0:T(8,128)(2,1)S(1)}, f32[512,2048]{1,0:T(8,128)S(1)}, f32[512,2048]{1,0:T(8,128)S(1)}, f32[8,128]{1,0:T(8,128)S(1)}) custom-call(s32[8,8]{1,0:T(8,128)S(1)} %fusion.1.l_tgt, ...), custom_call_target="tpu_custom_call", output_to_operand_aliasing={{0}: (10, {}), {1}: (11, {}), {2}: (12, {}), {3}: (13, {})} | custom-call | tf_op jit(solution)/shard_map/pallas_call | solution.py:168
  133.4 1.3 collective-permute-done.18.refs_4_
  134.7 2.3 %collective-permute-done.21.refs_9_ = f32[3,2,256,128]{3,2,1,0:T(8,128)S(1)} collective-permute-done((f32[3,2,256,128]{3,2,1,0:T(8,128)S(1)}, f32[3,2,256,128]{3,2,1,0:T(8,128)S(1)}, u32[]{:S(2)}, u32[]{:S(2)}) %collective-permute-start.21) | collective-permute-done | bytes 786464 | tf_op jit(solution)/shard_map/ppermute | solution.py:217
  139.1 1.3 collective-permute-start.17
  140.4 6.9 %shard_map.77 = (bf16[3,1024,512]{2,1,0:T(8,128)(2,1)S(1)}, bf16[3,512,2048]{2,1,0:T(8,128)(2,1)S(1)}, f32[8,128]{1,0:T(8,128)S(1)}) custom-call(s32[8,8]{1,0:T(8,128)S(1)} %fusion.1.l_tgt, s32[8,16]{1,0:T(8,128)S(1)} %bitcast.42, s32[5]{0:T(128)S(1)} %bitcast.46, s32[6]{0:T(128)S(1)} %bitcast.49, f32[3,2,128,256]{3,2,1,0:T(8,128)} %copy-done.10, ...), custom_call_target="tpu_custom_call" | custom-call | tf_op jit(solution)/shard_map/pallas_call | solution.py:168
  147.3 5.9 %collective-permute-done.22.refs_2_ = f32[3,2,256,128]{3,2,1,0:T(8,128)S(1)} collective-permute-done((f32[3,2,256,128]{3,2,1,0:T(8,128)S(1)}, f32[3,2,256,128]{3,2,1,0:T(8,128)S(1)}, u32[]{:S(2)}, u32[]{:S(2)}) %collective-permute-start.22) | collective-permute-done | bytes 786464 | tf_op jit(solution)/shard_map/ppermute | solution.py:217
  153.2 7.2 %shard_map.78 = (bf16[3,1024,512]{2,1,0:T(8,128)(2,1)S(1)}, bf16[3,512,2048]{2,1,0:T(8,128)(2,1)S(1)}, f32[512,2048]{1,0:T(8,128)S(1)}, f32[8,128]{1,0:T(8,128)S(1)}) custom-call(s32[8,8]{1,0:T(8,128)S(1)} %fusion.1.l_tgt, s32[8,16]{1,0:T(8,128)S(1)} %bitcast.43, s32[2]{0:T(128)S(1)} %slice.44.l_base, ...), custom_call_target="tpu_custom_call", output_to_operand_aliasing={{0}: (10, {}), {1}: (11, {}), {2}: (12, {})} | custom-call | tf_op jit(solution)/shard_map/pallas_call | solution.py:168
  160.4 6.7 %collective-permute-start.24 = (f32[512,2048]{1,0:T(8,128)S(1)}, f32[512,2048]{1,0:T(8,128)S(1)}, u32[]{:S(2)}, u32[]{:S(2)}) collective-permute-start(f32[512,2048]{1,0:T(8,128)S(1)} %get-tuple-element.146), channel_id=1, source_target_pairs={{0,16},{16,0},{1,17},{17,1},{2,18},{18,2},{3,19},{19,3},{4,20},{20... | collective-permute-start | bytes 12582920 | tf_op jit(solution)/shard_map/ppermute | solution.py:369
  167.2 5.9 %shard_map.79 = f32[512,2048]{1,0:T(8,128)S(1)} custom-call(bf16[3,1024,512]{2,1,0:T(8,128)(2,1)S(1)} %get-tuple-element.142.l_cats, bf16[3,512,2048]{2,1,0:T(8,128)(2,1)S(1)} %get-tuple-element.143.u_cats, f32[8,128]{1,0:T(8,128)S(1)} %get-tuple-element.144._, f32[512,2048]{1,0:T(8,128)S(1)} %get-tuple-element.145.keep_in), custom_call_target="tpu_custom_call", output_to_operand_aliasing={{}: (3, {})} | custom-call | tf_op jit(solution)/shard_map/pallas_call | solution.py:353
  173.9 2.8 %subtract_bitcast_fusion = f32[1,512,2048]{2,1,0:T(8,128)} fusion(f32[512,2048]{1,0:T(8,128)S(1)} %shard_map.79, f32[512,2048]{1,0:T(8,128)S(1)} %collective-permute-done.24), kind=kLoop, calls=%fused_computation | loop fusion | flops 1048576 | bytes 12582912 | tf_op jit(solution)/shard_map/broadcast_in_dim | solution.py:370
  (84 shorter events, 12.0 us)
Async XLA Ops:
  1.5 69.8 %copy-start.5 = (f32[5,2,128,256]{3,2,1,0:T(8,128)}, f32[5,2,128,256]{3,2,1,0:T(8,128)S(1)}, u32[]{:S(2)}) copy-start(f32[5,2,128,256]{3,2,1,0:T(8,128)S(1)} %slice_bitcast_fusion.refs_0_) | copy-start | bytes 3932164
  1.5 71.3 %copy-start.22 = (s32[8]{0:T(128)S(1)}, s32[8]{0:T(128)}, u32[]{:S(2)}) copy-start(s32[8]{0:T(128)} %constant.60) | copy-start | bytes 100
  1.5 71.3 %copy-start.21 = (s32[1,8,1,8]{3,2,1,0:T(1,128)S(1)}, s32[1,8,1,8]{3,2,1,0:T(1,128)}, u32[]{:S(2)}) copy-start(s32[1,8,1,8]{3,2,1,0:T(1,128)} %param.8) | copy-start | bytes 772
  1.5 31.8 %collective-permute-start = (f32[5,2,128,256]{3,2,1,0:T(8,128)S(1)}, f32[5,2,128,256]{3,2,1,0:T(8,128)S(1)}, u32[]{:S(2)}, u32[]{:S(2)}) collective-permute-start(f32[5,2,128,256]{3,2,1,0:T(8,128)S(1)} %slice_bitcast_fusion.refs_0_), channel_id=1, source_target_pairs={{0,1},{1,2},{2,3},{4,5},{5,6},{6,7},{8,9},{9,10},{10,11},{12,13},{... | collective-permute-start | bytes 3932168 | tf_op jit(solution)/shard_map/ppermute | solution.py:217
  4.8 31.6 %collective-permute-start.3 = (f32[5,2,128,256]{3,2,1,0:T(8,128)S(1)}, f32[5,2,128,256]{3,2,1,0:T(8,128)S(1)}, u32[]{:S(2)}, u32[]{:S(2)}) collective-permute-start(f32[5,2,128,256]{3,2,1,0:T(8,128)S(1)} %slice_bitcast_fusion.refs_0_), channel_id=1, source_target_pairs={{1,0},{2,1},{3,2},{5,4},{6,5},{7,6},{9,8},{10,9},{11,10},{13,12},{... | collective-permute-start | bytes 3932168 | tf_op jit(solution)/shard_map/ppermute | solution.py:217
  8.8 61.3 %copy-start.4 = (f32[5,2,256,128]{3,2,1,0:T(8,128)}, f32[5,2,256,128]{3,2,1,0:T(8,128)S(1)}, u32[]{:S(2)}) copy-start(f32[5,2,256,128]{3,2,1,0:T(8,128)S(1)} %get-tuple-element.87.refs_5_) | copy-start | bytes 3932164
  8.8 67.0 %copy-start.3 = (f32[5,2,256,128]{3,2,1,0:T(8,128)}, f32[5,2,256,128]{3,2,1,0:T(8,128)S(1)}, u32[]{:S(2)}) copy-start(f32[5,2,256,128]{3,2,1,0:T(8,128)S(1)} %get-tuple-element.85.refs_6_) | copy-start | bytes 3932164
  8.8 67.0 %copy-start = (f32[1,8,256,256]{3,2,1,0:T(8,128)S(1)}, f32[1,8,256,256]{3,2,1,0:T(8,128)}, u32[]{:S(2)}) copy-start(f32[1,8,256,256]{3,2,1,0:T(8,128)} %param.11) | copy-start | bytes 6291460
  8.8 67.0 %copy-start.2 = (s32[1,8,1,16]{3,2,1,0:T(1,128)S(1)}, s32[1,8,1,16]{3,2,1,0:T(1,128)}, u32[]{:S(2)}) copy-start(s32[1,8,1,16]{3,2,1,0:T(1,128)} %param.10) | copy-start | bytes 1540
  8.9 31.9 %collective-permute-start.5 = (f32[5,2,256,128]{3,2,1,0:T(8,128)S(1)}, f32[5,2,256,128]{3,2,1,0:T(8,128)}, u32[]{:S(2)}, u32[]{:S(2)}) collective-permute-start(f32[5,2,256,128]{3,2,1,0:T(8,128)S(1)} %get-tuple-element.87.refs_5_), channel_id=1, source_target_pairs={{0,4},{4,0},{8,12},{12,8},{1,5},{5,1},{9,13},{13,9},{2,6},{6,2},{1... | collective-permute-start | bytes 3932168 | tf_op jit(solution)/shard_map/ppermute | solution.py:217
  10.1 31.8 %collective-permute-start.6 = (f32[5,2,256,128]{3,2,1,0:T(8,128)S(1)}, f32[5,2,256,128]{3,2,1,0:T(8,128)}, u32[]{:S(2)}, u32[]{:S(2)}) collective-permute-start(f32[5,2,256,128]{3,2,1,0:T(8,128)S(1)} %get-tuple-element.85.refs_6_), channel_id=1, source_target_pairs={{0,8},{4,12},{8,0},{12,4},{1,9},{5,13},{9,1},{13,5},{2,10},{6,14},... | collective-permute-start | bytes 3932168 | tf_op jit(solution)/shard_map/ppermute | solution.py:217
  33.3 30.8 %collective-permute-start.1 = (f32[5,2,128,256]{3,2,1,0:T(8,128)S(1)}, f32[5,2,128,256]{3,2,1,0:T(8,128)}, u32[]{:S(2)}, u32[]{:S(2)}) collective-permute-start(f32[5,2,128,256]{3,2,1,0:T(8,128)S(1)} %collective-permute-done.refs_1_), channel_id=1, source_target_pairs={{1,2},{2,3},{5,6},{6,7},{9,10},{10,11},{13,14},{14,15},{17,18},{18... | collective-permute-start | bytes 3932168 | tf_op jit(solution)/shard_map/ppermute | solution.py:217
  36.5 31.9 %collective-permute-start.4 = (f32[5,2,128,256]{3,2,1,0:T(8,128)S(1)}, f32[5,2,128,256]{3,2,1,0:T(8,128)}, u32[]{:S(2)}, u32[]{:S(2)}) collective-permute-start(f32[5,2,128,256]{3,2,1,0:T(8,128)S(1)} %collective-permute-done.3.refs_2_), channel_id=1, source_target_pairs={{1,0},{2,1},{5,4},{6,5},{9,8},{10,9},{13,12},{14,13},{17,16},{18,1... | collective-permute-start | bytes 3932168 | tf_op jit(solution)/shard_map/ppermute | solution.py:217
  40.7 29.4 %collective-permute-start.7 = (f32[5,2,256,128]{3,2,1,0:T(8,128)S(1)}, f32[5,2,256,128]{3,2,1,0:T(8,128)S(1)}, u32[]{:S(2)}, u32[]{:S(2)}) collective-permute-start(f32[5,2,256,128]{3,2,1,0:T(8,128)S(1)} %get-tuple-element.85.refs_6_), channel_id=1, source_target_pairs={{0,4},{4,0},{8,12},{12,8},{1,5},{5,1},{9,13},{13,9},{2,6},{6,2},{1... | collective-permute-start | bytes 3932168 | tf_op jit(solution)/shard_map/ppermute | solution.py:217
  41.9 29.4 %collective-permute-start.8 = (f32[5,2,256,128]{3,2,1,0:T(8,128)S(1)}, f32[5,2,256,128]{3,2,1,0:T(8,128)S(1)}, u32[]{:S(2)}, u32[]{:S(2)}) collective-permute-start(f32[5,2,256,128]{3,2,1,0:T(8,128)S(1)} %get-tuple-element.87.refs_5_), channel_id=1, source_target_pairs={{0,8},{4,12},{8,0},{12,4},{1,9},{5,13},{9,1},{13,5},{2,10},{6,14},... | collective-permute-start | bytes 3932168 | tf_op jit(solution)/shard_map/ppermute | solution.py:217
  64.1 29.2 %collective-permute-start.2 = (f32[5,2,128,256]{3,2,1,0:T(8,128)}, f32[5,2,128,256]{3,2,1,0:T(8,128)}, u32[]{:S(2)}, u32[]{:S(2)}) collective-permute-start(f32[5,2,128,256]{3,2,1,0:T(8,128)} %collective-permute-done.1.refs_3_), channel_id=1, source_target_pairs={{2,3},{6,7},{10,11},{14,15},{18,19},{22,23},{26,27},{30,31}} | collective-permute-start | bytes 3932168 | tf_op jit(solution)/shard_map/ppermute | solution.py:217
  68.3 29.1 %collective-permute-start.10 = (f32[5,2,128,256]{3,2,1,0:T(8,128)}, f32[5,2,128,256]{3,2,1,0:T(8,128)}, u32[]{:S(2)}, u32[]{:S(2)}) collective-permute-start(f32[5,2,128,256]{3,2,1,0:T(8,128)} %collective-permute-done.4.refs_4_), channel_id=1, source_target_pairs={{1,0},{5,4},{9,8},{13,12},{17,16},{21,20},{25,24},{29,28}} | collective-permute-start | bytes 3932168 | tf_op jit(solution)/shard_map/ppermute | solution.py:217
  70.1 29.3 %collective-permute-start.12 = (f32[5,2,256,128]{3,2,1,0:T(8,128)}, f32[5,2,256,128]{3,2,1,0:T(8,128)}, u32[]{:S(2)}, u32[]{:S(2)}) collective-permute-start(f32[5,2,256,128]{3,2,1,0:T(8,128)} %collective-permute-done.6.refs_8_), channel_id=1, source_target_pairs={{0,4},{4,0},{8,12},{12,8},{1,5},{5,1},{9,13},{13,9},{2,6},{6,2},{1... | collective-permute-start | bytes 3932168 | tf_op jit(solution)/shard_map/ppermute | solution.py:217
  71.3 29.3 %collective-permute-start.11 = (f32[5,2,256,128]{3,2,1,0:T(8,128)}, f32[5,2,256,128]{3,2,1,0:T(8,128)}, u32[]{:S(2)}, u32[]{:S(2)}) collective-permute-start(f32[5,2,256,128]{3,2,1,0:T(8,128)} %collective-permute-done.5.refs_7_), channel_id=1, source_target_pairs={{0,8},{4,12},{8,0},{12,4},{1,9},{5,13},{9,1},{13,5},{2,10},{6,14},... | collective-permute-start | bytes 3932168 | tf_op jit(solution)/shard_map/ppermute | solution.py:217
  93.3 23.2 %collective-permute-start.9 = (f32[3,2,128,256]{3,2,1,0:T(8,128)S(1)}, f32[3,2,128,256]{3,2,1,0:T(8,128)S(1)}, u32[]{:S(2)}, u32[]{:S(2)}) collective-permute-start(f32[3,2,128,256]{3,2,1,0:T(8,128)S(1)} %slice_bitcast_fusion.1.refs_0_), channel_id=1, source_target_pairs={{0,1},{1,2},{2,3},{4,5},{5,6},{6,7},{8,9},{9,10},{10,11},{12,13},{... | collective-permute-start | bytes 2359304 | tf_op jit(solution)/shard_map/ppermute | solution.py:217
  97.4 19.1 %collective-permute-start.16 = (f32[3,2,128,256]{3,2,1,0:T(8,128)S(1)}, f32[3,2,128,256]{3,2,1,0:T(8,128)S(1)}, u32[]{:S(2)}, u32[]{:S(2)}) collective-permute-start(f32[3,2,128,256]{3,2,1,0:T(8,128)S(1)} %slice_bitcast_fusion.1.refs_0_), channel_id=1, source_target_pairs={{1,0},{2,1},{3,2},{5,4},{6,5},{7,6},{9,8},{10,9},{11,10},{13,12},{... | collective-permute-start | bytes 2359304 | tf_op jit(solution)/shard_map/ppermute | solution.py:217
  99.4 23.1 %collective-permute-start.15 = (f32[3,2,256,128]{3,2,1,0:T(8,128)S(1)}, f32[3,2,256,128]{3,2,1,0:T(8,128)S(1)}, u32[]{:S(2)}, u32[]{:S(2)}) collective-permute-start(f32[3,2,256,128]{3,2,1,0:T(8,128)S(1)} %get-tuple-element.124.refs_5_), channel_id=1, source_target_pairs={{0,4},{4,0},{8,12},{12,8},{1,5},{5,1},{9,13},{13,9},{2,6},{6,2},{1... | collective-permute-start | bytes 2359304 | tf_op jit(solution)/shard_map/ppermute | solution.py:217
  100.6 22.3 %collective-permute-start.14 = (f32[3,2,256,128]{3,2,1,0:T(8,128)S(1)}, f32[3,2,256,128]{3,2,1,0:T(8,128)S(1)}, u32[]{:S(2)}, u32[]{:S(2)}) collective-permute-start(f32[3,2,256,128]{3,2,1,0:T(8,128)S(1)} %get-tuple-element.126.refs_6_), channel_id=1, source_target_pairs={{0,8},{4,12},{8,0},{12,4},{1,9},{5,13},{9,1},{13,5},{2,10},{6,14},... | collective-permute-start | bytes 2359304 | tf_op jit(solution)/shard_map/ppermute | solution.py:217
  116.5 16.9 %collective-permute-start.13 = (f32[3,2,128,256]{3,2,1,0:T(8,128)S(1)}, f32[3,2,128,256]{3,2,1,0:T(8,128)S(1)}, u32[]{:S(2)}, u32[]{:S(2)}) collective-permute-start(f32[3,2,128,256]{3,2,1,0:T(8,128)S(1)} %collective-permute-done.9.refs_1_), channel_id=1, source_target_pairs={{1,2},{2,3},{5,6},{6,7},{9,10},{10,11},{13,14},{14,15},{17,18},{18... | collective-permute-start | bytes 2359304 | tf_op jit(solution)/shard_map/ppermute | solution.py:217
  120.9 13.7 %collective-permute-start.18 = (f32[3,2,128,256]{3,2,1,0:T(8,128)S(1)}, f32[3,2,128,256]{3,2,1,0:T(8,128)S(1)}, u32[]{:S(2)}, u32[]{:S(2)}) collective-permute-start(f32[3,2,128,256]{3,2,1,0:T(8,128)S(1)} %collective-permute-done.16.refs_2_), channel_id=1, source_target_pairs={{1,0},{2,1},{5,4},{6,5},{9,8},{10,9},{13,12},{14,13},{17,16},{18,1... | collective-permute-start | bytes 2359304 | tf_op jit(solution)/shard_map/ppermute | solution.py:217
  122.5 14.4 %collective-permute-start.21 = (f32[3,2,256,128]{3,2,1,0:T(8,128)S(1)}, f32[3,2,256,128]{3,2,1,0:T(8,128)S(1)}, u32[]{:S(2)}, u32[]{:S(2)}) collective-permute-start(f32[3,2,256,128]{3,2,1,0:T(8,128)S(1)} %get-tuple-element.126.refs_6_), channel_id=1, source_target_pairs={{0,4},{4,0},{8,12},{12,8},{1,5},{5,1},{9,13},{13,9},{2,6},{6,2},{1... | collective-permute-start | bytes 2359304 | tf_op jit(solution)/shard_map/ppermute | solution.py:217
  123.0 14.2 %collective-permute-start.20 = (f32[3,2,256,128]{3,2,1,0:T(8,128)S(1)}, f32[3,2,256,128]{3,2,1,0:T(8,128)S(1)}, u32[]{:S(2)}, u32[]{:S(2)}) collective-permute-start(f32[3,2,256,128]{3,2,1,0:T(8,128)S(1)} %get-tuple-element.124.refs_5_), channel_id=1, source_target_pairs={{0,8},{4,12},{8,0},{12,4},{1,9},{5,13},{9,1},{13,5},{2,10},{6,14},... | collective-permute-start | bytes 2359304 | tf_op jit(solution)/shard_map/ppermute | solution.py:217
  137.2 16.0 %collective-permute-start.22 = (f32[3,2,256,128]{3,2,1,0:T(8,128)S(1)}, f32[3,2,256,128]{3,2,1,0:T(8,128)S(1)}, u32[]{:S(2)}, u32[]{:S(2)}) collective-permute-start(f32[3,2,256,128]{3,2,1,0:T(8,128)S(1)} %collective-permute-done.15.refs_7_), channel_id=1, source_target_pairs={{0,8},{4,12},{8,0},{12,4},{1,9},{5,13},{9,1},{13,5},{2,10},{6,14},... | collective-permute-start | bytes 2359304 | tf_op jit(solution)/shard_map/ppermute | solution.py:217
  137.5 15.7 %collective-permute-start.23 = (f32[3,2,256,128]{3,2,1,0:T(8,128)S(1)}, f32[3,2,256,128]{3,2,1,0:T(8,128)S(1)}, u32[]{:S(2)}, u32[]{:S(2)}) collective-permute-start(f32[3,2,256,128]{3,2,1,0:T(8,128)S(1)} %collective-permute-done.14.refs_8_), channel_id=1, source_target_pairs={{0,4},{4,0},{8,12},{12,8},{1,5},{5,1},{9,13},{13,9},{2,6},{6,2},{1... | collective-permute-start | bytes 2359304 | tf_op jit(solution)/shard_map/ppermute | solution.py:217
  138.4 14.8 %collective-permute-start.19 = (f32[3,2,128,256]{3,2,1,0:T(8,128)S(1)}, f32[3,2,128,256]{3,2,1,0:T(8,128)S(1)}, u32[]{:S(2)}, u32[]{:S(2)}) collective-permute-start(f32[3,2,128,256]{3,2,1,0:T(8,128)S(1)} %collective-permute-done.18.refs_4_), channel_id=1, source_target_pairs={{1,0},{5,4},{9,8},{13,12},{17,16},{21,20},{25,24},{29,28}} | collective-permute-start | bytes 2359304 | tf_op jit(solution)/shard_map/ppermute | solution.py:217
  139.1 14.1 %collective-permute-start.17 = (f32[3,2,128,256]{3,2,1,0:T(8,128)S(1)}, f32[3,2,128,256]{3,2,1,0:T(8,128)S(1)}, u32[]{:S(2)}, u32[]{:S(2)}) collective-permute-start(f32[3,2,128,256]{3,2,1,0:T(8,128)S(1)} %collective-permute-done.13.refs_3_), channel_id=1, source_target_pairs={{2,3},{6,7},{10,11},{14,15},{18,19},{22,23},{26,27},{30,31}} | collective-permute-start | bytes 2359304 | tf_op jit(solution)/shard_map/ppermute | solution.py:217
  160.4 13.5 %collective-permute-start.24 = (f32[512,2048]{1,0:T(8,128)S(1)}, f32[512,2048]{1,0:T(8,128)S(1)}, u32[]{:S(2)}, u32[]{:S(2)}) collective-permute-start(f32[512,2048]{1,0:T(8,128)S(1)} %get-tuple-element.146), channel_id=1, source_target_pairs={{0,16},{16,0},{1,17},{17,1},{2,18},{18,2},{3,19},{19,3},{4,20},{20... | collective-permute-start | bytes 12582920 | tf_op jit(solution)/shard_map/ppermute | solution.py:369
  (16 other events, 297.5 us)

commit v5 on v4

--- a/solution.py
+++ b/solution.py
@@ -243,18 +243,18 @@
 
     def first(self):
         lx, ly, lu, ld = self.links
+        self.x0, self.y1 = lx.send(self.h[0], side(1)), ly.send(self.h[1], side(2))
         self.u1, self.d1 = lu.send(self.l, up(1)), ld.send(self.l, down(1))
-        self.x0, self.y1 = lx.send(self.h[0], side(1)), ly.send(self.h[1], side(2))
 
     def second(self):
         lx, ly, lu, ld = self.links
+        self.x1, self.y0 = lx.send(self.h[1], side(1)), ly.send(self.h[0], side(2))
         self.u2, self.d2 = lu.send(self.u1.value, up(2)), ld.send(self.d1.value, down(2))
-        self.x1, self.y0 = lx.send(self.h[1], side(1)), ly.send(self.h[0], side(2))
 
     def third(self, here):
         lx, ly, lu, ld = self.links
+        f1, f0 = lx.send(self.y1.value[here], side(1)), ly.send(self.x0.value[here], side(2))
         u3, d3 = lu.send(self.u2.value[here], up(3)), ld.send(self.d2.value[here], down(3))
-        f1, f0 = lx.send(self.y1.value[here], side(1)), ly.send(self.x0.value[here], side(2))
         return u3, d3, f0, f1
 
     def buffers(self, third):

time: 179 us -> 177 us (0.989)
    ppermute x24, starting transfers between devices: 44.9 us -> 42.6 us  [send(): out = Box(lax.ppermute(after(x, self.wait), self.axis, pairs))]
    slice x1 -> x0, local copies, waits for them, and re-layouts: 1.89 us -> none  [body(): u_own[here, half:]]
  transfers between devices with their start and end apart: 25 -> 25, of which waited for: 9 -> 13; matrix products, arithmetic and copies ran while one was open for 3% -> 2% of each run, Pallas kernels for 28% -> 28%
where the time goes in v5:
time: 177 us; the launch traced here: 174 us
  waiting for transfers between devices  59.4 us (34%)
  Pallas kernels  56.3 us (32%)
  starting transfers between devices  50.2 us (28%)
  local copies, waits for them, and re-layouts  5.27 us (3%)
  other arithmetic  2.8 us (2%)
    ppermute x24, waiting for transfers between devices, send(): out = Box(lax.ppermute(after(x, self.wait), self.axis, pairs))  58.4 us
    pallas_call x6, Pallas kernels, call(): pl.pallas_call(functools.partial(kernel, len(l_bufs), len(u_bufs), start)...  50.5 us
    ppermute x24, starting transfers between devices, send(): out = Box(lax.ppermute(after(x, self.wait), self.axis, pairs))  42.6 us
    ppermute x1, starting transfers between devices, body(): other = lax.ppermute(send, 'gz', [(0, 1), (1, 0)])  7.58 us
    pallas_call x1, Pallas kernels, body(): pl.pallas_call(keep_kernel, grid=(nodes - size,), out_shape=ACC, in_specs...  5.87 us
  transfers between devices with their start and end apart: 25, of which 13 were waited for; matrix products, arithmetic and copies ran while one was open for 2% of the time, Pallas kernels for 28%

profile of v5, /device:TPU:17, one launch (start us, length us, event | category | flops | bytes accessed | tf_op | source)
XLA Modules:
  0.0 174.4 jit_solution(3722331791551354895)
XLA Ops:
  0.0 2.0 %fusion.3 = (f32[5,2,256,128]{3,2,1,0:T(8,128)S(1)}, f32[5,2,256,128]{3,2,1,0:T(8,128)S(1)}) fusion(f32[8,4,256,128]{3,2,1,0:T(8,128)} %bitcast.50), kind=kLoop, calls=%fused_computation.11 | loop fusion | bytes 5242880 | tf_op jit(solution)/shard_map/slice | solution.py:289
  2.1 1.3 collective-permute-start.4
  4.8 3.2 %collective-permute-start = (f32[5,2,128,256]{3,2,1,0:T(8,128)S(1)}, f32[5,2,128,256]{3,2,1,0:T(8,128)S(1)}, u32[]{:S(2)}, u32[]{:S(2)}) collective-permute-start(f32[5,2,128,256]{3,2,1,0:T(8,128)S(1)} %slice_bitcast_fusion.refs_0_), channel_id=1, source_target_pairs={{0,1},{1,2},{2,3},{4,5},{5,6},{6,7},{8,9},{9,10},{10,11},{12,13},{... | collective-permute-start | bytes 3932168 | tf_op jit(solution)/shard_map/ppermute | solution.py:217
  8.0 2.1 %collective-permute-start.9 = (f32[5,2,128,256]{3,2,1,0:T(8,128)S(1)}, f32[5,2,128,256]{3,2,1,0:T(8,128)S(1)}, u32[]{:S(2)}, u32[]{:S(2)}) collective-permute-start(f32[5,2,128,256]{3,2,1,0:T(8,128)S(1)} %slice_bitcast_fusion.refs_0_), channel_id=1, source_target_pairs={{1,0},{2,1},{3,2},{5,4},{6,5},{7,6},{9,8},{10,9},{11,10},{13,12},{... | collective-permute-start | bytes 3932168 | tf_op jit(solution)/shard_map/ppermute | solution.py:217
  10.1 22.8 %collective-permute-done.3.refs_7_ = f32[5,2,256,128]{3,2,1,0:T(8,128)} collective-permute-done((f32[5,2,256,128]{3,2,1,0:T(8,128)S(1)}, f32[5,2,256,128]{3,2,1,0:T(8,128)}, u32[]{:S(2)}, u32[]{:S(2)}) %collective-permute-start.3) | collective-permute-done | bytes 1310752 | tf_op jit(solution)/shard_map/ppermute | solution.py:217
  34.3 1.4 collective-permute-done.refs_1_
  35.7 3.2 %collective-permute-start.1 = (f32[5,2,128,256]{3,2,1,0:T(8,128)S(1)}, f32[5,2,128,256]{3,2,1,0:T(8,128)}, u32[]{:S(2)}, u32[]{:S(2)}) collective-permute-start(f32[5,2,128,256]{3,2,1,0:T(8,128)S(1)} %collective-permute-done.refs_1_), channel_id=1, source_target_pairs={{1,2},{2,3},{5,6},{6,7},{9,10},{10,11},{13,14},{14,15},{17,18},{18... | collective-permute-start | bytes 3932168 | tf_op jit(solution)/shard_map/ppermute | solution.py:217
  38.9 4.2 %collective-permute-start.10 = (f32[5,2,128,256]{3,2,1,0:T(8,128)S(1)}, f32[5,2,128,256]{3,2,1,0:T(8,128)}, u32[]{:S(2)}, u32[]{:S(2)}) collective-permute-start(f32[5,2,128,256]{3,2,1,0:T(8,128)S(1)} %collective-permute-done.9.refs_2_), channel_id=1, source_target_pairs={{1,0},{2,1},{5,4},{6,5},{9,8},{10,9},{13,12},{14,13},{17,16},{18,1... | collective-permute-start | bytes 3932168 | tf_op jit(solution)/shard_map/ppermute | solution.py:217
  43.1 18.2 %collective-permute-done.7.refs_9_ = f32[5,2,256,128]{3,2,1,0:T(8,128)S(1)} collective-permute-done((f32[5,2,256,128]{3,2,1,0:T(8,128)S(1)}, f32[5,2,256,128]{3,2,1,0:T(8,128)S(1)}, u32[]{:S(2)}, u32[]{:S(2)}) %collective-permute-start.7) | collective-permute-done | bytes 1310752 | tf_op jit(solution)/shard_map/ppermute | solution.py:217
  62.9 2.9 %collective-permute-done.1.refs_3_ = f32[5,2,128,256]{3,2,1,0:T(8,128)} collective-permute-done((f32[5,2,128,256]{3,2,1,0:T(8,128)S(1)}, f32[5,2,128,256]{3,2,1,0:T(8,128)}, u32[]{:S(2)}, u32[]{:S(2)}) %collective-permute-start.1) | collective-permute-done | bytes 1310752 | tf_op jit(solution)/shard_map/ppermute | solution.py:217
  65.8 4.3 %collective-permute-start.2 = (f32[5,2,128,256]{3,2,1,0:T(8,128)}, f32[5,2,128,256]{3,2,1,0:T(8,128)}, u32[]{:S(2)}, u32[]{:S(2)}) collective-permute-start(f32[5,2,128,256]{3,2,1,0:T(8,128)} %collective-permute-done.1.refs_3_), channel_id=1, source_target_pairs={{2,3},{6,7},{10,11},{14,15},{18,19},{22,23},{26,27},{30,31}} | collective-permute-start | bytes 3932168 | tf_op jit(solution)/shard_map/ppermute | solution.py:217
  70.1 1.8 %collective-permute-start.14 = (f32[5,2,128,256]{3,2,1,0:T(8,128)}, f32[5,2,128,256]{3,2,1,0:T(8,128)}, u32[]{:S(2)}, u32[]{:S(2)}) collective-permute-start(f32[5,2,128,256]{3,2,1,0:T(8,128)} %collective-permute-done.10.refs_4_), channel_id=1, source_target_pairs={{1,0},{5,4},{9,8},{13,12},{17,16},{21,20},{25,24},{29,28}} | collective-permute-start | bytes 3932168 | tf_op jit(solution)/shard_map/ppermute | solution.py:217
  72.0 1.5 fusion.2
  73.6 6.9 %shard_map.73 = (bf16[3,1024,512]{2,1,0:T(8,128)(2,1)S(1)}, bf16[3,512,2048]{2,1,0:T(8,128)(2,1)S(1)}, f32[8,128]{1,0:T(8,128)S(1)}) custom-call(s32[8,8]{1,0:T(8,128)S(1)} %fusion.1.l_tgt, s32[8,16]{1,0:T(8,128)S(1)} %bitcast.38, s32[5]{0:T(128)S(1)} %bitcast.44, s32[6]{0:T(128)S(1)} %bitcast.47, f32[5,2,128,256]{3,2,1,0:T(8,128)} %copy-done.5, ...), custom_call_target="tpu_custom_call" | custom-call | tf_op jit(solution)/shard_map/pallas_call | solution.py:168
  80.5 5.6 %shard_map.74 = (bf16[2,1024,512]{2,1,0:T(8,128)(2,1)S(1)}, bf16[2,512,2048]{2,1,0:T(8,128)(2,1)S(1)}, f32[8,128]{1,0:T(8,128)S(1)}) custom-call(s32[8,8]{1,0:T(8,128)S(1)} %fusion.1.l_tgt, s32[8,16]{1,0:T(8,128)S(1)} %bitcast.39, s32[5]{0:T(128)S(1)} %bitcast.45, s32[6]{0:T(128)S(1)} %bitcast.48, f32[5,2,128,256]{3,2,1,0:T(8,128)} %copy-done.5, ...), custom_call_target="tpu_custom_call" | custom-call | tf_op jit(solution)/shard_map/pallas_call | solution.py:168
  86.2 3.1 %collective-permute-done.8.refs_3_ = f32[5,2,256,128]{3,2,1,0:T(8,128)} collective-permute-done((f32[5,2,256,128]{3,2,1,0:T(8,128)}, f32[5,2,256,128]{3,2,1,0:T(8,128)}, u32[]{:S(2)}, u32[]{:S(2)}) %collective-permute-start.8) | collective-permute-done | bytes 1310752 | tf_op jit(solution)/shard_map/ppermute | solution.py:217
  92.0 2.3 %collective-permute-done.2.refs_0_ = f32[5,2,128,256]{3,2,1,0:T(8,128)} collective-permute-done((f32[5,2,128,256]{3,2,1,0:T(8,128)}, f32[5,2,128,256]{3,2,1,0:T(8,128)}, u32[]{:S(2)}, u32[]{:S(2)}) %collective-permute-start.2) | collective-permute-done | bytes 1310752 | tf_op jit(solution)/shard_map/ppermute | solution.py:217
  94.3 4.1 %collective-permute-start.11 = (f32[3,2,128,256]{3,2,1,0:T(8,128)S(1)}, f32[3,2,128,256]{3,2,1,0:T(8,128)S(1)}, u32[]{:S(2)}, u32[]{:S(2)}) collective-permute-start(f32[3,2,128,256]{3,2,1,0:T(8,128)S(1)} %slice_bitcast_fusion.1.refs_0_), channel_id=1, source_target_pairs={{0,1},{1,2},{2,3},{4,5},{5,6},{6,7},{8,9},{9,10},{10,11},{12,13},{... | collective-permute-start | bytes 2359304 | tf_op jit(solution)/shard_map/ppermute | solution.py:217
  98.4 1.9 %collective-permute-start.18 = (f32[3,2,128,256]{3,2,1,0:T(8,128)S(1)}, f32[3,2,128,256]{3,2,1,0:T(8,128)S(1)}, u32[]{:S(2)}, u32[]{:S(2)}) collective-permute-start(f32[3,2,128,256]{3,2,1,0:T(8,128)S(1)} %slice_bitcast_fusion.1.refs_0_), channel_id=1, source_target_pairs={{1,0},{2,1},{3,2},{5,4},{6,5},{7,6},{9,8},{10,9},{11,10},{13,12},{... | collective-permute-start | bytes 2359304 | tf_op jit(solution)/shard_map/ppermute | solution.py:217
  100.5 14.3 %shard_map.75 = (bf16[3,1024,512]{2,1,0:T(8,128)(2,1)S(1)}, bf16[3,512,2048]{2,1,0:T(8,128)(2,1)S(1)}, f32[512,2048]{1,0:T(8,128)S(1)}, f32[512,2048]{1,0:T(8,128)S(1)}, f32[8,128]{1,0:T(8,128)S(1)}) custom-call(s32[8,8]{1,0:T(8,128)S(1)} %fusion.1.l_tgt, s32[8,16]{1,0:T(8,128)S(1)} %bitcast.40, ...), custom_call_target="tpu_custom_call", output_to_operand_aliasing={{0}: (10, {}), {1}: (11, {})} | custom-call | tf_op jit(solution)/shard_map/pallas_call | solution.py:168
  115.7 4.5 %collective-permute-start.15 = (f32[3,2,128,256]{3,2,1,0:T(8,128)S(1)}, f32[3,2,128,256]{3,2,1,0:T(8,128)S(1)}, u32[]{:S(2)}, u32[]{:S(2)}) collective-permute-start(f32[3,2,128,256]{3,2,1,0:T(8,128)S(1)} %collective-permute-done.11.refs_1_), channel_id=1, source_target_pairs={{1,2},{2,3},{5,6},{6,7},{9,10},{10,11},{13,14},{14,15},{17,18},{18... | collective-permute-start | bytes 2359304 | tf_op jit(solution)/shard_map/ppermute | solution.py:217
  120.3 1.5 collective-permute-start.20
  121.8 9.8 %shard_map.76 = (bf16[2,1024,512]{2,1,0:T(8,128)(2,1)S(1)}, bf16[2,512,2048]{2,1,0:T(8,128)(2,1)S(1)}, f32[512,2048]{1,0:T(8,128)S(1)}, f32[512,2048]{1,0:T(8,128)S(1)}, f32[8,128]{1,0:T(8,128)S(1)}) custom-call(s32[8,8]{1,0:T(8,128)S(1)} %fusion.1.l_tgt, ...), custom_call_target="tpu_custom_call", output_to_operand_aliasing={{0}: (10, {}), {1}: (11, {}), {2}: (12, {}), {3}: (13, {})} | custom-call | tf_op jit(solution)/shard_map/pallas_call | solution.py:168
  132.2 1.3 collective-permute-done.20.refs_4_
  134.3 2.8 %collective-permute-start.19 = (f32[3,2,128,256]{3,2,1,0:T(8,128)S(1)}, f32[3,2,128,256]{3,2,1,0:T(8,128)S(1)}, u32[]{:S(2)}, u32[]{:S(2)}) collective-permute-start(f32[3,2,128,256]{3,2,1,0:T(8,128)S(1)} %collective-permute-done.15.refs_3_), channel_id=1, source_target_pairs={{2,3},{6,7},{10,11},{14,15},{18,19},{22,23},{26,27},{30,31}} | collective-permute-start | bytes 2359304 | tf_op jit(solution)/shard_map/ppermute | solution.py:217
  138.6 6.8 %shard_map.77 = (bf16[3,1024,512]{2,1,0:T(8,128)(2,1)S(1)}, bf16[3,512,2048]{2,1,0:T(8,128)(2,1)S(1)}, f32[8,128]{1,0:T(8,128)S(1)}) custom-call(s32[8,8]{1,0:T(8,128)S(1)} %fusion.1.l_tgt, s32[8,16]{1,0:T(8,128)S(1)} %bitcast.42, s32[5]{0:T(128)S(1)} %bitcast.46, s32[6]{0:T(128)S(1)} %bitcast.49, f32[3,2,128,256]{3,2,1,0:T(8,128)} %copy-done.10, ...), custom_call_target="tpu_custom_call" | custom-call | tf_op jit(solution)/shard_map/pallas_call | solution.py:168
  145.4 2.8 %collective-permute-done.19.refs_0_ = f32[3,2,128,256]{3,2,1,0:T(8,128)S(1)} collective-permute-done((f32[3,2,128,256]{3,2,1,0:T(8,128)S(1)}, f32[3,2,128,256]{3,2,1,0:T(8,128)S(1)}, u32[]{:S(2)}, u32[]{:S(2)}) %collective-permute-start.19) | collective-permute-done | bytes 786464 | tf_op jit(solution)/shard_map/ppermute | solution.py:217
  148.2 1.9 %collective-permute-done.22.refs_2_ = f32[3,2,256,128]{3,2,1,0:T(8,128)S(1)} collective-permute-done((f32[3,2,256,128]{3,2,1,0:T(8,128)S(1)}, f32[3,2,256,128]{3,2,1,0:T(8,128)S(1)}, u32[]{:S(2)}, u32[]{:S(2)}) %collective-permute-start.22) | collective-permute-done | bytes 786464 | tf_op jit(solution)/shard_map/ppermute | solution.py:217
  150.3 7.0 %shard_map.78 = (bf16[3,1024,512]{2,1,0:T(8,128)(2,1)S(1)}, bf16[3,512,2048]{2,1,0:T(8,128)(2,1)S(1)}, f32[512,2048]{1,0:T(8,128)S(1)}, f32[8,128]{1,0:T(8,128)S(1)}) custom-call(s32[8,8]{1,0:T(8,128)S(1)} %fusion.1.l_tgt, s32[8,16]{1,0:T(8,128)S(1)} %bitcast.43, s32[2]{0:T(128)S(1)} %slice.44.l_base, ...), custom_call_target="tpu_custom_call", output_to_operand_aliasing={{0}: (10, {}), {1}: (11, {}), {2}: (12, {})} | custom-call | tf_op jit(solution)/shard_map/pallas_call | solution.py:168
  157.3 7.6 %collective-permute-start.24 = (f32[512,2048]{1,0:T(8,128)S(1)}, f32[512,2048]{1,0:T(8,128)S(1)}, u32[]{:S(2)}, u32[]{:S(2)}) collective-permute-start(f32[512,2048]{1,0:T(8,128)S(1)} %get-tuple-element.146), channel_id=1, source_target_pairs={{0,16},{16,0},{1,17},{17,1},{2,18},{18,2},{3,19},{19,3},{4,20},{20... | collective-permute-start | bytes 12582920 | tf_op jit(solution)/shard_map/ppermute | solution.py:369
  164.8 5.9 %shard_map.79 = f32[512,2048]{1,0:T(8,128)S(1)} custom-call(bf16[3,1024,512]{2,1,0:T(8,128)(2,1)S(1)} %get-tuple-element.142.l_cats, bf16[3,512,2048]{2,1,0:T(8,128)(2,1)S(1)} %get-tuple-element.143.u_cats, f32[8,128]{1,0:T(8,128)S(1)} %get-tuple-element.144._, f32[512,2048]{1,0:T(8,128)S(1)} %get-tuple-element.145.keep_in), custom_call_target="tpu_custom_call", output_to_operand_aliasing={{}: (3, {})} | custom-call | tf_op jit(solution)/shard_map/pallas_call | solution.py:353
  171.6 2.8 %subtract_bitcast_fusion = f32[1,512,2048]{2,1,0:T(8,128)} fusion(f32[512,2048]{1,0:T(8,128)S(1)} %shard_map.79, f32[512,2048]{1,0:T(8,128)S(1)} %collective-permute-done.24), kind=kLoop, calls=%fused_computation | loop fusion | flops 1048576 | bytes 12582912 | tf_op jit(solution)/shard_map/broadcast_in_dim | solution.py:370
  (86 shorter events, 12.1 us)
Async XLA Ops:
  0.0 72.0 %copy-start.23 = (s32[8]{0:T(128)S(1)}, s32[8]{0:T(128)}, u32[]{:S(2)}) copy-start(s32[8]{0:T(128)} %constant.60) | copy-start | bytes 100
  0.0 72.0 %copy-start.22 = (s32[1,8,1,8]{3,2,1,0:T(1,128)S(1)}, s32[1,8,1,8]{3,2,1,0:T(1,128)}, u32[]{:S(2)}) copy-start(s32[1,8,1,8]{3,2,1,0:T(1,128)} %param.8) | copy-start | bytes 772
  2.0 60.5 %copy-start.4 = (f32[5,2,256,128]{3,2,1,0:T(8,128)}, f32[5,2,256,128]{3,2,1,0:T(8,128)S(1)}, u32[]{:S(2)}) copy-start(f32[5,2,256,128]{3,2,1,0:T(8,128)S(1)} %get-tuple-element.82.refs_6_) | copy-start | bytes 3932164
  2.1 71.5 %copy-start.3 = (f32[5,2,256,128]{3,2,1,0:T(8,128)}, f32[5,2,256,128]{3,2,1,0:T(8,128)S(1)}, u32[]{:S(2)}) copy-start(f32[5,2,256,128]{3,2,1,0:T(8,128)S(1)} %get-tuple-element.79.refs_5_) | copy-start | bytes 3932164
  2.1 71.5 %copy-start = (f32[1,8,256,256]{3,2,1,0:T(8,128)S(1)}, f32[1,8,256,256]{3,2,1,0:T(8,128)}, u32[]{:S(2)}) copy-start(f32[1,8,256,256]{3,2,1,0:T(8,128)} %param.11) | copy-start | bytes 6291460
  2.1 71.5 %copy-start.2 = (s32[1,8,1,16]{3,2,1,0:T(1,128)S(1)}, s32[1,8,1,16]{3,2,1,0:T(1,128)}, u32[]{:S(2)}) copy-start(s32[1,8,1,16]{3,2,1,0:T(1,128)} %param.10) | copy-start | bytes 1540
  2.1 32.0 %collective-permute-start.4 = (f32[5,2,256,128]{3,2,1,0:T(8,128)S(1)}, f32[5,2,256,128]{3,2,1,0:T(8,128)}, u32[]{:S(2)}, u32[]{:S(2)}) collective-permute-start(f32[5,2,256,128]{3,2,1,0:T(8,128)S(1)} %get-tuple-element.82.refs_6_), channel_id=1, source_target_pairs={{0,8},{4,12},{8,0},{12,4},{1,9},{5,13},{9,1},{13,5},{2,10},{6,14},... | collective-permute-start | bytes 3932168 | tf_op jit(solution)/shard_map/ppermute | solution.py:217
  3.4 29.4 %collective-permute-start.3 = (f32[5,2,256,128]{3,2,1,0:T(8,128)S(1)}, f32[5,2,256,128]{3,2,1,0:T(8,128)}, u32[]{:S(2)}, u32[]{:S(2)}) collective-permute-start(f32[5,2,256,128]{3,2,1,0:T(8,128)S(1)} %get-tuple-element.79.refs_5_), channel_id=1, source_target_pairs={{0,4},{4,0},{8,12},{12,8},{1,5},{5,1},{9,13},{13,9},{2,6},{6,2},{1... | collective-permute-start | bytes 3932168 | tf_op jit(solution)/shard_map/ppermute | solution.py:217
  4.7 58.1 %copy-start.5 = (f32[5,2,128,256]{3,2,1,0:T(8,128)}, f32[5,2,128,256]{3,2,1,0:T(8,128)S(1)}, u32[]{:S(2)}) copy-start(f32[5,2,128,256]{3,2,1,0:T(8,128)S(1)} %slice_bitcast_fusion.refs_0_) | copy-start | bytes 3932164
  4.8 30.9 %collective-permute-start = (f32[5,2,128,256]{3,2,1,0:T(8,128)S(1)}, f32[5,2,128,256]{3,2,1,0:T(8,128)S(1)}, u32[]{:S(2)}, u32[]{:S(2)}) collective-permute-start(f32[5,2,128,256]{3,2,1,0:T(8,128)S(1)} %slice_bitcast_fusion.refs_0_), channel_id=1, source_target_pairs={{0,1},{1,2},{2,3},{4,5},{5,6},{6,7},{8,9},{9,10},{10,11},{12,13},{... | collective-permute-start | bytes 3932168 | tf_op jit(solution)/shard_map/ppermute | solution.py:217
  8.0 30.9 %collective-permute-start.9 = (f32[5,2,128,256]{3,2,1,0:T(8,128)S(1)}, f32[5,2,128,256]{3,2,1,0:T(8,128)S(1)}, u32[]{:S(2)}, u32[]{:S(2)}) collective-permute-start(f32[5,2,128,256]{3,2,1,0:T(8,128)S(1)} %slice_bitcast_fusion.refs_0_), channel_id=1, source_target_pairs={{1,0},{2,1},{3,2},{5,4},{6,5},{7,6},{9,8},{10,9},{11,10},{13,12},{... | collective-permute-start | bytes 3932168 | tf_op jit(solution)/shard_map/ppermute | solution.py:217
  32.8 28.5 %collective-permute-start.7 = (f32[5,2,256,128]{3,2,1,0:T(8,128)S(1)}, f32[5,2,256,128]{3,2,1,0:T(8,128)S(1)}, u32[]{:S(2)}, u32[]{:S(2)}) collective-permute-start(f32[5,2,256,128]{3,2,1,0:T(8,128)S(1)} %get-tuple-element.82.refs_6_), channel_id=1, source_target_pairs={{0,4},{4,0},{8,12},{12,8},{1,5},{5,1},{9,13},{13,9},{2,6},{6,2},{1... | collective-permute-start | bytes 3932168 | tf_op jit(solution)/shard_map/ppermute | solution.py:217
  34.0 28.5 %collective-permute-start.5 = (f32[5,2,256,128]{3,2,1,0:T(8,128)S(1)}, f32[5,2,256,128]{3,2,1,0:T(8,128)S(1)}, u32[]{:S(2)}, u32[]{:S(2)}) collective-permute-start(f32[5,2,256,128]{3,2,1,0:T(8,128)S(1)} %get-tuple-element.79.refs_5_), channel_id=1, source_target_pairs={{0,8},{4,12},{8,0},{12,4},{1,9},{5,13},{9,1},{13,5},{2,10},{6,14},... | collective-permute-start | bytes 3932168 | tf_op jit(solution)/shard_map/ppermute | solution.py:217
  35.7 30.1 %collective-permute-start.1 = (f32[5,2,128,256]{3,2,1,0:T(8,128)S(1)}, f32[5,2,128,256]{3,2,1,0:T(8,128)}, u32[]{:S(2)}, u32[]{:S(2)}) collective-permute-start(f32[5,2,128,256]{3,2,1,0:T(8,128)S(1)} %collective-permute-done.refs_1_), channel_id=1, source_target_pairs={{1,2},{2,3},{5,6},{6,7},{9,10},{10,11},{13,14},{14,15},{17,18},{18... | collective-permute-start | bytes 3932168 | tf_op jit(solution)/shard_map/ppermute | solution.py:217
  38.9 31.2 %collective-permute-start.10 = (f32[5,2,128,256]{3,2,1,0:T(8,128)S(1)}, f32[5,2,128,256]{3,2,1,0:T(8,128)}, u32[]{:S(2)}, u32[]{:S(2)}) collective-permute-start(f32[5,2,128,256]{3,2,1,0:T(8,128)S(1)} %collective-permute-done.9.refs_2_), channel_id=1, source_target_pairs={{1,0},{2,1},{5,4},{6,5},{9,8},{10,9},{13,12},{14,13},{17,16},{18,1... | collective-permute-start | bytes 3932168 | tf_op jit(solution)/shard_map/ppermute | solution.py:217
  61.3 27.9 %collective-permute-start.8 = (f32[5,2,256,128]{3,2,1,0:T(8,128)}, f32[5,2,256,128]{3,2,1,0:T(8,128)}, u32[]{:S(2)}, u32[]{:S(2)}) collective-permute-start(f32[5,2,256,128]{3,2,1,0:T(8,128)} %collective-permute-done.4.refs_8_), channel_id=1, source_target_pairs={{0,4},{4,0},{8,12},{12,8},{1,5},{5,1},{9,13},{13,9},{2,6},{6,2},{1... | collective-permute-start | bytes 3932168 | tf_op jit(solution)/shard_map/ppermute | solution.py:217
  62.6 27.7 %collective-permute-start.6 = (f32[5,2,256,128]{3,2,1,0:T(8,128)}, f32[5,2,256,128]{3,2,1,0:T(8,128)}, u32[]{:S(2)}, u32[]{:S(2)}) collective-permute-start(f32[5,2,256,128]{3,2,1,0:T(8,128)} %collective-permute-done.3.refs_7_), channel_id=1, source_target_pairs={{0,8},{4,12},{8,0},{12,4},{1,9},{5,13},{9,1},{13,5},{2,10},{6,14},... | collective-permute-start | bytes 3932168 | tf_op jit(solution)/shard_map/ppermute | solution.py:217
  65.8 28.5 %collective-permute-start.2 = (f32[5,2,128,256]{3,2,1,0:T(8,128)}, f32[5,2,128,256]{3,2,1,0:T(8,128)}, u32[]{:S(2)}, u32[]{:S(2)}) collective-permute-start(f32[5,2,128,256]{3,2,1,0:T(8,128)} %collective-permute-done.1.refs_3_), channel_id=1, source_target_pairs={{2,3},{6,7},{10,11},{14,15},{18,19},{22,23},{26,27},{30,31}} | collective-permute-start | bytes 3932168 | tf_op jit(solution)/shard_map/ppermute | solution.py:217
  70.1 28.3 %collective-permute-start.14 = (f32[5,2,128,256]{3,2,1,0:T(8,128)}, f32[5,2,128,256]{3,2,1,0:T(8,128)}, u32[]{:S(2)}, u32[]{:S(2)}) collective-permute-start(f32[5,2,128,256]{3,2,1,0:T(8,128)} %collective-permute-done.10.refs_4_), channel_id=1, source_target_pairs={{1,0},{5,4},{9,8},{13,12},{17,16},{21,20},{25,24},{29,28}} | collective-permute-start | bytes 3932168 | tf_op jit(solution)/shard_map/ppermute | solution.py:217
  90.2 24.6 %collective-permute-start.13 = (f32[3,2,256,128]{3,2,1,0:T(8,128)S(1)}, f32[3,2,256,128]{3,2,1,0:T(8,128)S(1)}, u32[]{:S(2)}, u32[]{:S(2)}) collective-permute-start(f32[3,2,256,128]{3,2,1,0:T(8,128)S(1)} %get-tuple-element.112.refs_5_), channel_id=1, source_target_pairs={{0,4},{4,0},{8,12},{12,8},{1,5},{5,1},{9,13},{13,9},{2,6},{6,2},{1... | collective-permute-start | bytes 2359304 | tf_op jit(solution)/shard_map/ppermute | solution.py:217
  90.5 24.3 %collective-permute-start.12 = (f32[3,2,256,128]{3,2,1,0:T(8,128)S(1)}, f32[3,2,256,128]{3,2,1,0:T(8,128)S(1)}, u32[]{:S(2)}, u32[]{:S(2)}) collective-permute-start(f32[3,2,256,128]{3,2,1,0:T(8,128)S(1)} %get-tuple-element.114.refs_6_), channel_id=1, source_target_pairs={{0,8},{4,12},{8,0},{12,4},{1,9},{5,13},{9,1},{13,5},{2,10},{6,14},... | collective-permute-start | bytes 2359304 | tf_op jit(solution)/shard_map/ppermute | solution.py:217
  94.3 21.5 %collective-permute-start.11 = (f32[3,2,128,256]{3,2,1,0:T(8,128)S(1)}, f32[3,2,128,256]{3,2,1,0:T(8,128)S(1)}, u32[]{:S(2)}, u32[]{:S(2)}) collective-permute-start(f32[3,2,128,256]{3,2,1,0:T(8,128)S(1)} %slice_bitcast_fusion.1.refs_0_), channel_id=1, source_target_pairs={{0,1},{1,2},{2,3},{4,5},{5,6},{6,7},{8,9},{9,10},{10,11},{12,13},{... | collective-permute-start | bytes 2359304 | tf_op jit(solution)/shard_map/ppermute | solution.py:217
  98.4 21.9 %collective-permute-start.18 = (f32[3,2,128,256]{3,2,1,0:T(8,128)S(1)}, f32[3,2,128,256]{3,2,1,0:T(8,128)S(1)}, u32[]{:S(2)}, u32[]{:S(2)}) collective-permute-start(f32[3,2,128,256]{3,2,1,0:T(8,128)S(1)} %slice_bitcast_fusion.1.refs_0_), channel_id=1, source_target_pairs={{1,0},{2,1},{3,2},{5,4},{6,5},{7,6},{9,8},{10,9},{11,10},{13,12},{... | collective-permute-start | bytes 2359304 | tf_op jit(solution)/shard_map/ppermute | solution.py:217
  114.9 16.7 %collective-permute-start.17 = (f32[3,2,256,128]{3,2,1,0:T(8,128)S(1)}, f32[3,2,256,128]{3,2,1,0:T(8,128)S(1)}, u32[]{:S(2)}, u32[]{:S(2)}) collective-permute-start(f32[3,2,256,128]{3,2,1,0:T(8,128)S(1)} %get-tuple-element.114.refs_6_), channel_id=1, source_target_pairs={{0,4},{4,0},{8,12},{12,8},{1,5},{5,1},{9,13},{13,9},{2,6},{6,2},{1... | collective-permute-start | bytes 2359304 | tf_op jit(solution)/shard_map/ppermute | solution.py:217
  115.2 16.4 %collective-permute-start.16 = (f32[3,2,256,128]{3,2,1,0:T(8,128)S(1)}, f32[3,2,256,128]{3,2,1,0:T(8,128)S(1)}, u32[]{:S(2)}, u32[]{:S(2)}) collective-permute-start(f32[3,2,256,128]{3,2,1,0:T(8,128)S(1)} %get-tuple-element.112.refs_5_), channel_id=1, source_target_pairs={{0,8},{4,12},{8,0},{12,4},{1,9},{5,13},{9,1},{13,5},{2,10},{6,14},... | collective-permute-start | bytes 2359304 | tf_op jit(solution)/shard_map/ppermute | solution.py:217
  115.7 16.5 %collective-permute-start.15 = (f32[3,2,128,256]{3,2,1,0:T(8,128)S(1)}, f32[3,2,128,256]{3,2,1,0:T(8,128)S(1)}, u32[]{:S(2)}, u32[]{:S(2)}) collective-permute-start(f32[3,2,128,256]{3,2,1,0:T(8,128)S(1)} %collective-permute-done.11.refs_1_), channel_id=1, source_target_pairs={{1,2},{2,3},{5,6},{6,7},{9,10},{10,11},{13,14},{14,15},{17,18},{18... | collective-permute-start | bytes 2359304 | tf_op jit(solution)/shard_map/ppermute | solution.py:217
  120.3 13.2 %collective-permute-start.20 = (f32[3,2,128,256]{3,2,1,0:T(8,128)S(1)}, f32[3,2,128,256]{3,2,1,0:T(8,128)S(1)}, u32[]{:S(2)}, u32[]{:S(2)}) collective-permute-start(f32[3,2,128,256]{3,2,1,0:T(8,128)S(1)} %collective-permute-done.18.refs_2_), channel_id=1, source_target_pairs={{1,0},{2,1},{5,4},{6,5},{9,8},{10,9},{13,12},{14,13},{17,16},{18,1... | collective-permute-start | bytes 2359304 | tf_op jit(solution)/shard_map/ppermute | solution.py:217
  133.5 11.9 %collective-permute-start.21 = (f32[3,2,128,256]{3,2,1,0:T(8,128)S(1)}, f32[3,2,128,256]{3,2,1,0:T(8,128)S(1)}, u32[]{:S(2)}, u32[]{:S(2)}) collective-permute-start(f32[3,2,128,256]{3,2,1,0:T(8,128)S(1)} %collective-permute-done.20.refs_4_), channel_id=1, source_target_pairs={{1,0},{5,4},{9,8},{13,12},{17,16},{21,20},{25,24},{29,28}} | collective-permute-start | bytes 2359304 | tf_op jit(solution)/shard_map/ppermute | solution.py:217
  134.3 14.0 %collective-permute-start.19 = (f32[3,2,128,256]{3,2,1,0:T(8,128)S(1)}, f32[3,2,128,256]{3,2,1,0:T(8,128)S(1)}, u32[]{:S(2)}, u32[]{:S(2)}) collective-permute-start(f32[3,2,128,256]{3,2,1,0:T(8,128)S(1)} %collective-permute-done.15.refs_3_), channel_id=1, source_target_pairs={{2,3},{6,7},{10,11},{14,15},{18,19},{22,23},{26,27},{30,31}} | collective-permute-start | bytes 2359304 | tf_op jit(solution)/shard_map/ppermute | solution.py:217
  137.1 13.0 %collective-permute-start.22 = (f32[3,2,256,128]{3,2,1,0:T(8,128)S(1)}, f32[3,2,256,128]{3,2,1,0:T(8,128)S(1)}, u32[]{:S(2)}, u32[]{:S(2)}) collective-permute-start(f32[3,2,256,128]{3,2,1,0:T(8,128)S(1)} %collective-permute-done.13.refs_7_), channel_id=1, source_target_pairs={{0,8},{4,12},{8,0},{12,4},{1,9},{5,13},{9,1},{13,5},{2,10},{6,14},... | collective-permute-start | bytes 2359304 | tf_op jit(solution)/shard_map/ppermute | solution.py:217
  137.9 12.4 %collective-permute-start.23 = (f32[3,2,256,128]{3,2,1,0:T(8,128)S(1)}, f32[3,2,256,128]{3,2,1,0:T(8,128)S(1)}, u32[]{:S(2)}, u32[]{:S(2)}) collective-permute-start(f32[3,2,256,128]{3,2,1,0:T(8,128)S(1)} %collective-permute-done.12.refs_8_), channel_id=1, source_target_pairs={{0,4},{4,0},{8,12},{12,8},{1,5},{5,1},{9,13},{13,9},{2,6},{6,2},{1... | collective-permute-start | bytes 2359304 | tf_op jit(solution)/shard_map/ppermute | solution.py:217
  157.3 14.4 %collective-permute-start.24 = (f32[512,2048]{1,0:T(8,128)S(1)}, f32[512,2048]{1,0:T(8,128)S(1)}, u32[]{:S(2)}, u32[]{:S(2)}) collective-permute-start(f32[512,2048]{1,0:T(8,128)S(1)} %get-tuple-element.146), channel_id=1, source_target_pairs={{0,16},{16,0},{1,17},{17,1},{2,18},{18,2},{3,19},{19,3},{4,20},{20... | collective-permute-start | bytes 12582920 | tf_op jit(solution)/shard_map/ppermute | solution.py:369
  (17 other events, 307.4 us)

commit v6 on v5

--- a/solution.py
+++ b/solution.py
@@ -244,17 +244,17 @@
     def first(self):
         lx, ly, lu, ld = self.links
         self.x0, self.y1 = lx.send(self.h[0], side(1)), ly.send(self.h[1], side(2))
-        self.u1, self.d1 = lu.send(self.l, up(1)), ld.send(self.l, down(1))
+        self.d1, self.u1 = ld.send(self.l, down(1)), lu.send(self.l, up(1))
 
     def second(self):
         lx, ly, lu, ld = self.links
         self.x1, self.y0 = lx.send(self.h[1], side(1)), ly.send(self.h[0], side(2))
-        self.u2, self.d2 = lu.send(self.u1.value, up(2)), ld.send(self.d1.value, down(2))
+        self.d2, self.u2 = ld.send(self.d1.value, down(2)), lu.send(self.u1.value, up(2))
 
     def third(self, here):
         lx, ly, lu, ld = self.links
         f1, f0 = lx.send(self.y1.value[here], side(1)), ly.send(self.x0.value[here], side(2))
-        u3, d3 = lu.send(self.u2.value[here], up(3)), ld.send(self.d2.value[here], down(3))
+        d3, u3 = ld.send(self.d2.value[here], down(3)), lu.send(self.u2.value[here], up(3))
         return u3, d3, f0, f1
 
     def buffers(self, third):

time: 177 us -> 176 us (level)
  starting transfers between devices: 50.2 us -> 46 us
  waiting for transfers between devices: 59.4 us -> 62.3 us
    ppermute x24, starting transfers between devices: 42.6 us -> 37.8 us  [send(): out = Box(lax.ppermute(after(x, self.wait), self.axis, pairs))]
    ppermute x24, waiting for transfers between devices: 58.4 us -> 61.4 us  [send(): out = Box(lax.ppermute(after(x, self.wait), self.axis, pairs))]
  transfers between devices with their start and end apart: 25 -> 25, of which waited for: 13 -> 12; matrix products, arithmetic and copies ran while one was open for 2% -> 2% of each run, Pallas kernels for 28% -> 28%
where the time goes in v6:
time: 176 us; the launch traced here: 173 us
  waiting for transfers between devices  62.3 us (35%)
  Pallas kernels  56.1 us (32%)
  starting transfers between devices  46 us (26%)
  local copies, waits for them, and re-layouts  5.27 us (3%)
  other arithmetic  2.8 us (2%)
    ppermute x24, waiting for transfers between devices, send(): out = Box(lax.ppermute(after(x, self.wait), self.axis, pairs))  61.4 us
    pallas_call x6, Pallas kernels, call(): pl.pallas_call(functools.partial(kernel, len(l_bufs), len(u_bufs), start)...  50.2 us
    ppermute x24, starting transfers between devices, send(): out = Box(lax.ppermute(after(x, self.wait), self.axis, pairs))  37.8 us
    ppermute x1, starting transfers between devices, body(): other = lax.ppermute(send, 'gz', [(0, 1), (1, 0)])  8.13 us
    pallas_call x1, Pallas kernels, body(): pl.pallas_call(keep_kernel, grid=(nodes - size,), out_shape=ACC, in_specs...  5.87 us
  transfers between devices with their start and end apart: 25, of which 12 were waited for; matrix products, arithmetic and copies ran while one was open for 2% of the time, Pallas kernels for 28%

profile of v6, /device:TPU:17, one launch (start us, length us, event | category | flops | bytes accessed | tf_op | source)
XLA Modules:
  0.0 172.9 jit_solution(15062272874482304030)
XLA Ops:
  0.0 2.0 %fusion.3 = (f32[5,2,256,128]{3,2,1,0:T(8,128)S(1)}, f32[5,2,256,128]{3,2,1,0:T(8,128)S(1)}) fusion(f32[8,4,256,128]{3,2,1,0:T(8,128)} %bitcast.50), kind=kLoop, calls=%fused_computation.11 | loop fusion | bytes 5242880 | tf_op jit(solution)/shard_map/slice | solution.py:289
  2.1 1.3 collective-permute-start.7
  3.4 1.2 collective-permute-start.6
  4.8 2.1 %collective-permute-start.3 = (f32[5,2,128,256]{3,2,1,0:T(8,128)S(1)}, f32[5,2,128,256]{3,2,1,0:T(8,128)S(1)}, u32[]{:S(2)}, u32[]{:S(2)}) collective-permute-start(f32[5,2,128,256]{3,2,1,0:T(8,128)S(1)} %slice_bitcast_fusion.refs_0_), channel_id=1, source_target_pairs={{1,0},{2,1},{3,2},{5,4},{6,5},{7,6},{9,8},{10,9},{11,10},{13,12},{... | collective-permute-start | bytes 3932168 | tf_op jit(solution)/shard_map/ppermute | solution.py:217
  6.8 3.3 %collective-permute-start = (f32[5,2,128,256]{3,2,1,0:T(8,128)S(1)}, f32[5,2,128,256]{3,2,1,0:T(8,128)S(1)}, u32[]{:S(2)}, u32[]{:S(2)}) collective-permute-start(f32[5,2,128,256]{3,2,1,0:T(8,128)S(1)} %slice_bitcast_fusion.refs_0_), channel_id=1, source_target_pairs={{0,1},{1,2},{2,3},{4,5},{5,6},{6,7},{8,9},{9,10},{10,11},{12,13},{... | collective-permute-start | bytes 3932168 | tf_op jit(solution)/shard_map/ppermute | solution.py:217
  10.1 22.7 %collective-permute-done.6.refs_7_ = f32[5,2,256,128]{3,2,1,0:T(8,128)} collective-permute-done((f32[5,2,256,128]{3,2,1,0:T(8,128)S(1)}, f32[5,2,256,128]{3,2,1,0:T(8,128)}, u32[]{:S(2)}, u32[]{:S(2)}) %collective-permute-start.6) | collective-permute-done | bytes 1310752 | tf_op jit(solution)/shard_map/ppermute | solution.py:217
  34.3 1.4 collective-permute-done.3.refs_2_
  35.7 3.2 %collective-permute-start.4 = (f32[5,2,128,256]{3,2,1,0:T(8,128)S(1)}, f32[5,2,128,256]{3,2,1,0:T(8,128)}, u32[]{:S(2)}, u32[]{:S(2)}) collective-permute-start(f32[5,2,128,256]{3,2,1,0:T(8,128)S(1)} %collective-permute-done.3.refs_2_), channel_id=1, source_target_pairs={{1,0},{2,1},{5,4},{6,5},{9,8},{10,9},{13,12},{14,13},{17,16},{18,1... | collective-permute-start | bytes 3932168 | tf_op jit(solution)/shard_map/ppermute | solution.py:217
  38.9 1.9 %collective-permute-start.1 = (f32[5,2,128,256]{3,2,1,0:T(8,128)S(1)}, f32[5,2,128,256]{3,2,1,0:T(8,128)}, u32[]{:S(2)}, u32[]{:S(2)}) collective-permute-start(f32[5,2,128,256]{3,2,1,0:T(8,128)S(1)} %collective-permute-done.refs_1_), channel_id=1, source_target_pairs={{1,2},{2,3},{5,6},{6,7},{9,10},{10,11},{13,14},{14,15},{17,18},{18... | collective-permute-start | bytes 3932168 | tf_op jit(solution)/shard_map/ppermute | solution.py:217
  40.8 20.5 %collective-permute-done.10.refs_9_ = f32[5,2,256,128]{3,2,1,0:T(8,128)S(1)} collective-permute-done((f32[5,2,256,128]{3,2,1,0:T(8,128)S(1)}, f32[5,2,256,128]{3,2,1,0:T(8,128)S(1)}, u32[]{:S(2)}, u32[]{:S(2)}) %collective-permute-start.10) | collective-permute-done | bytes 1310752 | tf_op jit(solution)/shard_map/ppermute | solution.py:217
  63.7 1.7 %collective-permute-start.5 = (f32[5,2,128,256]{3,2,1,0:T(8,128)}, f32[5,2,128,256]{3,2,1,0:T(8,128)}, u32[]{:S(2)}, u32[]{:S(2)}) collective-permute-start(f32[5,2,128,256]{3,2,1,0:T(8,128)} %collective-permute-done.4.refs_4_), channel_id=1, source_target_pairs={{1,0},{5,4},{9,8},{13,12},{17,16},{21,20},{25,24},{29,28}} | collective-permute-start | bytes 3932168 | tf_op jit(solution)/shard_map/ppermute | solution.py:217
  65.4 3.3 %collective-permute-done.1.refs_3_ = f32[5,2,128,256]{3,2,1,0:T(8,128)} collective-permute-done((f32[5,2,128,256]{3,2,1,0:T(8,128)S(1)}, f32[5,2,128,256]{3,2,1,0:T(8,128)}, u32[]{:S(2)}, u32[]{:S(2)}) %collective-permute-start.1) | collective-permute-done | bytes 1310752 | tf_op jit(solution)/shard_map/ppermute | solution.py:217
  68.7 3.0 %collective-permute-start.2 = (f32[5,2,128,256]{3,2,1,0:T(8,128)}, f32[5,2,128,256]{3,2,1,0:T(8,128)}, u32[]{:S(2)}, u32[]{:S(2)}) collective-permute-start(f32[5,2,128,256]{3,2,1,0:T(8,128)} %collective-permute-done.1.refs_3_), channel_id=1, source_target_pairs={{2,3},{6,7},{10,11},{14,15},{18,19},{22,23},{26,27},{30,31}} | collective-permute-start | bytes 3932168 | tf_op jit(solution)/shard_map/ppermute | solution.py:217
  71.9 1.5 fusion.2
  73.5 6.7 %shard_map.73 = (bf16[3,1024,512]{2,1,0:T(8,128)(2,1)S(1)}, bf16[3,512,2048]{2,1,0:T(8,128)(2,1)S(1)}, f32[8,128]{1,0:T(8,128)S(1)}) custom-call(s32[8,8]{1,0:T(8,128)S(1)} %fusion.1.l_tgt, s32[8,16]{1,0:T(8,128)S(1)} %bitcast.38, s32[5]{0:T(128)S(1)} %bitcast.44, s32[6]{0:T(128)S(1)} %bitcast.47, f32[5,2,128,256]{3,2,1,0:T(8,128)} %copy-done.5, ...), custom_call_target="tpu_custom_call" | custom-call | tf_op jit(solution)/shard_map/pallas_call | solution.py:168
  80.2 5.5 %shard_map.74 = (bf16[2,1024,512]{2,1,0:T(8,128)(2,1)S(1)}, bf16[2,512,2048]{2,1,0:T(8,128)(2,1)S(1)}, f32[8,128]{1,0:T(8,128)S(1)}) custom-call(s32[8,8]{1,0:T(8,128)S(1)} %fusion.1.l_tgt, s32[8,16]{1,0:T(8,128)S(1)} %bitcast.39, s32[5]{0:T(128)S(1)} %bitcast.45, s32[6]{0:T(128)S(1)} %bitcast.48, f32[5,2,128,256]{3,2,1,0:T(8,128)} %copy-done.5, ...), custom_call_target="tpu_custom_call" | custom-call | tf_op jit(solution)/shard_map/pallas_call | solution.py:168
  85.7 3.5 %collective-permute-done.11.refs_3_ = f32[5,2,256,128]{3,2,1,0:T(8,128)} collective-permute-done((f32[5,2,256,128]{3,2,1,0:T(8,128)}, f32[5,2,256,128]{3,2,1,0:T(8,128)}, u32[]{:S(2)}, u32[]{:S(2)}) %collective-permute-start.11) | collective-permute-done | bytes 1310752 | tf_op jit(solution)/shard_map/ppermute | solution.py:217
  92.0 3.2 %collective-permute-start.13 = (f32[3,2,128,256]{3,2,1,0:T(8,128)S(1)}, f32[3,2,128,256]{3,2,1,0:T(8,128)S(1)}, u32[]{:S(2)}, u32[]{:S(2)}) collective-permute-start(f32[3,2,128,256]{3,2,1,0:T(8,128)S(1)} %slice_bitcast_fusion.1.refs_0_), channel_id=1, source_target_pairs={{1,0},{2,1},{3,2},{5,4},{6,5},{7,6},{9,8},{10,9},{11,10},{13,12},{... | collective-permute-start | bytes 2359304 | tf_op jit(solution)/shard_map/ppermute | solution.py:217
  95.7 4.1 %collective-permute-start.12 = (f32[3,2,128,256]{3,2,1,0:T(8,128)S(1)}, f32[3,2,128,256]{3,2,1,0:T(8,128)S(1)}, u32[]{:S(2)}, u32[]{:S(2)}) collective-permute-start(f32[3,2,128,256]{3,2,1,0:T(8,128)S(1)} %slice_bitcast_fusion.1.refs_0_), channel_id=1, source_target_pairs={{0,1},{1,2},{2,3},{4,5},{5,6},{6,7},{8,9},{9,10},{10,11},{12,13},{... | collective-permute-start | bytes 2359304 | tf_op jit(solution)/shard_map/ppermute | solution.py:217
  99.9 14.3 %shard_map.75 = (bf16[3,1024,512]{2,1,0:T(8,128)(2,1)S(1)}, bf16[3,512,2048]{2,1,0:T(8,128)(2,1)S(1)}, f32[512,2048]{1,0:T(8,128)S(1)}, f32[512,2048]{1,0:T(8,128)S(1)}, f32[8,128]{1,0:T(8,128)S(1)}) custom-call(s32[8,8]{1,0:T(8,128)S(1)} %fusion.1.l_tgt, s32[8,16]{1,0:T(8,128)S(1)} %bitcast.40, ...), custom_call_target="tpu_custom_call", output_to_operand_aliasing={{0}: (10, {}), {1}: (11, {})} | custom-call | tf_op jit(solution)/shard_map/pallas_call | solution.py:168
  115.1 2.4 %collective-permute-start.17 = (f32[3,2,128,256]{3,2,1,0:T(8,128)S(1)}, f32[3,2,128,256]{3,2,1,0:T(8,128)S(1)}, u32[]{:S(2)}, u32[]{:S(2)}) collective-permute-start(f32[3,2,128,256]{3,2,1,0:T(8,128)S(1)} %collective-permute-done.13.refs_2_), channel_id=1, source_target_pairs={{1,0},{2,1},{5,4},{6,5},{9,8},{10,9},{13,12},{14,13},{17,16},{18,1... | collective-permute-start | bytes 2359304 | tf_op jit(solution)/shard_map/ppermute | solution.py:217
  117.5 2.1 %collective-permute-start.16 = (f32[3,2,128,256]{3,2,1,0:T(8,128)S(1)}, f32[3,2,128,256]{3,2,1,0:T(8,128)S(1)}, u32[]{:S(2)}, u32[]{:S(2)}) collective-permute-start(f32[3,2,128,256]{3,2,1,0:T(8,128)S(1)} %collective-permute-done.12.refs_1_), channel_id=1, source_target_pairs={{1,2},{2,3},{5,6},{6,7},{9,10},{10,11},{13,14},{14,15},{17,18},{18... | collective-permute-start | bytes 2359304 | tf_op jit(solution)/shard_map/ppermute | solution.py:217
  119.6 9.8 %shard_map.76 = (bf16[2,1024,512]{2,1,0:T(8,128)(2,1)S(1)}, bf16[2,512,2048]{2,1,0:T(8,128)(2,1)S(1)}, f32[512,2048]{1,0:T(8,128)S(1)}, f32[512,2048]{1,0:T(8,128)S(1)}, f32[8,128]{1,0:T(8,128)S(1)}) custom-call(s32[8,8]{1,0:T(8,128)S(1)} %fusion.1.l_tgt, ...), custom_call_target="tpu_custom_call", output_to_operand_aliasing={{0}: (10, {}), {1}: (11, {}), {2}: (12, {}), {3}: (13, {})} | custom-call | tf_op jit(solution)/shard_map/pallas_call | solution.py:168
  129.4 4.3 %collective-permute-done.16.refs_3_ = f32[3,2,128,256]{3,2,1,0:T(8,128)S(1)} collective-permute-done((f32[3,2,128,256]{3,2,1,0:T(8,128)S(1)}, f32[3,2,128,256]{3,2,1,0:T(8,128)S(1)}, u32[]{:S(2)}, u32[]{:S(2)}) %collective-permute-start.16) | collective-permute-done | bytes 786464 | tf_op jit(solution)/shard_map/ppermute | solution.py:217
  133.7 1.7 collective-permute-start.20
  136.4 1.4 collective-permute-start.23
  137.8 7.0 %shard_map.77 = (bf16[3,1024,512]{2,1,0:T(8,128)(2,1)S(1)}, bf16[3,512,2048]{2,1,0:T(8,128)(2,1)S(1)}, f32[8,128]{1,0:T(8,128)S(1)}) custom-call(s32[8,8]{1,0:T(8,128)S(1)} %fusion.1.l_tgt, s32[8,16]{1,0:T(8,128)S(1)} %bitcast.42, s32[5]{0:T(128)S(1)} %bitcast.46, s32[6]{0:T(128)S(1)} %bitcast.49, f32[3,2,128,256]{3,2,1,0:T(8,128)} %copy-done.10, ...), custom_call_target="tpu_custom_call" | custom-call | tf_op jit(solution)/shard_map/pallas_call | solution.py:168
  144.8 2.4 %collective-permute-done.20.refs_0_ = f32[3,2,128,256]{3,2,1,0:T(8,128)S(1)} collective-permute-done((f32[3,2,128,256]{3,2,1,0:T(8,128)S(1)}, f32[3,2,128,256]{3,2,1,0:T(8,128)S(1)}, u32[]{:S(2)}, u32[]{:S(2)}) %collective-permute-start.20) | collective-permute-done | bytes 786464 | tf_op jit(solution)/shard_map/ppermute | solution.py:217
  148.3 7.0 %shard_map.78 = (bf16[3,1024,512]{2,1,0:T(8,128)(2,1)S(1)}, bf16[3,512,2048]{2,1,0:T(8,128)(2,1)S(1)}, f32[512,2048]{1,0:T(8,128)S(1)}, f32[8,128]{1,0:T(8,128)S(1)}) custom-call(s32[8,8]{1,0:T(8,128)S(1)} %fusion.1.l_tgt, s32[8,16]{1,0:T(8,128)S(1)} %bitcast.43, s32[2]{0:T(128)S(1)} %slice.44.l_base, ...), custom_call_target="tpu_custom_call", output_to_operand_aliasing={{0}: (10, {}), {1}: (11, {}), {2}: (12, {})} | custom-call | tf_op jit(solution)/shard_map/pallas_call | solution.py:168
  155.2 8.1 %collective-permute-start.24 = (f32[512,2048]{1,0:T(8,128)S(1)}, f32[512,2048]{1,0:T(8,128)S(1)}, u32[]{:S(2)}, u32[]{:S(2)}) collective-permute-start(f32[512,2048]{1,0:T(8,128)S(1)} %get-tuple-element.146), channel_id=1, source_target_pairs={{0,16},{16,0},{1,17},{17,1},{2,18},{18,2},{3,19},{19,3},{4,20},{20... | collective-permute-start | bytes 12582920 | tf_op jit(solution)/shard_map/ppermute | solution.py:369
  163.4 5.9 %shard_map.79 = f32[512,2048]{1,0:T(8,128)S(1)} custom-call(bf16[3,1024,512]{2,1,0:T(8,128)(2,1)S(1)} %get-tuple-element.142.l_cats, bf16[3,512,2048]{2,1,0:T(8,128)(2,1)S(1)} %get-tuple-element.143.u_cats, f32[8,128]{1,0:T(8,128)S(1)} %get-tuple-element.144._, f32[512,2048]{1,0:T(8,128)S(1)} %get-tuple-element.145.keep_in), custom_call_target="tpu_custom_call", output_to_operand_aliasing={{}: (3, {})} | custom-call | tf_op jit(solution)/shard_map/pallas_call | solution.py:353
  170.1 2.8 %subtract_bitcast_fusion = f32[1,512,2048]{2,1,0:T(8,128)} fusion(f32[512,2048]{1,0:T(8,128)S(1)} %shard_map.79, f32[512,2048]{1,0:T(8,128)S(1)} %collective-permute-done.24), kind=kLoop, calls=%fused_computation | loop fusion | flops 1048576 | bytes 12582912 | tf_op jit(solution)/shard_map/broadcast_in_dim | solution.py:370
  (86 shorter events, 11.2 us)
Async XLA Ops:
  0.0 71.9 %copy-start.23 = (s32[8]{0:T(128)S(1)}, s32[8]{0:T(128)}, u32[]{:S(2)}) copy-start(s32[8]{0:T(128)} %constant.60) | copy-start | bytes 100
  0.0 71.9 %copy-start.22 = (s32[1,8,1,8]{3,2,1,0:T(1,128)S(1)}, s32[1,8,1,8]{3,2,1,0:T(1,128)}, u32[]{:S(2)}) copy-start(s32[1,8,1,8]{3,2,1,0:T(1,128)} %param.8) | copy-start | bytes 772
  2.0 60.5 %copy-start.4 = (f32[5,2,256,128]{3,2,1,0:T(8,128)}, f32[5,2,256,128]{3,2,1,0:T(8,128)S(1)}, u32[]{:S(2)}) copy-start(f32[5,2,256,128]{3,2,1,0:T(8,128)S(1)} %get-tuple-element.84.refs_6_) | copy-start | bytes 3932164
  2.1 71.4 %copy-start.3 = (f32[5,2,256,128]{3,2,1,0:T(8,128)}, f32[5,2,256,128]{3,2,1,0:T(8,128)S(1)}, u32[]{:S(2)}) copy-start(f32[5,2,256,128]{3,2,1,0:T(8,128)S(1)} %get-tuple-element.81.refs_5_) | copy-start | bytes 3932164
  2.1 71.4 %copy-start = (f32[1,8,256,256]{3,2,1,0:T(8,128)S(1)}, f32[1,8,256,256]{3,2,1,0:T(8,128)}, u32[]{:S(2)}) copy-start(f32[1,8,256,256]{3,2,1,0:T(8,128)} %param.11) | copy-start | bytes 6291460
  2.1 71.4 %copy-start.2 = (s32[1,8,1,16]{3,2,1,0:T(1,128)S(1)}, s32[1,8,1,16]{3,2,1,0:T(1,128)}, u32[]{:S(2)}) copy-start(s32[1,8,1,16]{3,2,1,0:T(1,128)} %param.10) | copy-start | bytes 1540
  2.1 32.0 %collective-permute-start.7 = (f32[5,2,256,128]{3,2,1,0:T(8,128)S(1)}, f32[5,2,256,128]{3,2,1,0:T(8,128)}, u32[]{:S(2)}, u32[]{:S(2)}) collective-permute-start(f32[5,2,256,128]{3,2,1,0:T(8,128)S(1)} %get-tuple-element.84.refs_6_), channel_id=1, source_target_pairs={{0,8},{4,12},{8,0},{12,4},{1,9},{5,13},{9,1},{13,5},{2,10},{6,14},... | collective-permute-start | bytes 3932168 | tf_op jit(solution)/shard_map/ppermute | solution.py:217
  3.4 29.4 %collective-permute-start.6 = (f32[5,2,256,128]{3,2,1,0:T(8,128)S(1)}, f32[5,2,256,128]{3,2,1,0:T(8,128)}, u32[]{:S(2)}, u32[]{:S(2)}) collective-permute-start(f32[5,2,256,128]{3,2,1,0:T(8,128)S(1)} %get-tuple-element.81.refs_5_), channel_id=1, source_target_pairs={{0,4},{4,0},{8,12},{12,8},{1,5},{5,1},{9,13},{13,9},{2,6},{6,2},{1... | collective-permute-start | bytes 3932168 | tf_op jit(solution)/shard_map/ppermute | solution.py:217
  4.7 58.1 %copy-start.5 = (f32[5,2,128,256]{3,2,1,0:T(8,128)}, f32[5,2,128,256]{3,2,1,0:T(8,128)S(1)}, u32[]{:S(2)}) copy-start(f32[5,2,128,256]{3,2,1,0:T(8,128)S(1)} %slice_bitcast_fusion.refs_0_) | copy-start | bytes 3932164
  4.8 30.9 %collective-permute-start.3 = (f32[5,2,128,256]{3,2,1,0:T(8,128)S(1)}, f32[5,2,128,256]{3,2,1,0:T(8,128)S(1)}, u32[]{:S(2)}, u32[]{:S(2)}) collective-permute-start(f32[5,2,128,256]{3,2,1,0:T(8,128)S(1)} %slice_bitcast_fusion.refs_0_), channel_id=1, source_target_pairs={{1,0},{2,1},{3,2},{5,4},{6,5},{7,6},{9,8},{10,9},{11,10},{13,12},{... | collective-permute-start | bytes 3932168 | tf_op jit(solution)/shard_map/ppermute | solution.py:217
  6.8 32.0 %collective-permute-start = (f32[5,2,128,256]{3,2,1,0:T(8,128)S(1)}, f32[5,2,128,256]{3,2,1,0:T(8,128)S(1)}, u32[]{:S(2)}, u32[]{:S(2)}) collective-permute-start(f32[5,2,128,256]{3,2,1,0:T(8,128)S(1)} %slice_bitcast_fusion.refs_0_), channel_id=1, source_target_pairs={{0,1},{1,2},{2,3},{4,5},{5,6},{6,7},{8,9},{9,10},{10,11},{12,13},{... | collective-permute-start | bytes 3932168 | tf_op jit(solution)/shard_map/ppermute | solution.py:217
  32.8 28.5 %collective-permute-start.10 = (f32[5,2,256,128]{3,2,1,0:T(8,128)S(1)}, f32[5,2,256,128]{3,2,1,0:T(8,128)S(1)}, u32[]{:S(2)}, u32[]{:S(2)}) collective-permute-start(f32[5,2,256,128]{3,2,1,0:T(8,128)S(1)} %get-tuple-element.84.refs_6_), channel_id=1, source_target_pairs={{0,4},{4,0},{8,12},{12,8},{1,5},{5,1},{9,13},{13,9},{2,6},{6,2},{1... | collective-permute-start | bytes 3932168 | tf_op jit(solution)/shard_map/ppermute | solution.py:217
  34.0 28.5 %collective-permute-start.8 = (f32[5,2,256,128]{3,2,1,0:T(8,128)S(1)}, f32[5,2,256,128]{3,2,1,0:T(8,128)S(1)}, u32[]{:S(2)}, u32[]{:S(2)}) collective-permute-start(f32[5,2,256,128]{3,2,1,0:T(8,128)S(1)} %get-tuple-element.81.refs_5_), channel_id=1, source_target_pairs={{0,8},{4,12},{8,0},{12,4},{1,9},{5,13},{9,1},{13,5},{2,10},{6,14},... | collective-permute-start | bytes 3932168 | tf_op jit(solution)/shard_map/ppermute | solution.py:217
  35.7 28.0 %collective-permute-start.4 = (f32[5,2,128,256]{3,2,1,0:T(8,128)S(1)}, f32[5,2,128,256]{3,2,1,0:T(8,128)}, u32[]{:S(2)}, u32[]{:S(2)}) collective-permute-start(f32[5,2,128,256]{3,2,1,0:T(8,128)S(1)} %collective-permute-done.3.refs_2_), channel_id=1, source_target_pairs={{1,0},{2,1},{5,4},{6,5},{9,8},{10,9},{13,12},{14,13},{17,16},{18,1... | collective-permute-start | bytes 3932168 | tf_op jit(solution)/shard_map/ppermute | solution.py:217
  38.9 29.8 %collective-permute-start.1 = (f32[5,2,128,256]{3,2,1,0:T(8,128)S(1)}, f32[5,2,128,256]{3,2,1,0:T(8,128)}, u32[]{:S(2)}, u32[]{:S(2)}) collective-permute-start(f32[5,2,128,256]{3,2,1,0:T(8,128)S(1)} %collective-permute-done.refs_1_), channel_id=1, source_target_pairs={{1,2},{2,3},{5,6},{6,7},{9,10},{10,11},{13,14},{14,15},{17,18},{18... | collective-permute-start | bytes 3932168 | tf_op jit(solution)/shard_map/ppermute | solution.py:217
  61.3 27.9 %collective-permute-start.11 = (f32[5,2,256,128]{3,2,1,0:T(8,128)}, f32[5,2,256,128]{3,2,1,0:T(8,128)}, u32[]{:S(2)}, u32[]{:S(2)}) collective-permute-start(f32[5,2,256,128]{3,2,1,0:T(8,128)} %collective-permute-done.7.refs_8_), channel_id=1, source_target_pairs={{0,4},{4,0},{8,12},{12,8},{1,5},{5,1},{9,13},{13,9},{2,6},{6,2},{1... | collective-permute-start | bytes 3932168 | tf_op jit(solution)/shard_map/ppermute | solution.py:217
  62.6 27.7 %collective-permute-start.9 = (f32[5,2,256,128]{3,2,1,0:T(8,128)}, f32[5,2,256,128]{3,2,1,0:T(8,128)}, u32[]{:S(2)}, u32[]{:S(2)}) collective-permute-start(f32[5,2,256,128]{3,2,1,0:T(8,128)} %collective-permute-done.6.refs_7_), channel_id=1, source_target_pairs={{0,8},{4,12},{8,0},{12,4},{1,9},{5,13},{9,1},{13,5},{2,10},{6,14},... | collective-permute-start | bytes 3932168 | tf_op jit(solution)/shard_map/ppermute | solution.py:217
  63.7 28.3 %collective-permute-start.5 = (f32[5,2,128,256]{3,2,1,0:T(8,128)}, f32[5,2,128,256]{3,2,1,0:T(8,128)}, u32[]{:S(2)}, u32[]{:S(2)}) collective-permute-start(f32[5,2,128,256]{3,2,1,0:T(8,128)} %collective-permute-done.4.refs_4_), channel_id=1, source_target_pairs={{1,0},{5,4},{9,8},{13,12},{17,16},{21,20},{25,24},{29,28}} | collective-permute-start | bytes 3932168 | tf_op jit(solution)/shard_map/ppermute | solution.py:217
  68.7 27.0 %collective-permute-start.2 = (f32[5,2,128,256]{3,2,1,0:T(8,128)}, f32[5,2,128,256]{3,2,1,0:T(8,128)}, u32[]{:S(2)}, u32[]{:S(2)}) collective-permute-start(f32[5,2,128,256]{3,2,1,0:T(8,128)} %collective-permute-done.1.refs_3_), channel_id=1, source_target_pairs={{2,3},{6,7},{10,11},{14,15},{18,19},{22,23},{26,27},{30,31}} | collective-permute-start | bytes 3932168 | tf_op jit(solution)/shard_map/ppermute | solution.py:217
  90.2 24.0 %collective-permute-start.15 = (f32[3,2,256,128]{3,2,1,0:T(8,128)S(1)}, f32[3,2,256,128]{3,2,1,0:T(8,128)S(1)}, u32[]{:S(2)}, u32[]{:S(2)}) collective-permute-start(f32[3,2,256,128]{3,2,1,0:T(8,128)S(1)} %get-tuple-element.115.refs_5_), channel_id=1, source_target_pairs={{0,4},{4,0},{8,12},{12,8},{1,5},{5,1},{9,13},{13,9},{2,6},{6,2},{1... | collective-permute-start | bytes 2359304 | tf_op jit(solution)/shard_map/ppermute | solution.py:217
  90.5 23.8 %collective-permute-start.14 = (f32[3,2,256,128]{3,2,1,0:T(8,128)S(1)}, f32[3,2,256,128]{3,2,1,0:T(8,128)S(1)}, u32[]{:S(2)}, u32[]{:S(2)}) collective-permute-start(f32[3,2,256,128]{3,2,1,0:T(8,128)S(1)} %get-tuple-element.117.refs_6_), channel_id=1, source_target_pairs={{0,8},{4,12},{8,0},{12,4},{1,9},{5,13},{9,1},{13,5},{2,10},{6,14},... | collective-permute-start | bytes 2359304 | tf_op jit(solution)/shard_map/ppermute | solution.py:217
  92.0 23.1 %collective-permute-start.13 = (f32[3,2,128,256]{3,2,1,0:T(8,128)S(1)}, f32[3,2,128,256]{3,2,1,0:T(8,128)S(1)}, u32[]{:S(2)}, u32[]{:S(2)}) collective-permute-start(f32[3,2,128,256]{3,2,1,0:T(8,128)S(1)} %slice_bitcast_fusion.1.refs_0_), channel_id=1, source_target_pairs={{1,0},{2,1},{3,2},{5,4},{6,5},{7,6},{9,8},{10,9},{11,10},{13,12},{... | collective-permute-start | bytes 2359304 | tf_op jit(solution)/shard_map/ppermute | solution.py:217
  95.7 21.8 %collective-permute-start.12 = (f32[3,2,128,256]{3,2,1,0:T(8,128)S(1)}, f32[3,2,128,256]{3,2,1,0:T(8,128)S(1)}, u32[]{:S(2)}, u32[]{:S(2)}) collective-permute-start(f32[3,2,128,256]{3,2,1,0:T(8,128)S(1)} %slice_bitcast_fusion.1.refs_0_), channel_id=1, source_target_pairs={{0,1},{1,2},{2,3},{4,5},{5,6},{6,7},{8,9},{9,10},{10,11},{12,13},{... | collective-permute-start | bytes 2359304 | tf_op jit(solution)/shard_map/ppermute | solution.py:217
  114.3 15.1 %collective-permute-start.19 = (f32[3,2,256,128]{3,2,1,0:T(8,128)S(1)}, f32[3,2,256,128]{3,2,1,0:T(8,128)S(1)}, u32[]{:S(2)}, u32[]{:S(2)}) collective-permute-start(f32[3,2,256,128]{3,2,1,0:T(8,128)S(1)} %get-tuple-element.117.refs_6_), channel_id=1, source_target_pairs={{0,4},{4,0},{8,12},{12,8},{1,5},{5,1},{9,13},{13,9},{2,6},{6,2},{1... | collective-permute-start | bytes 2359304 | tf_op jit(solution)/shard_map/ppermute | solution.py:217
  114.6 14.8 %collective-permute-start.18 = (f32[3,2,256,128]{3,2,1,0:T(8,128)S(1)}, f32[3,2,256,128]{3,2,1,0:T(8,128)S(1)}, u32[]{:S(2)}, u32[]{:S(2)}) collective-permute-start(f32[3,2,256,128]{3,2,1,0:T(8,128)S(1)} %get-tuple-element.115.refs_5_), channel_id=1, source_target_pairs={{0,8},{4,12},{8,0},{12,4},{1,9},{5,13},{9,1},{13,5},{2,10},{6,14},... | collective-permute-start | bytes 2359304 | tf_op jit(solution)/shard_map/ppermute | solution.py:217
  115.1 14.3 %collective-permute-start.17 = (f32[3,2,128,256]{3,2,1,0:T(8,128)S(1)}, f32[3,2,128,256]{3,2,1,0:T(8,128)S(1)}, u32[]{:S(2)}, u32[]{:S(2)}) collective-permute-start(f32[3,2,128,256]{3,2,1,0:T(8,128)S(1)} %collective-permute-done.13.refs_2_), channel_id=1, source_target_pairs={{1,0},{2,1},{5,4},{6,5},{9,8},{10,9},{13,12},{14,13},{17,16},{18,1... | collective-permute-start | bytes 2359304 | tf_op jit(solution)/shard_map/ppermute | solution.py:217
  117.5 16.2 %collective-permute-start.16 = (f32[3,2,128,256]{3,2,1,0:T(8,128)S(1)}, f32[3,2,128,256]{3,2,1,0:T(8,128)S(1)}, u32[]{:S(2)}, u32[]{:S(2)}) collective-permute-start(f32[3,2,128,256]{3,2,1,0:T(8,128)S(1)} %collective-permute-done.12.refs_1_), channel_id=1, source_target_pairs={{1,2},{2,3},{5,6},{6,7},{9,10},{10,11},{13,14},{14,15},{17,18},{18... | collective-permute-start | bytes 2359304 | tf_op jit(solution)/shard_map/ppermute | solution.py:217
  133.7 13.6 %collective-permute-start.20 = (f32[3,2,128,256]{3,2,1,0:T(8,128)S(1)}, f32[3,2,128,256]{3,2,1,0:T(8,128)S(1)}, u32[]{:S(2)}, u32[]{:S(2)}) collective-permute-start(f32[3,2,128,256]{3,2,1,0:T(8,128)S(1)} %collective-permute-done.16.refs_3_), channel_id=1, source_target_pairs={{2,3},{6,7},{10,11},{14,15},{18,19},{22,23},{26,27},{30,31}} | collective-permute-start | bytes 2359304 | tf_op jit(solution)/shard_map/ppermute | solution.py:217
  135.4 11.8 %collective-permute-start.21 = (f32[3,2,128,256]{3,2,1,0:T(8,128)S(1)}, f32[3,2,128,256]{3,2,1,0:T(8,128)S(1)}, u32[]{:S(2)}, u32[]{:S(2)}) collective-permute-start(f32[3,2,128,256]{3,2,1,0:T(8,128)S(1)} %collective-permute-done.17.refs_4_), channel_id=1, source_target_pairs={{1,0},{5,4},{9,8},{13,12},{17,16},{21,20},{25,24},{29,28}} | collective-permute-start | bytes 2359304 | tf_op jit(solution)/shard_map/ppermute | solution.py:217
  136.1 12.1 %collective-permute-start.22 = (f32[3,2,256,128]{3,2,1,0:T(8,128)S(1)}, f32[3,2,256,128]{3,2,1,0:T(8,128)S(1)}, u32[]{:S(2)}, u32[]{:S(2)}) collective-permute-start(f32[3,2,256,128]{3,2,1,0:T(8,128)S(1)} %collective-permute-done.15.refs_7_), channel_id=1, source_target_pairs={{0,8},{4,12},{8,0},{12,4},{1,9},{5,13},{9,1},{13,5},{2,10},{6,14},... | collective-permute-start | bytes 2359304 | tf_op jit(solution)/shard_map/ppermute | solution.py:217
  136.4 11.8 %collective-permute-start.23 = (f32[3,2,256,128]{3,2,1,0:T(8,128)S(1)}, f32[3,2,256,128]{3,2,1,0:T(8,128)S(1)}, u32[]{:S(2)}, u32[]{:S(2)}) collective-permute-start(f32[3,2,256,128]{3,2,1,0:T(8,128)S(1)} %collective-permute-done.14.refs_8_), channel_id=1, source_target_pairs={{0,4},{4,0},{8,12},{12,8},{1,5},{5,1},{9,13},{13,9},{2,6},{6,2},{1... | collective-permute-start | bytes 2359304 | tf_op jit(solution)/shard_map/ppermute | solution.py:217
  155.2 14.9 %collective-permute-start.24 = (f32[512,2048]{1,0:T(8,128)S(1)}, f32[512,2048]{1,0:T(8,128)S(1)}, u32[]{:S(2)}, u32[]{:S(2)}) collective-permute-start(f32[512,2048]{1,0:T(8,128)S(1)} %get-tuple-element.146), channel_id=1, source_target_pairs={{0,16},{16,0},{1,17},{17,1},{2,18},{18,2},{3,19},{19,3},{4,20},{20... | collective-permute-start | bytes 12582920 | tf_op jit(solution)/shard_map/ppermute | solution.py:369
  (17 other events, 299.2 us)

commit v7 on v6

--- a/solution.py
+++ b/solution.py
@@ -243,17 +243,17 @@
 
     def first(self):
         lx, ly, lu, ld = self.links
-        self.x0, self.y1 = lx.send(self.h[0], side(1)), ly.send(self.h[1], side(2))
+        self.y1, self.x0 = ly.send(self.h[1], side(2)), lx.send(self.h[0], side(1))
         self.d1, self.u1 = ld.send(self.l, down(1)), lu.send(self.l, up(1))
 
     def second(self):
         lx, ly, lu, ld = self.links
-        self.x1, self.y0 = lx.send(self.h[1], side(1)), ly.send(self.h[0], side(2))
+        self.y0, self.x1 = ly.send(self.h[0], side(2)), lx.send(self.h[1], side(1))
         self.d2, self.u2 = ld.send(self.d1.value, down(2)), lu.send(self.u1.value, up(2))
 
     def third(self, here):
         lx, ly, lu, ld = self.links
-        f1, f0 = lx.send(self.y1.value[here], side(1)), ly.send(self.x0.value[here], side(2))
+        f0, f1 = ly.send(self.x0.value[here], side(2)), lx.send(self.y1.value[here], side(1))
         d3, u3 = ld.send(self.d2.value[here], down(3)), lu.send(self.u2.value[here], up(3))
         return u3, d3, f0, f1
 

time: 176 us -> 176 us (level)
    ppermute x24, starting transfers between devices: 37.8 us -> 39.9 us  [send(): out = Box(lax.ppermute(after(x, self.wait), self.axis, pairs))]
  transfers between devices with their start and end apart: 25 -> 25, of which waited for: 12 -> 13; matrix products, arithmetic and copies ran while one was open for 2% -> 2% of each run, Pallas kernels for 28% -> 28%
where the time goes in v7:
time: 176 us; the launch traced here: 173 us
  waiting for transfers between devices  61.2 us (35%)
  Pallas kernels  56.3 us (32%)
  starting transfers between devices  47.2 us (27%)
  local copies, waits for them, and re-layouts  5.27 us (3%)
  other arithmetic  2.8 us (2%)
    ppermute x24, waiting for transfers between devices, send(): out = Box(lax.ppermute(after(x, self.wait), self.axis, pairs))  60.3 us
    pallas_call x6, Pallas kernels, call(): pl.pallas_call(functools.partial(kernel, len(l_bufs), len(u_bufs), start)...  50.4 us
    ppermute x24, starting transfers between devices, send(): out = Box(lax.ppermute(after(x, self.wait), self.axis, pairs))  39.9 us
    ppermute x1, starting transfers between devices, body(): other = lax.ppermute(send, 'gz', [(0, 1), (1, 0)])  7.31 us
    pallas_call x1, Pallas kernels, body(): pl.pallas_call(keep_kernel, grid=(nodes - size,), out_shape=ACC, in_specs...  5.87 us
  transfers between devices with their start and end apart: 25, of which 13 were waited for; matrix products, arithmetic and copies ran while one was open for 2% of the time, Pallas kernels for 28%

profile of v7, /device:TPU:17, one launch (start us, length us, event | category | flops | bytes accessed | tf_op | source)
XLA Modules:
  0.0 173.1 jit_solution(4199298143554092442)
XLA Ops:
  0.0 2.0 %fusion.3 = (f32[5,2,256,128]{3,2,1,0:T(8,128)S(1)}, f32[5,2,256,128]{3,2,1,0:T(8,128)S(1)}) fusion(f32[8,4,256,128]{3,2,1,0:T(8,128)} %bitcast.50), kind=kLoop, calls=%fused_computation.11 | loop fusion | bytes 5242880 | tf_op jit(solution)/shard_map/slice | solution.py:289
  2.1 1.3 collective-permute-start.6
  4.8 2.1 %collective-permute-start.3 = (f32[5,2,128,256]{3,2,1,0:T(8,128)S(1)}, f32[5,2,128,256]{3,2,1,0:T(8,128)S(1)}, u32[]{:S(2)}, u32[]{:S(2)}) collective-permute-start(f32[5,2,128,256]{3,2,1,0:T(8,128)S(1)} %slice_bitcast_fusion.refs_0_), channel_id=1, source_target_pairs={{1,0},{2,1},{3,2},{5,4},{6,5},{7,6},{9,8},{10,9},{11,10},{13,12},{... | collective-permute-start | bytes 3932168 | tf_op jit(solution)/shard_map/ppermute | solution.py:217
  6.8 3.3 %collective-permute-start = (f32[5,2,128,256]{3,2,1,0:T(8,128)S(1)}, f32[5,2,128,256]{3,2,1,0:T(8,128)S(1)}, u32[]{:S(2)}, u32[]{:S(2)}) collective-permute-start(f32[5,2,128,256]{3,2,1,0:T(8,128)S(1)} %slice_bitcast_fusion.refs_0_), channel_id=1, source_target_pairs={{0,1},{1,2},{2,3},{4,5},{5,6},{6,7},{8,9},{9,10},{10,11},{12,13},{... | collective-permute-start | bytes 3932168 | tf_op jit(solution)/shard_map/ppermute | solution.py:217
  10.1 21.8 %collective-permute-done.6.refs_8_ = f32[5,2,256,128]{3,2,1,0:T(8,128)} collective-permute-done((f32[5,2,256,128]{3,2,1,0:T(8,128)S(1)}, f32[5,2,256,128]{3,2,1,0:T(8,128)}, u32[]{:S(2)}, u32[]{:S(2)}) %collective-permute-start.6) | collective-permute-done | bytes 1310752 | tf_op jit(solution)/shard_map/ppermute | solution.py:217
  34.4 1.3 collective-permute-done.3.refs_2_
  35.7 3.2 %collective-permute-start.4 = (f32[5,2,128,256]{3,2,1,0:T(8,128)S(1)}, f32[5,2,128,256]{3,2,1,0:T(8,128)}, u32[]{:S(2)}, u32[]{:S(2)}) collective-permute-start(f32[5,2,128,256]{3,2,1,0:T(8,128)S(1)} %collective-permute-done.3.refs_2_), channel_id=1, source_target_pairs={{1,0},{2,1},{5,4},{6,5},{9,8},{10,9},{13,12},{14,13},{17,16},{18,1... | collective-permute-start | bytes 3932168 | tf_op jit(solution)/shard_map/ppermute | solution.py:217
  38.9 1.9 %collective-permute-start.1 = (f32[5,2,128,256]{3,2,1,0:T(8,128)S(1)}, f32[5,2,128,256]{3,2,1,0:T(8,128)}, u32[]{:S(2)}, u32[]{:S(2)}) collective-permute-start(f32[5,2,128,256]{3,2,1,0:T(8,128)S(1)} %collective-permute-done.refs_1_), channel_id=1, source_target_pairs={{1,2},{2,3},{5,6},{6,7},{9,10},{10,11},{13,14},{14,15},{17,18},{18... | collective-permute-start | bytes 3932168 | tf_op jit(solution)/shard_map/ppermute | solution.py:217
  40.8 19.9 %collective-permute-done.10.refs_10_ = f32[5,2,256,128]{3,2,1,0:T(8,128)S(1)} collective-permute-done((f32[5,2,256,128]{3,2,1,0:T(8,128)S(1)}, f32[5,2,256,128]{3,2,1,0:T(8,128)S(1)}, u32[]{:S(2)}, u32[]{:S(2)}) %collective-permute-start.10) | collective-permute-done | bytes 1310752 | tf_op jit(solution)/shard_map/ppermute | solution.py:217
  62.0 1.3 collective-permute-start.9
  63.7 1.8 %collective-permute-start.5 = (f32[5,2,128,256]{3,2,1,0:T(8,128)}, f32[5,2,128,256]{3,2,1,0:T(8,128)}, u32[]{:S(2)}, u32[]{:S(2)}) collective-permute-start(f32[5,2,128,256]{3,2,1,0:T(8,128)} %collective-permute-done.4.refs_4_), channel_id=1, source_target_pairs={{1,0},{5,4},{9,8},{13,12},{17,16},{21,20},{25,24},{29,28}} | collective-permute-start | bytes 3932168 | tf_op jit(solution)/shard_map/ppermute | solution.py:217
  65.4 3.3 %collective-permute-done.1.refs_3_ = f32[5,2,128,256]{3,2,1,0:T(8,128)} collective-permute-done((f32[5,2,128,256]{3,2,1,0:T(8,128)S(1)}, f32[5,2,128,256]{3,2,1,0:T(8,128)}, u32[]{:S(2)}, u32[]{:S(2)}) %collective-permute-start.1) | collective-permute-done | bytes 1310752 | tf_op jit(solution)/shard_map/ppermute | solution.py:217
  68.7 3.0 %collective-permute-start.2 = (f32[5,2,128,256]{3,2,1,0:T(8,128)}, f32[5,2,128,256]{3,2,1,0:T(8,128)}, u32[]{:S(2)}, u32[]{:S(2)}) collective-permute-start(f32[5,2,128,256]{3,2,1,0:T(8,128)} %collective-permute-done.1.refs_3_), channel_id=1, source_target_pairs={{2,3},{6,7},{10,11},{14,15},{18,19},{22,23},{26,27},{30,31}} | collective-permute-start | bytes 3932168 | tf_op jit(solution)/shard_map/ppermute | solution.py:217
  72.0 1.5 fusion.2
  73.5 7.0 %shard_map.73 = (bf16[3,1024,512]{2,1,0:T(8,128)(2,1)S(1)}, bf16[3,512,2048]{2,1,0:T(8,128)(2,1)S(1)}, f32[8,128]{1,0:T(8,128)S(1)}) custom-call(s32[8,8]{1,0:T(8,128)S(1)} %fusion.1.l_tgt, s32[8,16]{1,0:T(8,128)S(1)} %bitcast.38, s32[5]{0:T(128)S(1)} %bitcast.44, s32[6]{0:T(128)S(1)} %bitcast.47, f32[5,2,128,256]{3,2,1,0:T(8,128)} %copy-done.5, ...), custom_call_target="tpu_custom_call" | custom-call | tf_op jit(solution)/shard_map/pallas_call | solution.py:168
  80.5 5.5 %shard_map.74 = (bf16[2,1024,512]{2,1,0:T(8,128)(2,1)S(1)}, bf16[2,512,2048]{2,1,0:T(8,128)(2,1)S(1)}, f32[8,128]{1,0:T(8,128)S(1)}) custom-call(s32[8,8]{1,0:T(8,128)S(1)} %fusion.1.l_tgt, s32[8,16]{1,0:T(8,128)S(1)} %bitcast.39, s32[5]{0:T(128)S(1)} %bitcast.45, s32[6]{0:T(128)S(1)} %bitcast.48, f32[5,2,128,256]{3,2,1,0:T(8,128)} %copy-done.5, ...), custom_call_target="tpu_custom_call" | custom-call | tf_op jit(solution)/shard_map/pallas_call | solution.py:168
  86.0 3.0 %collective-permute-done.11.refs_2_ = f32[5,2,256,128]{3,2,1,0:T(8,128)} collective-permute-done((f32[5,2,256,128]{3,2,1,0:T(8,128)}, f32[5,2,256,128]{3,2,1,0:T(8,128)}, u32[]{:S(2)}, u32[]{:S(2)}) %collective-permute-start.11) | collective-permute-done | bytes 1310752 | tf_op jit(solution)/shard_map/ppermute | solution.py:217
  92.7 2.5 %collective-permute-start.13 = (f32[3,2,128,256]{3,2,1,0:T(8,128)S(1)}, f32[3,2,128,256]{3,2,1,0:T(8,128)S(1)}, u32[]{:S(2)}, u32[]{:S(2)}) collective-permute-start(f32[3,2,128,256]{3,2,1,0:T(8,128)S(1)} %slice_bitcast_fusion.1.refs_0_), channel_id=1, source_target_pairs={{1,0},{2,1},{3,2},{5,4},{6,5},{7,6},{9,8},{10,9},{11,10},{13,12},{... | collective-permute-start | bytes 2359304 | tf_op jit(solution)/shard_map/ppermute | solution.py:217
  95.7 4.1 %collective-permute-start.12 = (f32[3,2,128,256]{3,2,1,0:T(8,128)S(1)}, f32[3,2,128,256]{3,2,1,0:T(8,128)S(1)}, u32[]{:S(2)}, u32[]{:S(2)}) collective-permute-start(f32[3,2,128,256]{3,2,1,0:T(8,128)S(1)} %slice_bitcast_fusion.1.refs_0_), channel_id=1, source_target_pairs={{0,1},{1,2},{2,3},{4,5},{5,6},{6,7},{8,9},{9,10},{10,11},{12,13},{... | collective-permute-start | bytes 2359304 | tf_op jit(solution)/shard_map/ppermute | solution.py:217
  100.0 14.4 %shard_map.75 = (bf16[3,1024,512]{2,1,0:T(8,128)(2,1)S(1)}, bf16[3,512,2048]{2,1,0:T(8,128)(2,1)S(1)}, f32[512,2048]{1,0:T(8,128)S(1)}, f32[512,2048]{1,0:T(8,128)S(1)}, f32[8,128]{1,0:T(8,128)S(1)}) custom-call(s32[8,8]{1,0:T(8,128)S(1)} %fusion.1.l_tgt, s32[8,16]{1,0:T(8,128)S(1)} %bitcast.40, ...), custom_call_target="tpu_custom_call", output_to_operand_aliasing={{0}: (10, {}), {1}: (11, {})} | custom-call | tf_op jit(solution)/shard_map/pallas_call | solution.py:168
  115.2 2.2 %collective-permute-start.17 = (f32[3,2,128,256]{3,2,1,0:T(8,128)S(1)}, f32[3,2,128,256]{3,2,1,0:T(8,128)S(1)}, u32[]{:S(2)}, u32[]{:S(2)}) collective-permute-start(f32[3,2,128,256]{3,2,1,0:T(8,128)S(1)} %collective-permute-done.13.refs_2_), channel_id=1, source_target_pairs={{1,0},{2,1},{5,4},{6,5},{9,8},{10,9},{13,12},{14,13},{17,16},{18,1... | collective-permute-start | bytes 2359304 | tf_op jit(solution)/shard_map/ppermute | solution.py:217
  117.5 2.1 %collective-permute-start.16 = (f32[3,2,128,256]{3,2,1,0:T(8,128)S(1)}, f32[3,2,128,256]{3,2,1,0:T(8,128)S(1)}, u32[]{:S(2)}, u32[]{:S(2)}) collective-permute-start(f32[3,2,128,256]{3,2,1,0:T(8,128)S(1)} %collective-permute-done.12.refs_1_), channel_id=1, source_target_pairs={{1,2},{2,3},{5,6},{6,7},{9,10},{10,11},{13,14},{14,15},{17,18},{18... | collective-permute-start | bytes 2359304 | tf_op jit(solution)/shard_map/ppermute | solution.py:217
  119.6 9.8 %shard_map.76 = (bf16[2,1024,512]{2,1,0:T(8,128)(2,1)S(1)}, bf16[2,512,2048]{2,1,0:T(8,128)(2,1)S(1)}, f32[512,2048]{1,0:T(8,128)S(1)}, f32[512,2048]{1,0:T(8,128)S(1)}, f32[8,128]{1,0:T(8,128)S(1)}) custom-call(s32[8,8]{1,0:T(8,128)S(1)} %fusion.1.l_tgt, ...), custom_call_target="tpu_custom_call", output_to_operand_aliasing={{0}: (10, {}), {1}: (11, {}), {2}: (12, {}), {3}: (13, {})} | custom-call | tf_op jit(solution)/shard_map/pallas_call | solution.py:168
  129.6 4.0 %collective-permute-done.16.refs_3_ = f32[3,2,128,256]{3,2,1,0:T(8,128)S(1)} collective-permute-done((f32[3,2,128,256]{3,2,1,0:T(8,128)S(1)}, f32[3,2,128,256]{3,2,1,0:T(8,128)S(1)}, u32[]{:S(2)}, u32[]{:S(2)}) %collective-permute-start.16) | collective-permute-done | bytes 786464 | tf_op jit(solution)/shard_map/ppermute | solution.py:217
  133.7 2.1 %collective-permute-start.20 = (f32[3,2,128,256]{3,2,1,0:T(8,128)S(1)}, f32[3,2,128,256]{3,2,1,0:T(8,128)S(1)}, u32[]{:S(2)}, u32[]{:S(2)}) collective-permute-start(f32[3,2,128,256]{3,2,1,0:T(8,128)S(1)} %collective-permute-done.16.refs_3_), channel_id=1, source_target_pairs={{2,3},{6,7},{10,11},{14,15},{18,19},{22,23},{26,27},{30,31}} | collective-permute-start | bytes 2359304 | tf_op jit(solution)/shard_map/ppermute | solution.py:217
  137.6 6.9 %shard_map.77 = (bf16[3,1024,512]{2,1,0:T(8,128)(2,1)S(1)}, bf16[3,512,2048]{2,1,0:T(8,128)(2,1)S(1)}, f32[8,128]{1,0:T(8,128)S(1)}) custom-call(s32[8,8]{1,0:T(8,128)S(1)} %fusion.1.l_tgt, s32[8,16]{1,0:T(8,128)S(1)} %bitcast.42, s32[5]{0:T(128)S(1)} %bitcast.46, s32[6]{0:T(128)S(1)} %bitcast.49, f32[3,2,128,256]{3,2,1,0:T(8,128)} %copy-done.10, ...), custom_call_target="tpu_custom_call" | custom-call | tf_op jit(solution)/shard_map/pallas_call | solution.py:168
  144.6 3.1 %collective-permute-done.20.refs_0_ = f32[3,2,128,256]{3,2,1,0:T(8,128)S(1)} collective-permute-done((f32[3,2,128,256]{3,2,1,0:T(8,128)S(1)}, f32[3,2,128,256]{3,2,1,0:T(8,128)S(1)}, u32[]{:S(2)}, u32[]{:S(2)}) %collective-permute-start.20) | collective-permute-done | bytes 786464 | tf_op jit(solution)/shard_map/ppermute | solution.py:217
  147.6 1.7 collective-permute-done.23.refs_3_
  149.3 6.9 %shard_map.78 = (bf16[3,1024,512]{2,1,0:T(8,128)(2,1)S(1)}, bf16[3,512,2048]{2,1,0:T(8,128)(2,1)S(1)}, f32[512,2048]{1,0:T(8,128)S(1)}, f32[8,128]{1,0:T(8,128)S(1)}) custom-call(s32[8,8]{1,0:T(8,128)S(1)} %fusion.1.l_tgt, s32[8,16]{1,0:T(8,128)S(1)} %bitcast.43, s32[2]{0:T(128)S(1)} %slice.44.l_base, ...), custom_call_target="tpu_custom_call", output_to_operand_aliasing={{0}: (10, {}), {1}: (11, {}), {2}: (12, {})} | custom-call | tf_op jit(solution)/shard_map/pallas_call | solution.py:168
  156.3 7.3 %collective-permute-start.24 = (f32[512,2048]{1,0:T(8,128)S(1)}, f32[512,2048]{1,0:T(8,128)S(1)}, u32[]{:S(2)}, u32[]{:S(2)}) collective-permute-start(f32[512,2048]{1,0:T(8,128)S(1)} %get-tuple-element.146), channel_id=1, source_target_pairs={{0,16},{16,0},{1,17},{17,1},{2,18},{18,2},{3,19},{19,3},{4,20},{20... | collective-permute-start | bytes 12582920 | tf_op jit(solution)/shard_map/ppermute | solution.py:369
  163.6 5.9 %shard_map.79 = f32[512,2048]{1,0:T(8,128)S(1)} custom-call(bf16[3,1024,512]{2,1,0:T(8,128)(2,1)S(1)} %get-tuple-element.142.l_cats, bf16[3,512,2048]{2,1,0:T(8,128)(2,1)S(1)} %get-tuple-element.143.u_cats, f32[8,128]{1,0:T(8,128)S(1)} %get-tuple-element.144._, f32[512,2048]{1,0:T(8,128)S(1)} %get-tuple-element.145.keep_in), custom_call_target="tpu_custom_call", output_to_operand_aliasing={{}: (3, {})} | custom-call | tf_op jit(solution)/shard_map/pallas_call | solution.py:353
  170.4 2.8 %subtract_bitcast_fusion = f32[1,512,2048]{2,1,0:T(8,128)} fusion(f32[512,2048]{1,0:T(8,128)S(1)} %shard_map.79, f32[512,2048]{1,0:T(8,128)S(1)} %collective-permute-done.24), kind=kLoop, calls=%fused_computation | loop fusion | flops 1048576 | bytes 12582912 | tf_op jit(solution)/shard_map/broadcast_in_dim | solution.py:370
  (86 shorter events, 13.8 us)
Async XLA Ops:
  0.0 71.9 %copy-start.23 = (s32[8]{0:T(128)S(1)}, s32[8]{0:T(128)}, u32[]{:S(2)}) copy-start(s32[8]{0:T(128)} %constant.60) | copy-start | bytes 100
  0.0 72.0 %copy-start.22 = (s32[1,8,1,8]{3,2,1,0:T(1,128)S(1)}, s32[1,8,1,8]{3,2,1,0:T(1,128)}, u32[]{:S(2)}) copy-start(s32[1,8,1,8]{3,2,1,0:T(1,128)} %param.8) | copy-start | bytes 772
  2.0 59.9 %copy-start.4 = (f32[5,2,256,128]{3,2,1,0:T(8,128)}, f32[5,2,256,128]{3,2,1,0:T(8,128)S(1)}, u32[]{:S(2)}) copy-start(f32[5,2,256,128]{3,2,1,0:T(8,128)S(1)} %get-tuple-element.84.refs_5_) | copy-start | bytes 3932164
  2.1 71.4 %copy-start.3 = (f32[5,2,256,128]{3,2,1,0:T(8,128)}, f32[5,2,256,128]{3,2,1,0:T(8,128)S(1)}, u32[]{:S(2)}) copy-start(f32[5,2,256,128]{3,2,1,0:T(8,128)S(1)} %get-tuple-element.81.refs_6_) | copy-start | bytes 3932164
  2.1 71.4 %copy-start = (f32[1,8,256,256]{3,2,1,0:T(8,128)S(1)}, f32[1,8,256,256]{3,2,1,0:T(8,128)}, u32[]{:S(2)}) copy-start(f32[1,8,256,256]{3,2,1,0:T(8,128)} %param.11) | copy-start | bytes 6291460
  2.1 71.4 %copy-start.2 = (s32[1,8,1,16]{3,2,1,0:T(1,128)S(1)}, s32[1,8,1,16]{3,2,1,0:T(1,128)}, u32[]{:S(2)}) copy-start(s32[1,8,1,16]{3,2,1,0:T(1,128)} %param.10) | copy-start | bytes 1540
  2.1 29.8 %collective-permute-start.6 = (f32[5,2,256,128]{3,2,1,0:T(8,128)S(1)}, f32[5,2,256,128]{3,2,1,0:T(8,128)}, u32[]{:S(2)}, u32[]{:S(2)}) collective-permute-start(f32[5,2,256,128]{3,2,1,0:T(8,128)S(1)} %get-tuple-element.81.refs_6_), channel_id=1, source_target_pairs={{0,8},{4,12},{8,0},{12,4},{1,9},{5,13},{9,1},{13,5},{2,10},{6,14},... | collective-permute-start | bytes 3932168 | tf_op jit(solution)/shard_map/ppermute | solution.py:217
  3.4 29.8 %collective-permute-start.7 = (f32[5,2,256,128]{3,2,1,0:T(8,128)S(1)}, f32[5,2,256,128]{3,2,1,0:T(8,128)}, u32[]{:S(2)}, u32[]{:S(2)}) collective-permute-start(f32[5,2,256,128]{3,2,1,0:T(8,128)S(1)} %get-tuple-element.84.refs_5_), channel_id=1, source_target_pairs={{0,4},{4,0},{8,12},{12,8},{1,5},{5,1},{9,13},{13,9},{2,6},{6,2},{1... | collective-permute-start | bytes 3932168 | tf_op jit(solution)/shard_map/ppermute | solution.py:217
  4.7 58.5 %copy-start.5 = (f32[5,2,128,256]{3,2,1,0:T(8,128)}, f32[5,2,128,256]{3,2,1,0:T(8,128)S(1)}, u32[]{:S(2)}) copy-start(f32[5,2,128,256]{3,2,1,0:T(8,128)S(1)} %slice_bitcast_fusion.refs_0_) | copy-start | bytes 3932164
  4.8 30.9 %collective-permute-start.3 = (f32[5,2,128,256]{3,2,1,0:T(8,128)S(1)}, f32[5,2,128,256]{3,2,1,0:T(8,128)S(1)}, u32[]{:S(2)}, u32[]{:S(2)}) collective-permute-start(f32[5,2,128,256]{3,2,1,0:T(8,128)S(1)} %slice_bitcast_fusion.refs_0_), channel_id=1, source_target_pairs={{1,0},{2,1},{3,2},{5,4},{6,5},{7,6},{9,8},{10,9},{11,10},{13,12},{... | collective-permute-start | bytes 3932168 | tf_op jit(solution)/shard_map/ppermute | solution.py:217
  6.8 32.1 %collective-permute-start = (f32[5,2,128,256]{3,2,1,0:T(8,128)S(1)}, f32[5,2,128,256]{3,2,1,0:T(8,128)S(1)}, u32[]{:S(2)}, u32[]{:S(2)}) collective-permute-start(f32[5,2,128,256]{3,2,1,0:T(8,128)S(1)} %slice_bitcast_fusion.refs_0_), channel_id=1, source_target_pairs={{0,1},{1,2},{2,3},{4,5},{5,6},{6,7},{8,9},{9,10},{10,11},{12,13},{... | collective-permute-start | bytes 3932168 | tf_op jit(solution)/shard_map/ppermute | solution.py:217
  31.9 28.8 %collective-permute-start.10 = (f32[5,2,256,128]{3,2,1,0:T(8,128)S(1)}, f32[5,2,256,128]{3,2,1,0:T(8,128)S(1)}, u32[]{:S(2)}, u32[]{:S(2)}) collective-permute-start(f32[5,2,256,128]{3,2,1,0:T(8,128)S(1)} %get-tuple-element.84.refs_5_), channel_id=1, source_target_pairs={{0,8},{4,12},{8,0},{12,4},{1,9},{5,13},{9,1},{13,5},{2,10},{6,14},... | collective-permute-start | bytes 3932168 | tf_op jit(solution)/shard_map/ppermute | solution.py:217
  33.2 28.8 %collective-permute-start.8 = (f32[5,2,256,128]{3,2,1,0:T(8,128)S(1)}, f32[5,2,256,128]{3,2,1,0:T(8,128)S(1)}, u32[]{:S(2)}, u32[]{:S(2)}) collective-permute-start(f32[5,2,256,128]{3,2,1,0:T(8,128)S(1)} %get-tuple-element.81.refs_6_), channel_id=1, source_target_pairs={{0,4},{4,0},{8,12},{12,8},{1,5},{5,1},{9,13},{13,9},{2,6},{6,2},{1... | collective-permute-start | bytes 3932168 | tf_op jit(solution)/shard_map/ppermute | solution.py:217
  35.7 28.0 %collective-permute-start.4 = (f32[5,2,128,256]{3,2,1,0:T(8,128)S(1)}, f32[5,2,128,256]{3,2,1,0:T(8,128)}, u32[]{:S(2)}, u32[]{:S(2)}) collective-permute-start(f32[5,2,128,256]{3,2,1,0:T(8,128)S(1)} %collective-permute-done.3.refs_2_), channel_id=1, source_target_pairs={{1,0},{2,1},{5,4},{6,5},{9,8},{10,9},{13,12},{14,13},{17,16},{18,1... | collective-permute-start | bytes 3932168 | tf_op jit(solution)/shard_map/ppermute | solution.py:217
  38.9 29.8 %collective-permute-start.1 = (f32[5,2,128,256]{3,2,1,0:T(8,128)S(1)}, f32[5,2,128,256]{3,2,1,0:T(8,128)}, u32[]{:S(2)}, u32[]{:S(2)}) collective-permute-start(f32[5,2,128,256]{3,2,1,0:T(8,128)S(1)} %collective-permute-done.refs_1_), channel_id=1, source_target_pairs={{1,2},{2,3},{5,6},{6,7},{9,10},{10,11},{13,14},{14,15},{17,18},{18... | collective-permute-start | bytes 3932168 | tf_op jit(solution)/shard_map/ppermute | solution.py:217
  60.7 28.2 %collective-permute-start.11 = (f32[5,2,256,128]{3,2,1,0:T(8,128)}, f32[5,2,256,128]{3,2,1,0:T(8,128)}, u32[]{:S(2)}, u32[]{:S(2)}) collective-permute-start(f32[5,2,256,128]{3,2,1,0:T(8,128)} %collective-permute-done.7.refs_7_), channel_id=1, source_target_pairs={{0,8},{4,12},{8,0},{12,4},{1,9},{5,13},{9,1},{13,5},{2,10},{6,14},... | collective-permute-start | bytes 3932168 | tf_op jit(solution)/shard_map/ppermute | solution.py:217
  62.0 28.0 %collective-permute-start.9 = (f32[5,2,256,128]{3,2,1,0:T(8,128)}, f32[5,2,256,128]{3,2,1,0:T(8,128)}, u32[]{:S(2)}, u32[]{:S(2)}) collective-permute-start(f32[5,2,256,128]{3,2,1,0:T(8,128)} %collective-permute-done.6.refs_8_), channel_id=1, source_target_pairs={{0,4},{4,0},{8,12},{12,8},{1,5},{5,1},{9,13},{13,9},{2,6},{6,2},{1... | collective-permute-start | bytes 3932168 | tf_op jit(solution)/shard_map/ppermute | solution.py:217
  63.7 29.0 %collective-permute-start.5 = (f32[5,2,128,256]{3,2,1,0:T(8,128)}, f32[5,2,128,256]{3,2,1,0:T(8,128)}, u32[]{:S(2)}, u32[]{:S(2)}) collective-permute-start(f32[5,2,128,256]{3,2,1,0:T(8,128)} %collective-permute-done.4.refs_4_), channel_id=1, source_target_pairs={{1,0},{5,4},{9,8},{13,12},{17,16},{21,20},{25,24},{29,28}} | collective-permute-start | bytes 3932168 | tf_op jit(solution)/shard_map/ppermute | solution.py:217
  68.7 27.0 %collective-permute-start.2 = (f32[5,2,128,256]{3,2,1,0:T(8,128)}, f32[5,2,128,256]{3,2,1,0:T(8,128)}, u32[]{:S(2)}, u32[]{:S(2)}) collective-permute-start(f32[5,2,128,256]{3,2,1,0:T(8,128)} %collective-permute-done.1.refs_3_), channel_id=1, source_target_pairs={{2,3},{6,7},{10,11},{14,15},{18,19},{22,23},{26,27},{30,31}} | collective-permute-start | bytes 3932168 | tf_op jit(solution)/shard_map/ppermute | solution.py:217
  90.0 24.4 %collective-permute-start.15 = (f32[3,2,256,128]{3,2,1,0:T(8,128)S(1)}, f32[3,2,256,128]{3,2,1,0:T(8,128)S(1)}, u32[]{:S(2)}, u32[]{:S(2)}) collective-permute-start(f32[3,2,256,128]{3,2,1,0:T(8,128)S(1)} %get-tuple-element.115.refs_6_), channel_id=1, source_target_pairs={{0,8},{4,12},{8,0},{12,4},{1,9},{5,13},{9,1},{13,5},{2,10},{6,14},... | collective-permute-start | bytes 2359304 | tf_op jit(solution)/shard_map/ppermute | solution.py:217
  90.2 24.2 %collective-permute-start.14 = (f32[3,2,256,128]{3,2,1,0:T(8,128)S(1)}, f32[3,2,256,128]{3,2,1,0:T(8,128)S(1)}, u32[]{:S(2)}, u32[]{:S(2)}) collective-permute-start(f32[3,2,256,128]{3,2,1,0:T(8,128)S(1)} %get-tuple-element.117.refs_5_), channel_id=1, source_target_pairs={{0,4},{4,0},{8,12},{12,8},{1,5},{5,1},{9,13},{13,9},{2,6},{6,2},{1... | collective-permute-start | bytes 2359304 | tf_op jit(solution)/shard_map/ppermute | solution.py:217
  92.7 22.5 %collective-permute-start.13 = (f32[3,2,128,256]{3,2,1,0:T(8,128)S(1)}, f32[3,2,128,256]{3,2,1,0:T(8,128)S(1)}, u32[]{:S(2)}, u32[]{:S(2)}) collective-permute-start(f32[3,2,128,256]{3,2,1,0:T(8,128)S(1)} %slice_bitcast_fusion.1.refs_0_), channel_id=1, source_target_pairs={{1,0},{2,1},{3,2},{5,4},{6,5},{7,6},{9,8},{10,9},{11,10},{13,12},{... | collective-permute-start | bytes 2359304 | tf_op jit(solution)/shard_map/ppermute | solution.py:217
  95.7 21.7 %collective-permute-start.12 = (f32[3,2,128,256]{3,2,1,0:T(8,128)S(1)}, f32[3,2,128,256]{3,2,1,0:T(8,128)S(1)}, u32[]{:S(2)}, u32[]{:S(2)}) collective-permute-start(f32[3,2,128,256]{3,2,1,0:T(8,128)S(1)} %slice_bitcast_fusion.1.refs_0_), channel_id=1, source_target_pairs={{0,1},{1,2},{2,3},{4,5},{5,6},{6,7},{8,9},{9,10},{10,11},{12,13},{... | collective-permute-start | bytes 2359304 | tf_op jit(solution)/shard_map/ppermute | solution.py:217
  114.4 15.0 %collective-permute-start.19 = (f32[3,2,256,128]{3,2,1,0:T(8,128)S(1)}, f32[3,2,256,128]{3,2,1,0:T(8,128)S(1)}, u32[]{:S(2)}, u32[]{:S(2)}) collective-permute-start(f32[3,2,256,128]{3,2,1,0:T(8,128)S(1)} %get-tuple-element.117.refs_5_), channel_id=1, source_target_pairs={{0,8},{4,12},{8,0},{12,4},{1,9},{5,13},{9,1},{13,5},{2,10},{6,14},... | collective-permute-start | bytes 2359304 | tf_op jit(solution)/shard_map/ppermute | solution.py:217
  114.7 14.7 %collective-permute-start.18 = (f32[3,2,256,128]{3,2,1,0:T(8,128)S(1)}, f32[3,2,256,128]{3,2,1,0:T(8,128)S(1)}, u32[]{:S(2)}, u32[]{:S(2)}) collective-permute-start(f32[3,2,256,128]{3,2,1,0:T(8,128)S(1)} %get-tuple-element.115.refs_6_), channel_id=1, source_target_pairs={{0,4},{4,0},{8,12},{12,8},{1,5},{5,1},{9,13},{13,9},{2,6},{6,2},{1... | collective-permute-start | bytes 2359304 | tf_op jit(solution)/shard_map/ppermute | solution.py:217
  115.2 14.4 %collective-permute-start.17 = (f32[3,2,128,256]{3,2,1,0:T(8,128)S(1)}, f32[3,2,128,256]{3,2,1,0:T(8,128)S(1)}, u32[]{:S(2)}, u32[]{:S(2)}) collective-permute-start(f32[3,2,128,256]{3,2,1,0:T(8,128)S(1)} %collective-permute-done.13.refs_2_), channel_id=1, source_target_pairs={{1,0},{2,1},{5,4},{6,5},{9,8},{10,9},{13,12},{14,13},{17,16},{18,1... | collective-permute-start | bytes 2359304 | tf_op jit(solution)/shard_map/ppermute | solution.py:217
  117.5 16.2 %collective-permute-start.16 = (f32[3,2,128,256]{3,2,1,0:T(8,128)S(1)}, f32[3,2,128,256]{3,2,1,0:T(8,128)S(1)}, u32[]{:S(2)}, u32[]{:S(2)}) collective-permute-start(f32[3,2,128,256]{3,2,1,0:T(8,128)S(1)} %collective-permute-done.12.refs_1_), channel_id=1, source_target_pairs={{1,2},{2,3},{5,6},{6,7},{9,10},{10,11},{13,14},{14,15},{17,18},{18... | collective-permute-start | bytes 2359304 | tf_op jit(solution)/shard_map/ppermute | solution.py:217
  133.7 13.9 %collective-permute-start.20 = (f32[3,2,128,256]{3,2,1,0:T(8,128)S(1)}, f32[3,2,128,256]{3,2,1,0:T(8,128)S(1)}, u32[]{:S(2)}, u32[]{:S(2)}) collective-permute-start(f32[3,2,128,256]{3,2,1,0:T(8,128)S(1)} %collective-permute-done.16.refs_3_), channel_id=1, source_target_pairs={{2,3},{6,7},{10,11},{14,15},{18,19},{22,23},{26,27},{30,31}} | collective-permute-start | bytes 2359304 | tf_op jit(solution)/shard_map/ppermute | solution.py:217
  135.8 11.8 %collective-permute-start.21 = (f32[3,2,128,256]{3,2,1,0:T(8,128)S(1)}, f32[3,2,128,256]{3,2,1,0:T(8,128)S(1)}, u32[]{:S(2)}, u32[]{:S(2)}) collective-permute-start(f32[3,2,128,256]{3,2,1,0:T(8,128)S(1)} %collective-permute-done.17.refs_4_), channel_id=1, source_target_pairs={{1,0},{5,4},{9,8},{13,12},{17,16},{21,20},{25,24},{29,28}} | collective-permute-start | bytes 2359304 | tf_op jit(solution)/shard_map/ppermute | solution.py:217
  136.5 12.8 %collective-permute-start.23 = (f32[3,2,256,128]{3,2,1,0:T(8,128)S(1)}, f32[3,2,256,128]{3,2,1,0:T(8,128)S(1)}, u32[]{:S(2)}, u32[]{:S(2)}) collective-permute-start(f32[3,2,256,128]{3,2,1,0:T(8,128)S(1)} %collective-permute-done.15.refs_8_), channel_id=1, source_target_pairs={{0,4},{4,0},{8,12},{12,8},{1,5},{5,1},{9,13},{13,9},{2,6},{6,2},{1... | collective-permute-start | bytes 2359304 | tf_op jit(solution)/shard_map/ppermute | solution.py:217
  136.6 12.7 %collective-permute-start.22 = (f32[3,2,256,128]{3,2,1,0:T(8,128)S(1)}, f32[3,2,256,128]{3,2,1,0:T(8,128)S(1)}, u32[]{:S(2)}, u32[]{:S(2)}) collective-permute-start(f32[3,2,256,128]{3,2,1,0:T(8,128)S(1)} %collective-permute-done.14.refs_7_), channel_id=1, source_target_pairs={{0,8},{4,12},{8,0},{12,4},{1,9},{5,13},{9,1},{13,5},{2,10},{6,14},... | collective-permute-start | bytes 2359304 | tf_op jit(solution)/shard_map/ppermute | solution.py:217
  156.3 14.1 %collective-permute-start.24 = (f32[512,2048]{1,0:T(8,128)S(1)}, f32[512,2048]{1,0:T(8,128)S(1)}, u32[]{:S(2)}, u32[]{:S(2)}) collective-permute-start(f32[512,2048]{1,0:T(8,128)S(1)} %get-tuple-element.146), channel_id=1, source_target_pairs={{0,16},{16,0},{1,17},{17,1},{2,18},{18,2},{3,19},{19,3},{4,20},{20... | collective-permute-start | bytes 12582920 | tf_op jit(solution)/shard_map/ppermute | solution.py:369
  (17 other events, 298.9 us)
